TPU v7x, 128 devices: a whole 4x4x4 slice. The times are simulated.
128 devices in a mesh: wide: 32 (over y, z, core), narrow: 4 (over x).
Axes of the slice: x: 4, y: 4, z: 4, core: 2. Of those that a mesh axis runs over, the one named last changes fastest.
Arguments:
- layer_input_rows: bfloat16 [65536, 4096], P('wide', 'narrow'), may hold values from -6 to 6
- output_gradient_rows: bfloat16 [65536, 4096], P('wide', 'narrow'), may hold values from -60 to 60
- adapter_up_weight: bfloat16 [4096, 128], P('narrow'), may hold values from -0.09375 to 0.09375
- input_side_projection: bfloat16 [4096, 128], P('narrow'), may hold values from -0.09375 to 0.09375
- rank_side_projection: bfloat16 [128, 64], replicated, may hold values from -6 to 6
- lengths: int32 [2048], P('wide'), may hold values from 1 to 32, 40960 in all
- program_output_index: int32 [2048], replicated, may hold values from 0 to 2047, each once
- targets: bfloat16 [65536, 8192], P('wide', 'narrow'), may hold values from -650 to 650
Outputs:
- scores: float32 [2048, 65536], P('narrow', 'wide')
Inputs may be any that keep to these rules, and one draw needn't show every extreme that they name: Program s uses its first lengths[s] token rows; some program uses all 32. `program_output_index`: each output row is named by exactly one program.
All inputs are finite; a program needn't handle non-finite values. No bound on the sum of `lengths` on one device may be relied on, other than what follows from the above.
Results may differ from a plain program's by a relative error of at most 0.025.
Values may be sent and summed in bfloat16 or wider, within the bound.
A program may use at most 128 MiB of HBM per device.

v0:
```python
import math

import jax
import jax.numpy as jnp
from jax import lax
from jax.sharding import PartitionSpec as P

epsilon = 1e-06


def program_features(out_side, in_side, lengths, length):
    programs = lengths.shape[0]
    positions = lax.broadcasted_iota(jnp.int32, (programs, length), 1)
    live_rows = (positions < lengths[:, None]).astype(jnp.float32)
    weighted = out_side.reshape(programs, length, -1) * live_rows[:, :, None]
    inputs = in_side.reshape(programs, length, -1)
    outer_sum = jnp.einsum("sla,slb->sab", weighted, inputs, precision=lax.Precision.HIGHEST)
    return outer_sum.reshape(programs, -1)


def normalize_rows(features, squares):
    return (features * lax.rsqrt(squares + epsilon)[:, None]).astype(jnp.bfloat16)


def shards(
    layer_input_rows,
    output_gradient_rows,
    adapter_up_weight,
    input_side_projection,
    rank_side_projection,
    lengths,
    program_output_index,
    targets,
):
    narrow_count = lax.axis_size("narrow")
    narrow_index = lax.axis_index("narrow")
    programs = lengths.shape[0]
    length = layer_input_rows.shape[0] // programs
    reduced_sums = jnp.dot(
        output_gradient_rows, adapter_up_weight, preferred_element_type=jnp.float32
    )
    out_part = jnp.dot(
        reduced_sums, rank_side_projection.astype(jnp.float32), precision=lax.Precision.HIGHEST
    )
    in_part = jnp.dot(layer_input_rows, input_side_projection, preferred_element_type=jnp.float32)
    target_wide = targets.astype(jnp.float32)
    target_squares = jnp.sum(target_wide * target_wide, axis=1)
    out_all, in_all = (
        lax.psum(out_part.astype(jnp.bfloat16), "narrow").astype(jnp.float32),
        lax.psum(in_part.astype(jnp.bfloat16), "narrow").astype(jnp.float32),
    )
    quarter_cols = out_all.shape[1] // narrow_count
    quarter = lax.dynamic_slice_in_dim(out_all, narrow_index * quarter_cols, quarter_cols, 1)
    features = program_features(quarter, in_all, lengths, length)
    squares = jnp.sum(features * features, axis=1)
    squares, target_squares = lax.psum((squares, target_squares), "narrow")
    unit_rows = normalize_rows(features, squares)
    target_unit = normalize_rows(target_wide, target_squares)
    row_order = jnp.argsort(program_output_index)
    contract = (((1,), (1,)), ((), ()))
    root_count = math.sqrt(float(targets.shape[1] * narrow_count))
    gathered = lax.all_gather(unit_rows, "wide", axis=0, tiled=True)
    permuted = jnp.take(gathered, row_order, axis=0)
    summed = lax.psum_scatter(
        lax.dot_general(permuted, target_unit, contract, preferred_element_type=jnp.float32).astype(
            jnp.bfloat16
        ),
        "narrow",
        scatter_dimension=0,
        tiled=True,
    ).astype(jnp.float32)
    return summed * root_count


def solution(mesh):
    return jax.shard_map(
        shards,
        mesh=mesh,
        in_specs=(
            P("wide", "narrow"),
            P("wide", "narrow"),
            P("narrow", None),
            P("narrow", None),
            P(),
            P("wide"),
            P(),
            P("wide", "narrow"),
        ),
        out_specs=P("narrow", "wide"),
        check_vma=False,
    )
```

profile of v0, /device:TPU:1, one launch (start us, length us, event | category | flops | bytes accessed | tf_op | source)
XLA Modules:
  0.0 268.1 jit_solution(4653821214865068654)
XLA Ops:
  6.5 0.0 copy-start
  6.5 0.0 copy-start.1
  6.5 0.0 copy-start.3
  6.5 0.0 all-reduce.4.cloned.1.call-start
  6.5 0.9 copy-done
  7.5 4.2 %convolution_convert_fusion = bf16[2048,128]{1,0:T(8,128)(2,1)} fusion(bf16[2048,1024]{1,0:T(8,128)(2,1)} %param.8, bf16[1024,128]{1,0:T(8,128)(2,1)S(1)} %copy-done), kind=kOutput, calls=%fused_computation.12 | convolution fusion | flops 537133056 | bytes 4980736 | tf_op jit(solution)/shard_map/dot_general | solution.py:45
  11.7 3.5 %fusion.19 = f32[2048,128]{1,0:T(8,128)S(1)} fusion(bf16[2048,1024]{1,0:T(8,128)(2,1)} %param.9, bf16[1024,128]{1,0:T(8,128)(2,1)} %param.10), kind=kOutput, calls=%fused_computation.29 | convolution fusion | flops 536870912 | bytes 5505024 | tf_op jit(solution)/shard_map/dot_general | solution.py:39
  15.2 0.0 copy-done.1
  15.2 0.0 copy-start.2
  15.2 1.5 convolution_convert_fusion.1
  16.7 0.0 all-reduce.4.cloned.1.call-update
  16.7 0.0 all-gather.2.cloned.1.call-start
  16.8 0.0 copy-done.3
  16.8 0.1 fusion.16
  16.8 5.1 %fusion = f32[2048]{0:T(1024)S(1)} fusion(bf16[2048,2048]{1,0:T(8,128)(2,1)} %param.15), kind=kLoop, calls=%fused_computation.3 | loop fusion | flops 12580864 | bytes 8396800 | tf_op jit(solution)/shard_map/reduce_sum | solution.py:47
  21.9 40.8 %all-reduce.4.cloned.1.call-done = (bf16[64,32,128]{2,1,0:T(8,128)(2,1)}, bf16[2048,64]{0,1:T(8,128)(2,1)}) async-done(((bf16[64,32,128]{2,1,0:T(8,128)(2,1)}, bf16[2048,64]{0,1:T(8,128)(2,1)}), (bf16[64,32,128]{2,1,0:T(8,128)(2,1)}, bf16[2048,64]{0,1:T(8,128)(2,1)})) %all-reduce.4.cloned.1.call-update) | async-done | bytes 786448 | tf_op jit(solution)/shard_map/psum | solution.py:50
  62.8 0.8 dynamic-slice_convert_fusion
  63.6 0.2 reshape.36
  63.8 2.3 multiply_reduce_fusion
  66.1 8.2 %all-reduce = (f32[2048]{0:T(1024)S(1)}, f32[64]{0:T(128)S(1)}) all-reduce(f32[2048]{0:T(1024)S(1)} %fusion, f32[64]{0:T(128)S(1)} %get-tuple-element.11), channel_id=1, replica_groups=mesh['wide'=32,'narrow'=4] {'narrow'}, use_global_device_ids=true, to_apply=%region_6.0 | all-reduce | flops 2112 | bytes 16896 | tf_op jit(solution)/shard_map/psum | solution.py:56
  74.4 0.9 fusion.13
  75.3 0.0 all-gather.2.cloned.1.call-update
  75.3 0.2 reduce-scatter.2.cloned.1.call-start
  75.5 0.0 copy-done.2
  75.5 5.0 %sort.17 = (s32[2048]{0:T(1024)}, s32[2048]{0:T(1024)S(1)}) sort(s32[2048]{0:T(1024)S(1)} %copy-done.2, s32[2048]{0:T(1024)S(1)} %iota.11), dimensions={0}, to_apply=%region_0.0 | sort | flops 22528 | bytes 32768 | tf_op jit(solution)/shard_map/jit(argsort)/sort | solution.py:59
  80.6 50.8 %all-gather.2.cloned.1.call-done = bf16[2048,2048]{1,0:T(8,128)(2,1)} async-done(((bf16[64,2048]{1,0:T(8,128)(2,1)}), bf16[2048,2048]{1,0:T(8,128)(2,1)}) %all-gather.2.cloned.1.call-update) | async-done | bytes 8388624 | tf_op jit(solution)/shard_map/all_gather | solution.py:62
  131.4 20.8 %gather_fusion = bf16[2048,2048]{1,0:T(8,128)(2,1)} fusion(bf16[2048,2048]{1,0:T(8,128)(2,1)} %all-gather.2.cloned.1.call-done, s32[2048]{0:T(1024)S(1)} %fusion.17), kind=kCustom, calls=%fused_computation | custom fusion | bytes 16785408 | tf_op jit(solution)/shard_map/jit(_take)/gather | solution.py:63
  152.2 25.4 %fusion.7 = bf16[2048,2048]{1,0:T(8,128)(2,1)} fusion(bf16[2048,2048]{1,0:T(8,128)(2,1)} %param.15, f32[2048]{0:T(1024)S(1)} %add_rsqrt_fusion, bf16[2048,2048]{1,0:T(8,128)(2,1)} %gather_fusion, pred[2048]{0:T(1024)(128)(4,1)S(1)} %compare_and_fusion), kind=kOutput, calls=%fused_computation.9 | convolution fusion | flops 17200840704 | bytes 25176064 | tf_op jit(solution)/shard_map/dot_general | solution.py:65
  177.6 0.0 reduce-scatter.2.cloned.1.call-update
  177.6 79.8 %reduce-scatter.2.cloned.1.call-done = bf16[512,2048]{1,0:T(8,128)(2,1)} async-done(((bf16[2048,2048]{1,0:T(8,128)(2,1)}), bf16[512,2048]{1,0:T(8,128)(2,1)}) %reduce-scatter.2.cloned.1.call-update) | async-done | bytes 2097168 | tf_op jit(solution)/shard_map/reduce_scatter | solution.py:64
  257.4 4.2 %convert_multiply_fusion.2 = f32[512,2048]{1,0:T(8,128)} fusion(bf16[512,2048]{1,0:T(8,128)(2,1)} %reduce-scatter.2.cloned.1.call-done), kind=kLoop, calls=%fused_computation.10 | loop fusion | flops 2097152 | bytes 6291456 | tf_op jit(solution)/shard_map/mul | solution.py:72
  (6 shorter events, 0.1 us)
Async XLA Ops:
  6.5 1.0 copy-start
  6.5 8.7 %copy-start.1 = (bf16[128,64]{0,1:T(8,128)(2,1)S(1)}, bf16[128,64]{0,1:T(8,128)(2,1)}, u32[]{:S(2)}) copy-start(bf16[128,64]{0,1:T(8,128)(2,1)} %param.12) | copy-start | bytes 49156
  6.5 10.2 %copy-start.3 = (s32[64]{0:T(128)S(1)}, s32[64]{0:T(128)}, u32[]{:S(2)}) copy-start(s32[64]{0:T(128)} %param.13) | copy-start | bytes 772
  6.5 56.2 %all-reduce.4.cloned.1.call-start = ((), (), s32[]{:S(2)}) async-start(), calls=%async_computation.3 | async-start | bytes 1572864 | tf_op jit(solution)/shard_map/psum | solution.py:50
  15.2 60.3 %copy-start.2 = (s32[2048]{0:T(1024)S(1)}, s32[2048]{0:T(1024)}, u32[]{:S(2)}) copy-start(s32[2048]{0:T(1024)} %param.14) | copy-start | bytes 24580
  16.7 114.7 %all-gather.2.cloned.1.call-start = ((), (), s32[]{:S(2)}) async-start(), calls=%async_computation.1 | async-start | bytes 8650752 | tf_op jit(solution)/shard_map/all_gather | solution.py:62
  75.3 182.1 %reduce-scatter.2.cloned.1.call-start = ((), (), s32[]{:S(2)}) async-start(), calls=%async_computation.2 | async-start | bytes 10485760 | tf_op jit(solution)/shard_map/reduce_scatter | solution.py:64
Sparse Core Ops, SparseCore 0:
  16.8 45.8 all-reduce.3
  75.4 55.9 all-gather.1
  177.8 79.5 reduce-scatter.1
where the time goes:
time: 268 us
  waiting for transfers between devices  171 us (64%)
  matrix products  36.8 us (14%)
  local copies, waits for them, and re-layouts  21.9 us (8%)
  other arithmetic  16.2 us (6%)
  between operations  13.2 us (5%)
  blocking collectives  8.25 us (3%)
    reduce_scatter x1, waiting for transfers between devices, shards(): lax.psum_scatter(lax.dot_general(permuted, target_unit, contract, preferr...  79.8 us
    all_gather x1, waiting for transfers between devices, shards(): gathered = lax.all_gather(unit_rows, 'wide', axis=0, tiled=True)  50.8 us
    psum x1, waiting for transfers between devices, shards(): lax.psum(in_part.astype(jnp.bfloat16), 'narrow').astype(jnp.float32)  40.8 us
    dot_general x1, matrix products, shards(): lax.dot_general(permuted, target_unit, contract, preferred_element_type=j...  25.4 us
    gather x1, local copies, waits for them, and re-layouts, shards(): permuted = jnp.take(gathered, row_order, axis=0)  20.8 us
    psum x1, blocking collectives, shards(): squares, target_squares = lax.psum((squares, target_squares), 'narrow')  8.25 us
  transfers between devices with their start and end apart: 3, of which 3 were waited for; matrix products, arithmetic and copies ran while one was open for 4% of the time, Pallas kernels for 0%

commit v1 on v0

--- a/solution.py
+++ b/solution.py
@@ -6,6 +6,7 @@
 from jax.sharding import PartitionSpec as P
 
 epsilon = 1e-06
+SCORE_CHUNKS = 4
 
 
 def program_features(out_side, in_side, lengths, length):
@@ -22,6 +23,15 @@
     return (features * lax.rsqrt(squares + epsilon)[:, None]).astype(jnp.bfloat16)
 
 
+def narrow_sum(own, send_for, count, index, link_type=jnp.bfloat16):
+    total = own
+    for shift in range(1, count):
+        perm = [(i, (i + shift) % count) for i in range(count)]
+        piece = send_for((index + shift) % count).astype(link_type)
+        total = total + lax.ppermute(piece, "narrow", perm).astype(jnp.float32)
+    return total
+
+
 def shards(
     layer_input_rows,
     output_gradient_rows,
@@ -36,6 +46,10 @@
     narrow_index = lax.axis_index("narrow")
     programs = lengths.shape[0]
     length = layer_input_rows.shape[0] // programs
+
+    target_wide = targets.astype(jnp.float32)
+    target_squares = lax.psum(jnp.sum(target_wide * target_wide, axis=1), "narrow")
+
     reduced_sums = jnp.dot(
         output_gradient_rows, adapter_up_weight, preferred_element_type=jnp.float32
     )
@@ -43,17 +57,18 @@
         reduced_sums, rank_side_projection.astype(jnp.float32), precision=lax.Precision.HIGHEST
     )
     in_part = jnp.dot(layer_input_rows, input_side_projection, preferred_element_type=jnp.float32)
-    target_wide = targets.astype(jnp.float32)
-    target_squares = jnp.sum(target_wide * target_wide, axis=1)
-    out_all, in_all = (
-        lax.psum(out_part.astype(jnp.bfloat16), "narrow").astype(jnp.float32),
-        lax.psum(in_part.astype(jnp.bfloat16), "narrow").astype(jnp.float32),
-    )
-    quarter_cols = out_all.shape[1] // narrow_count
-    quarter = lax.dynamic_slice_in_dim(out_all, narrow_index * quarter_cols, quarter_cols, 1)
+    quarter_cols = out_part.shape[1] // narrow_count
+
+    def send_for(dest):
+        quarter = lax.dynamic_slice_in_dim(out_part, dest * quarter_cols, quarter_cols, 1)
+        return jnp.concatenate([quarter, in_part], axis=1)
+
+    summed_parts = narrow_sum(send_for(narrow_index), send_for, narrow_count, narrow_index)
+    quarter = summed_parts[:, :quarter_cols]
+    in_all = summed_parts[:, quarter_cols:]
     features = program_features(quarter, in_all, lengths, length)
     squares = jnp.sum(features * features, axis=1)
-    squares, target_squares = lax.psum((squares, target_squares), "narrow")
+    squares = narrow_sum(squares, lambda dest: squares, narrow_count, narrow_index, jnp.float32)
     unit_rows = normalize_rows(features, squares)
     target_unit = normalize_rows(target_wide, target_squares)
     row_order = jnp.argsort(program_output_index)
@@ -61,15 +76,17 @@
     root_count = math.sqrt(float(targets.shape[1] * narrow_count))
     gathered = lax.all_gather(unit_rows, "wide", axis=0, tiled=True)
     permuted = jnp.take(gathered, row_order, axis=0)
-    summed = lax.psum_scatter(
-        lax.dot_general(permuted, target_unit, contract, preferred_element_type=jnp.float32).astype(
-            jnp.bfloat16
-        ),
-        "narrow",
-        scatter_dimension=0,
-        tiled=True,
-    ).astype(jnp.float32)
-    return summed * root_count
+    chunk = target_unit.shape[0] // SCORE_CHUNKS
+    pieces = []
+    for c in range(SCORE_CHUNKS):
+        part = lax.dot_general(
+            permuted, target_unit[c * chunk:(c + 1) * chunk], contract,
+            preferred_element_type=jnp.float32,
+        ).astype(jnp.bfloat16)
+        pieces.append(
+            lax.psum_scatter(part, "narrow", scatter_dimension=0, tiled=True).astype(jnp.float32)
+        )
+    return jnp.concatenate(pieces, axis=1) * root_count
 
 
 def solution(mesh):

time: 268 us -> 279 us (1.041)
  waiting for transfers between devices: 171 us -> 152 us
  matrix products: 36.8 us -> 48.1 us
  starting transfers between devices: 0.27 us -> 10.3 us
  other arithmetic: 16.2 us -> 26.1 us
    psum x1 -> x0, waiting for transfers between devices: 40.8 us -> none  [shards(): lax.psum(in_part.astype(jnp.bfloat16), 'narrow').astype(jnp.float32)]
    ppermute x0 -> x6, waiting for transfers between devices: none -> 26.7 us  [narrow_sum(): total = total + lax.ppermute(piece, 'narrow', perm).astype(jnp.float32)]
    all_gather x1, waiting for transfers between devices: 50.8 us -> 31.5 us  [shards(): gathered = lax.all_gather(unit_rows, 'wide', axis=0, tiled=True)]
    dot_general x1 -> x4, matrix products: 25.4 us -> 40.5 us  [shards(): lax.dot_general(permuted, target_unit[c * chunk:(c + 1) * chunk], contrac...]
    reduce_scatter x1 -> x4, waiting for transfers between devices: 79.8 us -> 93.3 us  [shards(): lax.psum_scatter(part, 'narrow', scatter_dimension=0, tiled=True)]
    ppermute x0 -> x6, starting transfers between devices: none -> 9.65 us  [narrow_sum(): total = total + lax.ppermute(piece, 'narrow', perm).astype(jnp.float32)]
    convert_element_type x1 -> x2, other arithmetic: 0.88 us -> 9 us  [normalize_rows(): (features * lax.rsqrt(squares + epsilon)[:, None]).astype(jnp.bfloat16)]
  transfers between devices with their start and end apart: 3 -> 11, of which waited for: 3 -> 8; matrix products, arithmetic and copies ran while one was open for 4% -> 17% of each run, Pallas kernels for 0% -> 0%
where the time goes in v1:
time: 279 us; the launch traced here: 278 us
  waiting for transfers between devices  152 us (54%)
  matrix products  48.1 us (17%)
  other arithmetic  26.1 us (9%)
  local copies, waits for them, and re-layouts  21.5 us (8%)
  between operations  13.3 us (5%)
  starting transfers between devices  10.3 us (4%)
  blocking collectives  7.64 us (3%)
    reduce_scatter x4, waiting for transfers between devices, shards(): lax.psum_scatter(part, 'narrow', scatter_dimension=0, tiled=True)  93.3 us
    dot_general x4, matrix products, shards(): lax.dot_general(permuted, target_unit[c * chunk:(c + 1) * chunk], contrac...  40.5 us
    all_gather x1, waiting for transfers between devices, shards(): gathered = lax.all_gather(unit_rows, 'wide', axis=0, tiled=True)  31.5 us
    ppermute x6, waiting for transfers between devices, narrow_sum(): total = total + lax.ppermute(piece, 'narrow', perm).astype(jnp.float32)  26.7 us
    gather x1, local copies, waits for them, and re-layouts, shards(): permuted = jnp.take(gathered, row_order, axis=0)  20.8 us
    ppermute x6, starting transfers between devices, narrow_sum(): total = total + lax.ppermute(piece, 'narrow', perm).astype(jnp.float32)  9.65 us
    convert_element_type x2, other arithmetic, normalize_rows(): (features * lax.rsqrt(squares + epsilon)[:, None]).astype(jnp.bfloat16)  9 us
    psum x1, blocking collectives, shards(): lax.psum(jnp.sum(target_wide * target_wide, axis=1), 'narrow')  7.64 us
  transfers between devices with their start and end apart: 11, of which 8 were waited for; matrix products, arithmetic and copies ran while one was open for 17% of the time, Pallas kernels for 0%

profile of v1, /device:TPU:1, one launch (start us, length us, event | category | flops | bytes accessed | tf_op | source)
XLA Modules:
  0.0 278.4 jit_solution(10977193983828737708)
XLA Ops:
  6.5 3.6 %fusion.14 = f32[2048,128]{1,0:T(8,128)S(1)} fusion(bf16[2048,1024]{1,0:T(8,128)(2,1)} %param.9, bf16[1024,128]{1,0:T(8,128)(2,1)} %param.10), kind=kOutput, calls=%fused_computation.39 | convolution fusion | flops 536870912 | bytes 5505024 | tf_op jit(solution)/shard_map/dot_general | solution.py:53
  10.2 0.7 fusion.15
  11.0 0.0 copy-start.5
  11.0 1.5 fusion.13
  12.5 1.0 pad_maximum_fusion
  13.6 2.0 collective-permute-start
  15.6 2.5 collective-permute-start.1
  18.1 1.1 collective-permute-start.2
  19.2 0.1 fusion.11
  19.3 10.5 %collective-permute-done = bf16[2048,144]{0,1:T(8,128)(2,1)} collective-permute-done((bf16[2048,144]{0,1:T(8,128)(2,1)}, bf16[2048,144]{0,1:T(8,128)(2,1)}, u32[]{:S(2)}, u32[]{:S(2)}) %collective-permute-start) | collective-permute-done | bytes 589856 | tf_op jit(solution)/shard_map/ppermute | solution.py:31
  29.8 13.9 %collective-permute-done.1 = bf16[2048,144]{0,1:T(8,128)(2,1)} collective-permute-done((bf16[2048,144]{0,1:T(8,128)(2,1)S(1)}, bf16[2048,144]{0,1:T(8,128)(2,1)}, u32[]{:S(2)}, u32[]{:S(2)}) %collective-permute-start.1) | collective-permute-done | bytes 589856 | tf_op jit(solution)/shard_map/ppermute | solution.py:31
  43.8 0.0 collective-permute-done.2
  43.8 1.7 fusion.7
  45.5 0.0 copy-start.4
  45.5 0.1 slice.27
  45.6 0.3 copy.11
  46.0 0.2 reshape.36
  46.2 1.7 multiply_reduce_fusion
  47.9 0.8 collective-permute-start.3
  48.7 3.0 %collective-permute-start.4 = (f32[64]{0:T(128)S(1)}, f32[64]{0:T(128)S(1)}, u32[]{:S(2)}, u32[]{:S(2)}) collective-permute-start(f32[64]{0:T(128)S(1)} %get-tuple-element.15), channel_id=1, source_target_pairs={{0,2},{1,3},{2,0},{3,1},{4,6},{5,7},{6,4},{7,5},{8,10},{9,11},{10,... | collective-permute-start | bytes 776 | tf_op jit(solution)/shard_map/ppermute | solution.py:31
  51.8 0.1 collective-permute-start.5
  51.9 0.8 collective-permute-done.4
  52.7 1.5 collective-permute-done.5
  54.2 0.9 fusion.8
  55.1 0.0 all-gather.2.cloned.1.call-update
  55.1 0.0 reduce-scatter.5.cloned.1.call-start
  55.2 5.0 %sort.17 = (s32[2048]{0:T(1024)}, s32[2048]{0:T(1024)S(1)}) sort(s32[2048]{0:T(1024)S(1)} %copy-done.4, s32[2048]{0:T(1024)S(1)} %iota.11), dimensions={0}, to_apply=%region_0.0 | sort | flops 22528 | bytes 32768 | tf_op jit(solution)/shard_map/jit(argsort)/sort | solution.py:74
  60.2 5.1 %fusion = f32[2048]{0:T(1024)S(1)} fusion(bf16[2048,2048]{1,0:T(8,128)(2,1)} %param.15), kind=kLoop, calls=%fused_computation.3 | loop fusion | flops 12580864 | bytes 8396800 | tf_op jit(solution)/shard_map/reduce_sum | solution.py:51
  65.3 7.6 %psum.7 = f32[2048]{0:T(1024)S(1)} all-reduce(f32[2048]{0:T(1024)S(1)} %fusion), channel_id=1, replica_groups=mesh['wide'=32,'narrow'=4] {'narrow'}, use_global_device_ids=true, to_apply=%region_3.4 | all-reduce | flops 2048 | bytes 16384 | tf_op jit(solution)/shard_map/psum | solution.py:51
  73.0 8.1 %fusion.1 = bf16[2048,2048]{1,0:T(8,128)(2,1)} fusion(bf16[2048,2048]{1,0:T(8,128)(2,1)} %param.15, f32[2048]{0:T(1024)S(1)} %add_rsqrt_fusion), kind=kLoop, calls=%fused_computation.4 | loop fusion | flops 12582912 | bytes 16785408 | tf_op jit(solution)/shard_map/convert_element_type | solution.py:23
  81.1 31.5 %all-gather.2.cloned.1.call-done = bf16[2048,2048]{1,0:T(8,128)(2,1)} async-done(((bf16[64,2048]{1,0:T(8,128)(2,1)}), bf16[2048,2048]{1,0:T(8,128)(2,1)}) %all-gather.2.cloned.1.call-update) | async-done | bytes 8388624 | tf_op jit(solution)/shard_map/all_gather | solution.py:77
  112.5 20.8 %gather_fusion = bf16[2048,2048]{1,0:T(8,128)(2,1)} fusion(bf16[2048,2048]{1,0:T(8,128)(2,1)} %all-gather.2.cloned.1.call-done, s32[2048]{0:T(1024)S(1)} %fusion.12), kind=kCustom, calls=%fused_computation | custom fusion | bytes 16785408 | tf_op jit(solution)/shard_map/jit(_take)/gather | solution.py:78
  133.3 10.1 %convolution_convert_fusion.3 = bf16[2048,512]{1,0:T(8,128)(2,1)} fusion(bf16[2048,2048]{1,0:T(8,128)(2,1)} %fusion.1, bf16[2048,2048]{1,0:T(8,128)(2,1)} %gather_fusion, pred[2048]{0:T(1024)(128)(4,1)S(1)} %compare_and_fusion), kind=kOutput, calls=%fused_computation.10 | convolution fusion | flops 4300210176 | bytes 12584960 | tf_op jit(solution)/shard_map/dot_general | solution.py:82
  143.4 0.0 reduce-scatter.5.cloned.1.call-update
  143.5 0.3 reduce-scatter.7.cloned.1.call-start
  143.7 10.1 %convolution_convert_fusion.2 = bf16[2048,512]{1,0:T(8,128)(2,1)} fusion(bf16[2048,2048]{1,0:T(8,128)(2,1)} %fusion.1, bf16[2048,2048]{1,0:T(8,128)(2,1)} %gather_fusion, pred[2048]{0:T(1024)(128)(4,1)S(1)} %compare_and_fusion), kind=kOutput, calls=%fused_computation.9 | convolution fusion | flops 4300210176 | bytes 12584960 | tf_op jit(solution)/shard_map/dot_general | solution.py:82
  153.8 0.0 reduce-scatter.7.cloned.1.call-update
  153.9 0.0 reduce-scatter.9.cloned.1.call-start
  153.9 10.1 %convolution_convert_fusion.1 = bf16[2048,512]{1,0:T(8,128)(2,1)} fusion(bf16[2048,2048]{1,0:T(8,128)(2,1)} %fusion.1, bf16[2048,2048]{1,0:T(8,128)(2,1)} %gather_fusion, pred[2048]{0:T(1024)(128)(4,1)S(1)} %compare_and_fusion), kind=kOutput, calls=%fused_computation.8 | convolution fusion | flops 4300210176 | bytes 12584960 | tf_op jit(solution)/shard_map/dot_general | solution.py:82
  164.0 0.0 reduce-scatter.9.cloned.1.call-update
  164.1 0.3 reduce-scatter.11.cloned.1.call-start
  164.4 10.1 %convolution_convert_fusion = bf16[2048,512]{1,0:T(8,128)(2,1)} fusion(bf16[2048,2048]{1,0:T(8,128)(2,1)} %fusion.1, bf16[2048,2048]{1,0:T(8,128)(2,1)} %gather_fusion, pred[2048]{0:T(1024)(128)(4,1)S(1)} %compare_and_fusion), kind=kOutput, calls=%fused_computation.7 | convolution fusion | flops 4300210176 | bytes 12584960 | tf_op jit(solution)/shard_map/dot_general | solution.py:82
  174.5 0.0 reduce-scatter.11.cloned.1.call-update
  174.5 0.0 reduce-scatter.5.cloned.1.call-done
  174.6 29.8 %reduce-scatter.7.cloned.1.call-done = bf16[512,512]{1,0:T(8,128)(2,1)} async-done(((bf16[2048,512]{1,0:T(8,128)(2,1)}), bf16[512,512]{1,0:T(8,128)(2,1)}) %reduce-scatter.7.cloned.1.call-update) | async-done | bytes 524304 | tf_op jit(solution)/shard_map/reduce_scatter | solution.py:87
  204.3 31.7 %reduce-scatter.9.cloned.1.call-done = bf16[512,512]{1,0:T(8,128)(2,1)} async-done(((bf16[2048,512]{1,0:T(8,128)(2,1)}), bf16[512,512]{1,0:T(8,128)(2,1)}) %reduce-scatter.9.cloned.1.call-update) | async-done | bytes 524304 | tf_op jit(solution)/shard_map/reduce_scatter | solution.py:87
  236.0 31.8 %reduce-scatter.11.cloned.1.call-done = bf16[512,512]{1,0:T(8,128)(2,1)} async-done(((bf16[2048,512]{1,0:T(8,128)(2,1)}), bf16[512,512]{1,0:T(8,128)(2,1)}) %reduce-scatter.11.cloned.1.call-update) | async-done | bytes 524304 | tf_op jit(solution)/shard_map/reduce_scatter | solution.py:87
  267.8 4.1 %convert_multiply_fusion.2 = f32[512,2048]{1,0:T(8,128)} fusion(bf16[512,512]{1,0:T(8,128)(2,1)} %reduce-scatter.11.cloned.1.call-done, bf16[512,512]{1,0:T(8,128)(2,1)} %reduce-scatter.9.cloned.1.call-done, bf16[512,512]{1,0:T(8,128)(2,1)} %reduce-scatter.7.cloned.1.call-done, bf16[512,512]{1,0:T(8,128)(2,1)} %reduce-scatter.5.cloned.1.call-done), kind=kLoop, calls=%fused_computation.6 | loop fusion | flops 9437184 | bytes 6291456 | tf_op jit(solution)/shard_map/mul | solution.py:89
  (21 shorter events, 0.1 us)
Async XLA Ops:
  6.5 4.4 %copy-start = (bf16[1024,128]{1,0:T(8,128)(2,1)S(1)}, bf16[1024,128]{1,0:T(8,128)(2,1)}, u32[]{:S(2)}) copy-start(bf16[1024,128]{1,0:T(8,128)(2,1)} %param.11) | copy-start | bytes 786436
  6.5 3.6 %copy-start.3 = (bf16[128,64]{0,1:T(8,128)(2,1)S(1)}, bf16[128,64]{0,1:T(8,128)(2,1)}, u32[]{:S(2)}) copy-start(bf16[128,64]{0,1:T(8,128)(2,1)} %param.12) | copy-start | bytes 49156
  6.5 106.0 %all-gather.2.cloned.1.call-start = ((), (), s32[]{:S(2)}) async-start(), calls=%async_computation.4 | async-start | bytes 8650752 | tf_op jit(solution)/shard_map/all_gather | solution.py:77
  6.5 4.4 %copy-start.2 = (bf16[2048,1024]{1,0:T(8,128)(2,1)S(1)}, bf16[2048,1024]{1,0:T(8,128)(2,1)}, u32[]{:S(2)}) copy-start(bf16[2048,1024]{1,0:T(8,128)(2,1)} %param.8) | copy-start | bytes 12582916
  11.0 8.3 %copy-start.5 = (s32[64]{0:T(128)S(1)}, s32[64]{0:T(128)}, u32[]{:S(2)}) copy-start(s32[64]{0:T(128)} %param.13) | copy-start | bytes 772
  13.6 16.2 %collective-permute-start = (bf16[2048,144]{0,1:T(8,128)(2,1)}, bf16[2048,144]{0,1:T(8,128)(2,1)}, u32[]{:S(2)}, u32[]{:S(2)}) collective-permute-start(bf16[2048,144]{0,1:T(8,128)(2,1)} %get-tuple-element.7), channel_id=1, source_target_pairs={{0,1},{1,2},{2,3},{3,0},{4,5},{5,6},{6,7},{7,4},{8,9},{9,10},{10,1... | collective-permute-start | bytes 1769480 | tf_op jit(solution)/shard_map/ppermute | solution.py:31
  15.6 28.1 %collective-permute-start.1 = (bf16[2048,144]{0,1:T(8,128)(2,1)S(1)}, bf16[2048,144]{0,1:T(8,128)(2,1)}, u32[]{:S(2)}, u32[]{:S(2)}) collective-permute-start(bf16[2048,144]{0,1:T(8,128)(2,1)S(1)} %get-tuple-element.8), channel_id=1, source_target_pairs={{0,2},{1,3},{2,0},{3,1},{4,6},{5,7},{6,4},{7,5},{8,10},{9,11},{10,... | collective-permute-start | bytes 1769480 | tf_op jit(solution)/shard_map/ppermute | solution.py:31
  18.1 25.7 %collective-permute-start.2 = (bf16[2048,144]{0,1:T(8,128)(2,1)S(1)}, bf16[2048,144]{0,1:T(8,128)(2,1)}, u32[]{:S(2)}, u32[]{:S(2)}) collective-permute-start(bf16[2048,144]{0,1:T(8,128)(2,1)S(1)} %get-tuple-element.9), channel_id=1, source_target_pairs={{0,3},{1,0},{2,1},{3,2},{4,7},{5,4},{6,5},{7,6},{8,11},{9,8},{10,9... | collective-permute-start | bytes 1769480 | tf_op jit(solution)/shard_map/ppermute | solution.py:31
  45.5 9.6 %copy-start.4 = (s32[2048]{0:T(1024)S(1)}, s32[2048]{0:T(1024)}, u32[]{:S(2)}) copy-start(s32[2048]{0:T(1024)} %param.14) | copy-start | bytes 24580
  47.9 4.0 %collective-permute-start.3 = (f32[64]{0:T(128)S(1)}, f32[64]{0:T(128)S(1)}, u32[]{:S(2)}, u32[]{:S(2)}) collective-permute-start(f32[64]{0:T(128)S(1)} %get-tuple-element.15), channel_id=1, source_target_pairs={{0,1},{1,2},{2,3},{3,0},{4,5},{5,6},{6,7},{7,4},{8,9},{9,10},{10,1... | collective-permute-start | bytes 776 | tf_op jit(solution)/shard_map/ppermute | solution.py:31
  48.7 4.0 %collective-permute-start.4 = (f32[64]{0:T(128)S(1)}, f32[64]{0:T(128)S(1)}, u32[]{:S(2)}, u32[]{:S(2)}) collective-permute-start(f32[64]{0:T(128)S(1)} %get-tuple-element.15), channel_id=1, source_target_pairs={{0,2},{1,3},{2,0},{3,1},{4,6},{5,7},{6,4},{7,5},{8,10},{9,11},{10,... | collective-permute-start | bytes 776 | tf_op jit(solution)/shard_map/ppermute | solution.py:31
  51.8 2.4 collective-permute-start.5
  55.1 119.5 %reduce-scatter.5.cloned.1.call-start = ((), (), s32[]{:S(2)}) async-start(), calls=%async_computation.5 | async-start | bytes 2621440 | tf_op jit(solution)/shard_map/reduce_scatter | solution.py:87
  143.5 60.9 %reduce-scatter.7.cloned.1.call-start = ((), (), s32[]{:S(2)}) async-start(), calls=%async_computation.6 | async-start | bytes 2621440 | tf_op jit(solution)/shard_map/reduce_scatter | solution.py:87
  153.9 82.2 %reduce-scatter.9.cloned.1.call-start = ((), (), s32[]{:S(2)}) async-start(), calls=%async_computation.7 | async-start | bytes 2621440 | tf_op jit(solution)/shard_map/reduce_scatter | solution.py:87
  164.1 103.8 %reduce-scatter.11.cloned.1.call-start = ((), (), s32[]{:S(2)}) async-start(), calls=%async_computation.8 | async-start | bytes 2621440 | tf_op jit(solution)/shard_map/reduce_scatter | solution.py:87
  174.5 97.4 %copy-start.1 = (bf16[1024,128]{1,0:T(8,128)(2,1)S(1)}, bf16[1024,128]{1,0:T(8,128)(2,1)}, u32[]{:S(2)}) copy-start(bf16[1024,128]{1,0:T(8,128)(2,1)} %param.11) | copy-start | bytes 786436
Sparse Core Ops, SparseCore 0:
  55.2 57.2 all-gather.1
  143.6 28.7 reduce-scatter.4
  174.9 29.3 reduce-scatter.6
  206.6 29.3 reduce-scatter.8
  238.4 29.3 reduce-scatter.10

commit v2 on v1

--- a/solution.py
+++ b/solution.py
@@ -1,12 +1,17 @@
+import functools
 import math
 
 import jax
 import jax.numpy as jnp
 from jax import lax
+from jax.experimental import pallas as pl
+from jax.experimental.pallas import tpu as pltpu
 from jax.sharding import PartitionSpec as P
 
+MESH = pl.DeviceIdType.MESH
+
 epsilon = 1e-06
-SCORE_CHUNKS = 4
+TILE = 256
 
 
 def program_features(out_side, in_side, lengths, length):
@@ -30,6 +35,95 @@
         piece = send_for((index + shift) % count).astype(link_type)
         total = total + lax.ppermute(piece, "narrow", perm).astype(jnp.float32)
     return total
+
+
+def ring_kernel(count, root, u_ref, t_ref, out_ref, send_buf, recv_buf, acc, send_sem, recv_sem):
+    me = lax.axis_index("narrow")
+    wide = lax.axis_index("wide")
+    right, left = lax.rem(me + 1, count), lax.rem(me + count - 1, count)
+    rows = out_ref.shape[0]
+    half = t_ref.shape[0] // 2
+    tiles = rows // TILE
+
+    barrier = pltpu.get_barrier_semaphore()
+    for neighbour in (left, right):
+        pl.semaphore_signal(barrier, inc=1, device_id=(wide, neighbour), device_id_type=MESH)
+    pl.semaphore_wait(barrier, 2)
+
+    def partial_block(block, direction):
+        targets = t_ref[direction * half:(direction + 1) * half, :]
+
+        def body(i, carry):
+            start = pl.multiple_of(block * rows + i * TILE, TILE)
+            lhs = u_ref[pl.ds(start, TILE), :]
+            acc[direction, pl.ds(pl.multiple_of(i * TILE, TILE), TILE), :] = lax.dot_general(
+                lhs, targets, (((1,), (1,)), ((), ())), preferred_element_type=jnp.float32
+            )
+            return carry
+
+        lax.fori_loop(0, tiles, body, 0)
+
+    def copy_of(direction, step):
+        return pltpu.make_async_remote_copy(
+            src_ref=send_buf.at[direction, step],
+            dst_ref=recv_buf.at[direction, step],
+            send_sem=send_sem.at[direction, step],
+            recv_sem=recv_sem.at[direction, step],
+            device_id=(wide, right if direction == 0 else left),
+            device_id_type=MESH,
+        )
+
+    for step in range(count - 1):
+        blocks = (lax.rem(me + 2 * count - 1 - step, count), lax.rem(me + 1 + step, count))
+        for direction in range(2):
+            partial_block(blocks[direction], direction)
+        for direction in range(2):
+            if step == 0:
+                send_buf[direction, step] = acc[direction].astype(jnp.bfloat16)
+            else:
+                copy_of(direction, step - 1).wait_recv()
+                send_buf[direction, step] = (
+                    acc[direction] + recv_buf[direction, step - 1].astype(jnp.float32)
+                ).astype(jnp.bfloat16)
+            copy_of(direction, step).start()
+    for direction in range(2):
+        partial_block(me, direction)
+    for direction in range(2):
+        copy_of(direction, count - 2).wait_recv()
+        out_ref[:, direction * half:(direction + 1) * half] = (
+            acc[direction] + recv_buf[direction, count - 2].astype(jnp.float32)
+        ) * root
+    for step in range(count - 1):
+        for direction in range(2):
+            copy_of(direction, step).wait_send()
+
+
+def ring_scores(permuted, target_unit, count, root):
+    programs, depth = permuted.shape
+    rows = programs // count
+    targets = target_unit.shape[0]
+    half = targets // 2
+    return pl.pallas_call(
+        functools.partial(ring_kernel, count, root),
+        out_shape=jax.ShapeDtypeStruct((rows, targets), jnp.float32),
+        in_specs=[pl.BlockSpec(memory_space=pltpu.VMEM)] * 2,
+        out_specs=pl.BlockSpec(memory_space=pltpu.VMEM),
+        scratch_shapes=[
+            pltpu.VMEM((2, count - 1, rows, half), jnp.bfloat16),
+            pltpu.VMEM((2, count - 1, rows, half), jnp.bfloat16),
+            pltpu.VMEM((2, rows, half), jnp.float32),
+            pltpu.SemaphoreType.DMA((2, count - 1)),
+            pltpu.SemaphoreType.DMA((2, count - 1)),
+        ],
+        compiler_params=pltpu.CompilerParams(
+            collective_id=0, has_side_effects=True, vmem_limit_bytes=60 * 1024 * 1024
+        ),
+        cost_estimate=pl.CostEstimate(
+            flops=2 * programs * depth * targets,
+            bytes_accessed=2 * (programs + targets) * depth + 4 * rows * targets,
+            transcendentals=0,
+        ),
+    )(permuted, target_unit)
 
 
 def shards(
@@ -72,21 +166,10 @@
     unit_rows = normalize_rows(features, squares)
     target_unit = normalize_rows(target_wide, target_squares)
     row_order = jnp.argsort(program_output_index)
-    contract = (((1,), (1,)), ((), ()))
     root_count = math.sqrt(float(targets.shape[1] * narrow_count))
     gathered = lax.all_gather(unit_rows, "wide", axis=0, tiled=True)
     permuted = jnp.take(gathered, row_order, axis=0)
-    chunk = target_unit.shape[0] // SCORE_CHUNKS
-    pieces = []
-    for c in range(SCORE_CHUNKS):
-        part = lax.dot_general(
-            permuted, target_unit[c * chunk:(c + 1) * chunk], contract,
-            preferred_element_type=jnp.float32,
-        ).astype(jnp.bfloat16)
-        pieces.append(
-            lax.psum_scatter(part, "narrow", scatter_dimension=0, tiled=True).astype(jnp.float32)
-        )
-    return jnp.concatenate(pieces, axis=1) * root_count
+    return ring_scores(permuted, target_unit, narrow_count, root_count)
 
 
 def solution(mesh):

time: 279 us -> 239 us (0.86)
  waiting for transfers between devices: 152 us -> 59.3 us
  Pallas kernels: 0 us -> 86 us
  matrix products: 48.1 us -> 7.62 us
  local copies, waits for them, and re-layouts: 21.5 us -> 26.2 us
  other arithmetic: 26.1 us -> 29.5 us
    reduce_scatter x4 -> x0, waiting for transfers between devices: 93.3 us -> none  [shards(): lax.psum_scatter(part, 'narrow', scatter_dimension=0, tiled=True)]
    pallas_call x0 -> x1, Pallas kernels: none -> 86 us  [ring_scores(): pl.pallas_call(functools.partial(ring_kernel, count, root), out_shape=jax...]
    dot_general x4 -> x0, matrix products: 40.5 us -> none  [shards(): lax.dot_general(permuted, target_unit[c * chunk:(c + 1) * chunk], contrac...]
    select_n x0 -> x1, other arithmetic: none -> 7.44 us  [shards(): permuted = jnp.take(gathered, row_order, axis=0)]
    unnamed x12 -> x13, local copies, waits for them, and re-layouts: 0.03 us -> 4.73 us
    mul x1 -> x0, other arithmetic: 4.09 us -> none  [shards(): return jnp.concatenate(pieces, axis=1) * root_count]
  transfers between devices with their start and end apart: 11 -> 7, of which waited for: 8 -> 5; matrix products, arithmetic and copies ran while one was open for 17% -> 8% of each run, Pallas kernels for 0% -> 0%
where the time goes in v2:
time: 239 us; the launch traced here: 238 us
  Pallas kernels  86 us (36%)
  waiting for transfers between devices  59.3 us (25%)
  other arithmetic  29.5 us (12%)
  local copies, waits for them, and re-layouts  26.2 us (11%)
  between operations  13.6 us (6%)
  starting transfers between devices  9 us (4%)
  matrix products  7.62 us (3%)
  blocking collectives  6.57 us (3%)
    pallas_call x1, Pallas kernels, ring_scores(): pl.pallas_call(functools.partial(ring_kernel, count, root), out_shape=jax...  86 us
    all_gather x1, waiting for transfers between devices, shards(): gathered = lax.all_gather(unit_rows, 'wide', axis=0, tiled=True)  31.6 us
    ppermute x6, waiting for transfers between devices, narrow_sum(): total = total + lax.ppermute(piece, 'narrow', perm).astype(jnp.float32)  27.7 us
    gather x1, local copies, waits for them, and re-layouts, shards(): permuted = jnp.take(gathered, row_order, axis=0)  20.8 us
    convert_element_type x2, other arithmetic, normalize_rows(): (features * lax.rsqrt(squares + epsilon)[:, None]).astype(jnp.bfloat16)  9 us
    ppermute x6, starting transfers between devices, narrow_sum(): total = total + lax.ppermute(piece, 'narrow', perm).astype(jnp.float32)  8.99 us
    select_n x1, other arithmetic, shards(): permuted = jnp.take(gathered, row_order, axis=0)  7.44 us
    psum x1, blocking collectives, shards(): lax.psum(jnp.sum(target_wide * target_wide, axis=1), 'narrow')  6.57 us
  transfers between devices with their start and end apart: 7, of which 5 were waited for; matrix products, arithmetic and copies ran while one was open for 8% of the time, Pallas kernels for 0%

profile of v2, /device:TPU:1, one launch (start us, length us, event | category | flops | bytes accessed | tf_op | source)
XLA Modules:
  0.0 237.7 jit_solution(13684031613506867681)
XLA Ops:
  6.5 0.0 copy-start
  6.5 0.0 copy-start.3
  6.5 0.0 all-gather.2.cloned.1.call-start
  6.5 0.0 copy-start.2
  6.5 3.6 %fusion.10 = f32[2048,128]{1,0:T(8,128)S(1)} fusion(bf16[2048,1024]{1,0:T(8,128)(2,1)} %param.9, bf16[1024,128]{1,0:T(8,128)(2,1)} %param.10), kind=kOutput, calls=%fused_computation.30 | convolution fusion | flops 536870912 | bytes 5505024 | tf_op jit(solution)/shard_map/dot_general | solution.py:147
  10.2 0.0 copy-done.3
  10.2 0.7 fusion.11
  10.9 0.0 copy-done
  10.9 0.0 copy-done.2
  11.0 0.0 copy-start.5
  11.0 1.5 fusion.9
  12.5 1.0 pad_maximum_fusion
  13.6 2.0 collective-permute-start
  15.6 2.5 %collective-permute-start.1 = (bf16[2048,144]{0,1:T(8,128)(2,1)S(1)}, bf16[2048,144]{0,1:T(8,128)(2,1)}, u32[]{:S(2)}, u32[]{:S(2)}) collective-permute-start(bf16[2048,144]{0,1:T(8,128)(2,1)S(1)} %get-tuple-element.8), channel_id=1, source_target_pairs={{0,2},{1,3},{2,0},{3,1},{4,6},{5,7},{6,4},{7,5},{8,10},{9,11},{10,... | collective-permute-start | bytes 1769480 | tf_op jit(solution)/shard_map/ppermute | solution.py:36
  18.1 1.1 collective-permute-start.2
  19.2 0.0 copy-done.5
  19.2 0.1 fusion.7
  19.3 10.5 %collective-permute-done = bf16[2048,144]{0,1:T(8,128)(2,1)} collective-permute-done((bf16[2048,144]{0,1:T(8,128)(2,1)}, bf16[2048,144]{0,1:T(8,128)(2,1)}, u32[]{:S(2)}, u32[]{:S(2)}) %collective-permute-start) | collective-permute-done | bytes 589856 | tf_op jit(solution)/shard_map/ppermute | solution.py:36
  29.8 13.9 %collective-permute-done.1 = bf16[2048,144]{0,1:T(8,128)(2,1)} collective-permute-done((bf16[2048,144]{0,1:T(8,128)(2,1)S(1)}, bf16[2048,144]{0,1:T(8,128)(2,1)}, u32[]{:S(2)}, u32[]{:S(2)}) %collective-permute-start.1) | collective-permute-done | bytes 589856 | tf_op jit(solution)/shard_map/ppermute | solution.py:36
  43.8 0.0 collective-permute-done.2
  43.8 1.7 fusion.3
  45.5 0.0 copy-start.4
  45.5 0.1 slice.11
  45.6 0.3 copy.11
  46.0 0.2 reshape.36
  46.2 1.7 multiply_reduce_fusion
  47.9 2.7 %collective-permute-start.5 = (f32[64]{0:T(128)S(1)}, f32[64]{0:T(128)S(1)}, u32[]{:S(2)}, u32[]{:S(2)}) collective-permute-start(f32[64]{0:T(128)S(1)} %get-tuple-element.15), channel_id=1, source_target_pairs={{0,3},{1,0},{2,1},{3,2},{4,7},{5,4},{6,5},{7,6},{8,11},{9,8},{10,9... | collective-permute-start | bytes 776 | tf_op jit(solution)/shard_map/ppermute | solution.py:36
  50.6 0.0 collective-permute-start.4
  50.6 0.7 collective-permute-start.3
  51.3 0.1 collective-permute-done.5
  51.3 3.2 %collective-permute-done.4 = f32[64]{0:T(128)S(1)} collective-permute-done((f32[64]{0:T(128)S(1)}, f32[64]{0:T(128)S(1)}, u32[]{:S(2)}, u32[]{:S(2)}) %collective-permute-start.4) | collective-permute-done | bytes 288 | tf_op jit(solution)/shard_map/ppermute | solution.py:36
  54.5 0.0 collective-permute-done.3
  54.5 0.9 fusion.4
  55.4 0.0 all-gather.2.cloned.1.call-update
  55.4 0.0 copy-done.4
  55.4 5.0 %sort.17 = (s32[2048]{0:T(1024)}, s32[2048]{0:T(1024)S(1)}) sort(s32[2048]{0:T(1024)S(1)} %copy-done.4, s32[2048]{0:T(1024)S(1)} %iota.11), dimensions={0}, to_apply=%region_0.0 | sort | flops 22528 | bytes 32768 | tf_op jit(solution)/shard_map/jit(argsort)/sort | solution.py:168
  60.5 5.1 %fusion = f32[2048]{0:T(1024)S(1)} fusion(bf16[2048,2048]{1,0:T(8,128)(2,1)} %param.15), kind=kLoop, calls=%fused_computation.3 | loop fusion | flops 12580864 | bytes 8396800 | tf_op jit(solution)/shard_map/reduce_sum | solution.py:145
  65.5 6.6 %psum.7 = f32[2048]{0:T(1024)S(1)} all-reduce(f32[2048]{0:T(1024)S(1)} %fusion), channel_id=1, replica_groups=mesh['wide'=32,'narrow'=4] {'narrow'}, use_global_device_ids=true, to_apply=%region_3.4 | all-reduce | flops 2048 | bytes 16384 | tf_op jit(solution)/shard_map/psum | solution.py:145
  72.2 8.1 %fusion.1.t_ref = bf16[2048,2048]{1,0:T(8,128)(2,1)} fusion(bf16[2048,2048]{1,0:T(8,128)(2,1)} %param.15, f32[2048]{0:T(1024)S(1)} %add_rsqrt_fusion), kind=kLoop, calls=%fused_computation.4 | loop fusion | flops 12582912 | bytes 16785408 | tf_op jit(solution)/shard_map/convert_element_type | solution.py:28
  80.3 31.6 %all-gather.2.cloned.1.call-done = bf16[2048,2048]{1,0:T(8,128)(2,1)} async-done(((bf16[64,2048]{1,0:T(8,128)(2,1)}), bf16[2048,2048]{1,0:T(8,128)(2,1)}) %all-gather.2.cloned.1.call-update) | async-done | bytes 8388624 | tf_op jit(solution)/shard_map/all_gather | solution.py:170
  111.9 20.8 %gather_fusion = bf16[2048,2048]{1,0:T(8,128)(2,1)} fusion(bf16[2048,2048]{1,0:T(8,128)(2,1)} %all-gather.2.cloned.1.call-done, s32[2048]{0:T(1024)S(1)} %fusion.8), kind=kCustom, calls=%fused_computation | custom fusion | bytes 16785408 | tf_op jit(solution)/shard_map/jit(_take)/gather | solution.py:171
  132.7 7.4 %broadcast_select_fusion.u_ref = bf16[2048,2048]{1,0:T(8,128)(2,1)} fusion(bf16[2048,2048]{1,0:T(8,128)(2,1)} %gather_fusion, pred[2048]{0:T(1024)(128)(4,1)S(1)} %compare_and_fusion), kind=kLoop, calls=%fused_computation.5 | loop fusion | flops 4194304 | bytes 16779264 | tf_op jit(solution)/shard_map/jit(_take)/select_n | solution.py:171
  140.1 0.0 copy-start.1
  140.1 86.0 %shard_map.82 = f32[512,2048]{1,0:T(8,128)} custom-call(bf16[2048,2048]{1,0:T(8,128)(2,1)} %broadcast_select_fusion.u_ref, bf16[2048,2048]{1,0:T(8,128)(2,1)} %fusion.1.t_ref), custom_call_target="tpu_custom_call" | custom-call | flops 17179869184 | bytes 20971520 | tf_op jit(solution)/shard_map/pallas_call | solution.py:106
  226.1 4.7 %copy.20 = f32[512,2048]{1,0:T(8,128)} copy(f32[512,2048]{1,0:T(8,128)} %shard_map.82) | data formatting | bytes 8388608
  230.8 0.0 copy-done.1
  (9 shorter events, 0.1 us)
Async XLA Ops:
  6.5 4.4 %copy-start = (bf16[1024,128]{1,0:T(8,128)(2,1)S(1)}, bf16[1024,128]{1,0:T(8,128)(2,1)}, u32[]{:S(2)}) copy-start(bf16[1024,128]{1,0:T(8,128)(2,1)} %param.11) | copy-start | bytes 786436
  6.5 3.6 %copy-start.3 = (bf16[128,64]{0,1:T(8,128)(2,1)S(1)}, bf16[128,64]{0,1:T(8,128)(2,1)}, u32[]{:S(2)}) copy-start(bf16[128,64]{0,1:T(8,128)(2,1)} %param.12) | copy-start | bytes 49156
  6.5 105.3 %all-gather.2.cloned.1.call-start = ((), (), s32[]{:S(2)}) async-start(), calls=%async_computation | async-start | bytes 8650752 | tf_op jit(solution)/shard_map/all_gather | solution.py:170
  6.5 4.4 %copy-start.2 = (bf16[2048,1024]{1,0:T(8,128)(2,1)S(1)}, bf16[2048,1024]{1,0:T(8,128)(2,1)}, u32[]{:S(2)}) copy-start(bf16[2048,1024]{1,0:T(8,128)(2,1)} %param.8) | copy-start | bytes 12582916
  11.0 8.3 %copy-start.5 = (s32[64]{0:T(128)S(1)}, s32[64]{0:T(128)}, u32[]{:S(2)}) copy-start(s32[64]{0:T(128)} %param.13) | copy-start | bytes 772
  13.6 16.2 %collective-permute-start = (bf16[2048,144]{0,1:T(8,128)(2,1)}, bf16[2048,144]{0,1:T(8,128)(2,1)}, u32[]{:S(2)}, u32[]{:S(2)}) collective-permute-start(bf16[2048,144]{0,1:T(8,128)(2,1)} %get-tuple-element.7), channel_id=1, source_target_pairs={{0,1},{1,2},{2,3},{3,0},{4,5},{5,6},{6,7},{7,4},{8,9},{9,10},{10,1... | collective-permute-start | bytes 1769480 | tf_op jit(solution)/shard_map/ppermute | solution.py:36
  15.6 28.1 %collective-permute-start.1 = (bf16[2048,144]{0,1:T(8,128)(2,1)S(1)}, bf16[2048,144]{0,1:T(8,128)(2,1)}, u32[]{:S(2)}, u32[]{:S(2)}) collective-permute-start(bf16[2048,144]{0,1:T(8,128)(2,1)S(1)} %get-tuple-element.8), channel_id=1, source_target_pairs={{0,2},{1,3},{2,0},{3,1},{4,6},{5,7},{6,4},{7,5},{8,10},{9,11},{10,... | collective-permute-start | bytes 1769480 | tf_op jit(solution)/shard_map/ppermute | solution.py:36
  18.1 25.7 %collective-permute-start.2 = (bf16[2048,144]{0,1:T(8,128)(2,1)S(1)}, bf16[2048,144]{0,1:T(8,128)(2,1)}, u32[]{:S(2)}, u32[]{:S(2)}) collective-permute-start(bf16[2048,144]{0,1:T(8,128)(2,1)S(1)} %get-tuple-element.9), channel_id=1, source_target_pairs={{0,3},{1,0},{2,1},{3,2},{4,7},{5,4},{6,5},{7,6},{8,11},{9,8},{10,9... | collective-permute-start | bytes 1769480 | tf_op jit(solution)/shard_map/ppermute | solution.py:36
  45.5 9.9 %copy-start.4 = (s32[2048]{0:T(1024)S(1)}, s32[2048]{0:T(1024)}, u32[]{:S(2)}) copy-start(s32[2048]{0:T(1024)} %param.14) | copy-start | bytes 24580
  47.9 3.4 %collective-permute-start.5 = (f32[64]{0:T(128)S(1)}, f32[64]{0:T(128)S(1)}, u32[]{:S(2)}, u32[]{:S(2)}) collective-permute-start(f32[64]{0:T(128)S(1)} %get-tuple-element.15), channel_id=1, source_target_pairs={{0,3},{1,0},{2,1},{3,2},{4,7},{5,4},{6,5},{7,6},{8,11},{9,8},{10,9... | collective-permute-start | bytes 776 | tf_op jit(solution)/shard_map/ppermute | solution.py:36
  50.6 3.9 %collective-permute-start.4 = (f32[64]{0:T(128)S(1)}, f32[64]{0:T(128)S(1)}, u32[]{:S(2)}, u32[]{:S(2)}) collective-permute-start(f32[64]{0:T(128)S(1)} %get-tuple-element.15), channel_id=1, source_target_pairs={{0,2},{1,3},{2,0},{3,1},{4,6},{5,7},{6,4},{7,5},{8,10},{9,11},{10,... | collective-permute-start | bytes 776 | tf_op jit(solution)/shard_map/ppermute | solution.py:36
  50.6 3.9 %collective-permute-start.3 = (f32[64]{0:T(128)S(1)}, f32[64]{0:T(128)S(1)}, u32[]{:S(2)}, u32[]{:S(2)}) collective-permute-start(f32[64]{0:T(128)S(1)} %get-tuple-element.15), channel_id=1, source_target_pairs={{0,1},{1,2},{2,3},{3,0},{4,5},{5,6},{6,7},{7,4},{8,9},{9,10},{10,1... | collective-permute-start | bytes 776 | tf_op jit(solution)/shard_map/ppermute | solution.py:36
  140.1 90.7 %copy-start.1 = (bf16[1024,128]{1,0:T(8,128)(2,1)S(1)}, bf16[1024,128]{1,0:T(8,128)(2,1)}, u32[]{:S(2)}) copy-start(bf16[1024,128]{1,0:T(8,128)(2,1)} %param.11) | copy-start | bytes 786436
Sparse Core Ops, SparseCore 0:
  55.5 56.2 all-gather.1

commit v3 on v2

--- a/solution.py
+++ b/solution.py
@@ -168,7 +168,7 @@
     row_order = jnp.argsort(program_output_index)
     root_count = math.sqrt(float(targets.shape[1] * narrow_count))
     gathered = lax.all_gather(unit_rows, "wide", axis=0, tiled=True)
-    permuted = jnp.take(gathered, row_order, axis=0)
+    permuted = gathered.at[row_order].get(mode="promise_in_bounds", unique_indices=True)
     return ring_scores(permuted, target_unit, narrow_count, root_count)
 
 

time: 239 us -> 231 us (0.967)
  other arithmetic: 29.5 us -> 22 us
    select_n x1 -> x0, other arithmetic: 7.44 us -> none  [shards(): permuted = jnp.take(gathered, row_order, axis=0)]
where the time goes in v3:
time: 231 us; the launch traced here: 230 us
  Pallas kernels  86 us (37%)
  waiting for transfers between devices  59.3 us (26%)
  local copies, waits for them, and re-layouts  26.2 us (11%)
  other arithmetic  22 us (10%)
  between operations  13.6 us (6%)
  starting transfers between devices  9 us (4%)
  matrix products  7.62 us (3%)
  blocking collectives  6.57 us (3%)
    pallas_call x1, Pallas kernels, ring_scores(): pl.pallas_call(functools.partial(ring_kernel, count, root), out_shape=jax...  86 us
    all_gather x1, waiting for transfers between devices, shards(): gathered = lax.all_gather(unit_rows, 'wide', axis=0, tiled=True)  31.6 us
    ppermute x6, waiting for transfers between devices, narrow_sum(): total = total + lax.ppermute(piece, 'narrow', perm).astype(jnp.float32)  27.7 us
    gather x1, local copies, waits for them, and re-layouts, shards(): gathered.at[row_order].get(mode='promise_in_bounds', unique_indices=True)  20.8 us
    ppermute x6, starting transfers between devices, narrow_sum(): total = total + lax.ppermute(piece, 'narrow', perm).astype(jnp.float32)  8.99 us
    convert_element_type x2, other arithmetic, normalize_rows(): (features * lax.rsqrt(squares + epsilon)[:, None]).astype(jnp.bfloat16)  8.99 us
    psum x1, blocking collectives, shards(): lax.psum(jnp.sum(target_wide * target_wide, axis=1), 'narrow')  6.57 us
    reduce_sum x1, other arithmetic, shards(): jnp.sum(target_wide * target_wide, axis=1)  5.08 us
  transfers between devices with their start and end apart: 7, of which 5 were waited for; matrix products, arithmetic and copies ran while one was open for 8% of the time, Pallas kernels for 0%

profile of v3, /device:TPU:1, one launch (start us, length us, event | category | flops | bytes accessed | tf_op | source)
XLA Modules:
  0.0 230.2 jit_solution(6363050248263968816)
XLA Ops:
  6.5 0.0 copy-start
  6.5 0.0 copy-start.2
  6.5 0.0 all-gather.2.cloned.1.call-start
  6.5 0.0 copy-start.1
  6.5 3.6 %fusion.10 = f32[2048,128]{1,0:T(8,128)S(1)} fusion(bf16[2048,1024]{1,0:T(8,128)(2,1)} %param.9, bf16[1024,128]{1,0:T(8,128)(2,1)} %param.10), kind=kOutput, calls=%fused_computation.28 | convolution fusion | flops 536870912 | bytes 5505024 | tf_op jit(solution)/shard_map/dot_general | solution.py:147
  10.2 0.0 copy-done.2
  10.2 0.7 fusion.11
  10.9 0.0 copy-done
  10.9 0.0 copy-done.1
  11.0 0.0 copy-start.4
  11.0 1.5 fusion.9
  12.5 1.0 pad_maximum_fusion
  13.6 2.0 collective-permute-start
  15.6 2.5 %collective-permute-start.1 = (bf16[2048,144]{0,1:T(8,128)(2,1)S(1)}, bf16[2048,144]{0,1:T(8,128)(2,1)}, u32[]{:S(2)}, u32[]{:S(2)}) collective-permute-start(bf16[2048,144]{0,1:T(8,128)(2,1)S(1)} %get-tuple-element.8), channel_id=1, source_target_pairs={{0,2},{1,3},{2,0},{3,1},{4,6},{5,7},{6,4},{7,5},{8,10},{9,11},{10,... | collective-permute-start | bytes 1769480 | tf_op jit(solution)/shard_map/ppermute | solution.py:36
  18.1 1.1 collective-permute-start.2
  19.2 0.0 copy-done.4
  19.2 0.1 fusion.7
  19.3 10.5 %collective-permute-done = bf16[2048,144]{0,1:T(8,128)(2,1)} collective-permute-done((bf16[2048,144]{0,1:T(8,128)(2,1)}, bf16[2048,144]{0,1:T(8,128)(2,1)}, u32[]{:S(2)}, u32[]{:S(2)}) %collective-permute-start) | collective-permute-done | bytes 589856 | tf_op jit(solution)/shard_map/ppermute | solution.py:36
  29.8 13.9 %collective-permute-done.1 = bf16[2048,144]{0,1:T(8,128)(2,1)} collective-permute-done((bf16[2048,144]{0,1:T(8,128)(2,1)S(1)}, bf16[2048,144]{0,1:T(8,128)(2,1)}, u32[]{:S(2)}, u32[]{:S(2)}) %collective-permute-start.1) | collective-permute-done | bytes 589856 | tf_op jit(solution)/shard_map/ppermute | solution.py:36
  43.8 0.0 collective-permute-done.2
  43.8 1.7 fusion.3
  45.5 0.0 copy-start.3
  45.5 0.1 slice.11
  45.6 0.3 copy.11
  46.0 0.2 reshape.31
  46.2 1.7 multiply_reduce_fusion
  47.9 2.7 %collective-permute-start.5 = (f32[64]{0:T(128)S(1)}, f32[64]{0:T(128)S(1)}, u32[]{:S(2)}, u32[]{:S(2)}) collective-permute-start(f32[64]{0:T(128)S(1)} %get-tuple-element.15), channel_id=1, source_target_pairs={{0,3},{1,0},{2,1},{3,2},{4,7},{5,4},{6,5},{7,6},{8,11},{9,8},{10,9... | collective-permute-start | bytes 776 | tf_op jit(solution)/shard_map/ppermute | solution.py:36
  50.6 0.0 collective-permute-start.4
  50.6 0.7 collective-permute-start.3
  51.3 0.1 collective-permute-done.5
  51.3 3.2 %collective-permute-done.4 = f32[64]{0:T(128)S(1)} collective-permute-done((f32[64]{0:T(128)S(1)}, f32[64]{0:T(128)S(1)}, u32[]{:S(2)}, u32[]{:S(2)}) %collective-permute-start.4) | collective-permute-done | bytes 288 | tf_op jit(solution)/shard_map/ppermute | solution.py:36
  54.5 0.0 collective-permute-done.3
  54.5 0.9 fusion.4
  55.4 0.0 all-gather.2.cloned.1.call-update
  55.4 0.0 copy-done.3
  55.4 5.0 %sort.17 = (s32[2048]{0:T(1024)}, s32[2048]{0:T(1024)S(1)}) sort(s32[2048]{0:T(1024)S(1)} %copy-done.3, s32[2048]{0:T(1024)S(1)} %iota.12), dimensions={0}, to_apply=%region_1.0 | sort | flops 22528 | bytes 32768 | tf_op jit(solution)/shard_map/jit(argsort)/sort | solution.py:168
  60.5 5.1 %fusion = f32[2048]{0:T(1024)S(1)} fusion(bf16[2048,2048]{1,0:T(8,128)(2,1)} %param.15), kind=kLoop, calls=%fused_computation.3 | loop fusion | flops 12580864 | bytes 8396800 | tf_op jit(solution)/shard_map/reduce_sum | solution.py:145
  65.5 6.6 %psum.7 = f32[2048]{0:T(1024)S(1)} all-reduce(f32[2048]{0:T(1024)S(1)} %fusion), channel_id=1, replica_groups=mesh['wide'=32,'narrow'=4] {'narrow'}, use_global_device_ids=true, to_apply=%region_3.4 | all-reduce | flops 2048 | bytes 16384 | tf_op jit(solution)/shard_map/psum | solution.py:145
  72.2 8.1 %fusion.1.t_ref = bf16[2048,2048]{1,0:T(8,128)(2,1)} fusion(bf16[2048,2048]{1,0:T(8,128)(2,1)} %param.15, f32[2048]{0:T(1024)S(1)} %add_rsqrt_fusion), kind=kLoop, calls=%fused_computation.4 | loop fusion | flops 12582912 | bytes 16785408 | tf_op jit(solution)/shard_map/convert_element_type | solution.py:28
  80.3 31.6 %all-gather.2.cloned.1.call-done = bf16[2048,2048]{1,0:T(8,128)(2,1)} async-done(((bf16[64,2048]{1,0:T(8,128)(2,1)}), bf16[2048,2048]{1,0:T(8,128)(2,1)}) %all-gather.2.cloned.1.call-update) | async-done | bytes 8388624 | tf_op jit(solution)/shard_map/all_gather | solution.py:170
  111.9 20.8 %gather_fusion = bf16[2048,2048]{1,0:T(8,128)(2,1)} fusion(bf16[2048,2048]{1,0:T(8,128)(2,1)} %all-gather.2.cloned.1.call-done, s32[2048]{0:T(1024)S(1)} %fusion.8), kind=kCustom, calls=%fused_computation | custom fusion | bytes 16785408 | tf_op jit(solution)/shard_map/gather | solution.py:171
  132.6 86.0 %shard_map.82 = f32[512,2048]{1,0:T(8,128)} custom-call(bf16[2048,2048]{1,0:T(8,128)(2,1)} %gather_fusion, bf16[2048,2048]{1,0:T(8,128)(2,1)} %fusion.1.t_ref), custom_call_target="tpu_custom_call" | custom-call | flops 17179869184 | bytes 20971520 | tf_op jit(solution)/shard_map/pallas_call | solution.py:106
  218.6 4.7 %copy.20 = f32[512,2048]{1,0:T(8,128)} copy(f32[512,2048]{1,0:T(8,128)} %shard_map.82) | data formatting | bytes 8388608
  (8 shorter events, 0.1 us)
Async XLA Ops:
  6.5 4.4 %copy-start = (bf16[1024,128]{1,0:T(8,128)(2,1)S(1)}, bf16[1024,128]{1,0:T(8,128)(2,1)}, u32[]{:S(2)}) copy-start(bf16[1024,128]{1,0:T(8,128)(2,1)} %param.11) | copy-start | bytes 786436
  6.5 3.6 %copy-start.2 = (bf16[128,64]{0,1:T(8,128)(2,1)S(1)}, bf16[128,64]{0,1:T(8,128)(2,1)}, u32[]{:S(2)}) copy-start(bf16[128,64]{0,1:T(8,128)(2,1)} %param.12) | copy-start | bytes 49156
  6.5 105.3 %all-gather.2.cloned.1.call-start = ((), (), s32[]{:S(2)}) async-start(), calls=%async_computation | async-start | bytes 8650752 | tf_op jit(solution)/shard_map/all_gather | solution.py:170
  6.5 4.4 %copy-start.1 = (bf16[2048,1024]{1,0:T(8,128)(2,1)S(1)}, bf16[2048,1024]{1,0:T(8,128)(2,1)}, u32[]{:S(2)}) copy-start(bf16[2048,1024]{1,0:T(8,128)(2,1)} %param.8) | copy-start | bytes 12582916
  11.0 8.3 %copy-start.4 = (s32[64]{0:T(128)S(1)}, s32[64]{0:T(128)}, u32[]{:S(2)}) copy-start(s32[64]{0:T(128)} %param.13) | copy-start | bytes 772
  13.6 16.2 %collective-permute-start = (bf16[2048,144]{0,1:T(8,128)(2,1)}, bf16[2048,144]{0,1:T(8,128)(2,1)}, u32[]{:S(2)}, u32[]{:S(2)}) collective-permute-start(bf16[2048,144]{0,1:T(8,128)(2,1)} %get-tuple-element.7), channel_id=1, source_target_pairs={{0,1},{1,2},{2,3},{3,0},{4,5},{5,6},{6,7},{7,4},{8,9},{9,10},{10,1... | collective-permute-start | bytes 1769480 | tf_op jit(solution)/shard_map/ppermute | solution.py:36
  15.6 28.1 %collective-permute-start.1 = (bf16[2048,144]{0,1:T(8,128)(2,1)S(1)}, bf16[2048,144]{0,1:T(8,128)(2,1)}, u32[]{:S(2)}, u32[]{:S(2)}) collective-permute-start(bf16[2048,144]{0,1:T(8,128)(2,1)S(1)} %get-tuple-element.8), channel_id=1, source_target_pairs={{0,2},{1,3},{2,0},{3,1},{4,6},{5,7},{6,4},{7,5},{8,10},{9,11},{10,... | collective-permute-start | bytes 1769480 | tf_op jit(solution)/shard_map/ppermute | solution.py:36
  18.1 25.7 %collective-permute-start.2 = (bf16[2048,144]{0,1:T(8,128)(2,1)S(1)}, bf16[2048,144]{0,1:T(8,128)(2,1)}, u32[]{:S(2)}, u32[]{:S(2)}) collective-permute-start(bf16[2048,144]{0,1:T(8,128)(2,1)S(1)} %get-tuple-element.9), channel_id=1, source_target_pairs={{0,3},{1,0},{2,1},{3,2},{4,7},{5,4},{6,5},{7,6},{8,11},{9,8},{10,9... | collective-permute-start | bytes 1769480 | tf_op jit(solution)/shard_map/ppermute | solution.py:36
  45.5 9.9 %copy-start.3 = (s32[2048]{0:T(1024)S(1)}, s32[2048]{0:T(1024)}, u32[]{:S(2)}) copy-start(s32[2048]{0:T(1024)} %param.14) | copy-start | bytes 24580
  47.9 3.4 %collective-permute-start.5 = (f32[64]{0:T(128)S(1)}, f32[64]{0:T(128)S(1)}, u32[]{:S(2)}, u32[]{:S(2)}) collective-permute-start(f32[64]{0:T(128)S(1)} %get-tuple-element.15), channel_id=1, source_target_pairs={{0,3},{1,0},{2,1},{3,2},{4,7},{5,4},{6,5},{7,6},{8,11},{9,8},{10,9... | collective-permute-start | bytes 776 | tf_op jit(solution)/shard_map/ppermute | solution.py:36
  50.6 3.9 %collective-permute-start.4 = (f32[64]{0:T(128)S(1)}, f32[64]{0:T(128)S(1)}, u32[]{:S(2)}, u32[]{:S(2)}) collective-permute-start(f32[64]{0:T(128)S(1)} %get-tuple-element.15), channel_id=1, source_target_pairs={{0,2},{1,3},{2,0},{3,1},{4,6},{5,7},{6,4},{7,5},{8,10},{9,11},{10,... | collective-permute-start | bytes 776 | tf_op jit(solution)/shard_map/ppermute | solution.py:36
  50.6 3.9 %collective-permute-start.3 = (f32[64]{0:T(128)S(1)}, f32[64]{0:T(128)S(1)}, u32[]{:S(2)}, u32[]{:S(2)}) collective-permute-start(f32[64]{0:T(128)S(1)} %get-tuple-element.15), channel_id=1, source_target_pairs={{0,1},{1,2},{2,3},{3,0},{4,5},{5,6},{6,7},{7,4},{8,9},{9,10},{10,1... | collective-permute-start | bytes 776 | tf_op jit(solution)/shard_map/ppermute | solution.py:36
Sparse Core Ops, SparseCore 0:
  55.5 56.2 all-gather.1

commit v4 on v3

--- a/solution.py
+++ b/solution.py
@@ -39,7 +39,6 @@
 
 def ring_kernel(count, root, u_ref, t_ref, out_ref, send_buf, recv_buf, acc, send_sem, recv_sem):
     me = lax.axis_index("narrow")
-    wide = lax.axis_index("wide")
     right, left = lax.rem(me + 1, count), lax.rem(me + count - 1, count)
     rows = out_ref.shape[0]
     half = t_ref.shape[0] // 2
@@ -47,7 +46,7 @@
 
     barrier = pltpu.get_barrier_semaphore()
     for neighbour in (left, right):
-        pl.semaphore_signal(barrier, inc=1, device_id=(wide, neighbour), device_id_type=MESH)
+        pl.semaphore_signal(barrier, inc=1, device_id={"narrow": neighbour}, device_id_type=MESH)
     pl.semaphore_wait(barrier, 2)
 
     def partial_block(block, direction):
@@ -69,7 +68,7 @@
             dst_ref=recv_buf.at[direction, step],
             send_sem=send_sem.at[direction, step],
             recv_sem=recv_sem.at[direction, step],
-            device_id=(wide, right if direction == 0 else left),
+            device_id={"narrow": right if direction == 0 else left},
             device_id_type=MESH,
         )
 
@@ -167,25 +166,37 @@
     target_unit = normalize_rows(target_wide, target_squares)
     row_order = jnp.argsort(program_output_index)
     root_count = math.sqrt(float(targets.shape[1] * narrow_count))
-    gathered = lax.all_gather(unit_rows, "wide", axis=0, tiled=True)
-    permuted = gathered.at[row_order].get(mode="promise_in_bounds", unique_indices=True)
+    local = unit_rows.shape[0]
+    chips = lax.axis_size("chips")
+    cores = lax.axis_size("core")
+    gathered = lax.all_gather(unit_rows, "chips", axis=0, tiled=True)
+    gathered = lax.all_gather(gathered, "core", axis=0, tiled=True)
+    owner = row_order // local
+    place = (owner % cores) * (chips * local) + (owner // cores) * local + row_order % local
+    permuted = gathered.at[place].get(mode="promise_in_bounds", unique_indices=True)
     return ring_scores(permuted, target_unit, narrow_count, root_count)
 
 
 def solution(mesh):
+    cores = 2
+    wide, narrow = mesh.shape["wide"], mesh.shape["narrow"]
+    split = jax.sharding.Mesh(
+        mesh.devices.reshape(wide // cores, cores, narrow), ("chips", "core", "narrow")
+    )
+    rows = ("chips", "core")
     return jax.shard_map(
         shards,
-        mesh=mesh,
+        mesh=split,
         in_specs=(
-            P("wide", "narrow"),
-            P("wide", "narrow"),
+            P(rows, "narrow"),
+            P(rows, "narrow"),
             P("narrow", None),
             P("narrow", None),
             P(),
-            P("wide"),
+            P(rows),
             P(),
-            P("wide", "narrow"),
+            P(rows, "narrow"),
         ),
-        out_specs=P("narrow", "wide"),
+        out_specs=P("narrow", rows),
         check_vma=False,
     )

time: 231 us -> 254 us (1.100)
  waiting for transfers between devices: 59.3 us -> 82.3 us
  Pallas kernels: 86 us -> 82.6 us
    all_gather x1 -> x2, waiting for transfers between devices: 31.6 us -> 54.6 us  [the longest x1 54.6 us: shards(): gathered = lax.all_gather(unit_rows, 'chips', axis=0, tiled=True)]
    pallas_call x1, Pallas kernels: 86 us -> 82.6 us  [ring_scores(): pl.pallas_call(functools.partial(ring_kernel, count, root), out_shape=jax...]
  transfers between devices with their start and end apart: 7 -> 8, of which waited for: 5 -> 5; matrix products, arithmetic and copies ran while one was open for 8% -> 7% of each run, Pallas kernels for 0% -> 0%
where the time goes in v4:
time: 254 us; the launch traced here: 252 us
  Pallas kernels  82.6 us (33%)
  waiting for transfers between devices  82.3 us (32%)
  local copies, waits for them, and re-layouts  26.2 us (10%)
  other arithmetic  22 us (9%)
  between operations  13.6 us (5%)
  starting transfers between devices  9.04 us (4%)
  blocking collectives  8.69 us (3%)
  matrix products  7.62 us (3%)
    pallas_call x1, Pallas kernels, ring_scores(): pl.pallas_call(functools.partial(ring_kernel, count, root), out_shape=jax...  82.6 us
    all_gather x1, waiting for transfers between devices, shards(): gathered = lax.all_gather(unit_rows, 'chips', axis=0, tiled=True)  54.6 us
    ppermute x6, waiting for transfers between devices, narrow_sum(): total = total + lax.ppermute(piece, 'narrow', perm).astype(jnp.float32)  27.7 us
    gather x1, local copies, waits for them, and re-layouts, shards(): gathered.at[place].get(mode='promise_in_bounds', unique_indices=True)  20.8 us
    ppermute x6, starting transfers between devices, narrow_sum(): total = total + lax.ppermute(piece, 'narrow', perm).astype(jnp.float32)  8.99 us
    convert_element_type x2, other arithmetic, normalize_rows(): (features * lax.rsqrt(squares + epsilon)[:, None]).astype(jnp.bfloat16)  8.98 us
    psum x1, blocking collectives, shards(): lax.psum(jnp.sum(target_wide * target_wide, axis=1), 'narrow')  8.69 us
  transfers between devices with their start and end apart: 8, of which 5 were waited for; matrix products, arithmetic and copies ran while one was open for 7% of the time, Pallas kernels for 0%

profile of v4, /device:TPU:1, one launch (start us, length us, event | category | flops | bytes accessed | tf_op | source)
XLA Modules:
  0.0 252.0 jit_solution(13756706818133604362)
XLA Ops:
  6.5 0.0 copy-start
  6.5 0.0 copy-start.3
  6.5 0.0 all-gather.3.cloned.1.call-start
  6.5 0.0 copy-start.2
  6.5 3.6 %fusion.20 = f32[2048,128]{1,0:T(8,128)S(1)} fusion(bf16[2048,1024]{1,0:T(8,128)(2,1)} %param.9, bf16[1024,128]{1,0:T(8,128)(2,1)} %param.10), kind=kOutput, calls=%fused_computation.50 | convolution fusion | flops 536870912 | bytes 5505024 | tf_op jit(solution)/shard_map/dot_general | solution.py:146
  10.2 0.0 copy-done.3
  10.2 0.7 fusion.21
  10.9 0.0 copy-done
  10.9 0.0 copy-done.2
  11.0 0.0 copy-start.5
  11.0 1.5 fusion.19
  12.5 1.0 pad_maximum_fusion
  13.6 2.0 collective-permute-start
  15.6 2.5 collective-permute-start.1
  18.1 1.1 collective-permute-start.2
  19.2 0.0 copy-done.5
  19.2 0.1 fusion.7
  19.3 10.5 %collective-permute-done = bf16[2048,144]{0,1:T(8,128)(2,1)} collective-permute-done((bf16[2048,144]{0,1:T(8,128)(2,1)}, bf16[2048,144]{0,1:T(8,128)(2,1)}, u32[]{:S(2)}, u32[]{:S(2)}) %collective-permute-start) | collective-permute-done | bytes 589856 | tf_op jit(solution)/shard_map/ppermute | solution.py:36
  29.8 13.9 %collective-permute-done.1 = bf16[2048,144]{0,1:T(8,128)(2,1)} collective-permute-done((bf16[2048,144]{0,1:T(8,128)(2,1)S(1)}, bf16[2048,144]{0,1:T(8,128)(2,1)}, u32[]{:S(2)}, u32[]{:S(2)}) %collective-permute-start.1) | collective-permute-done | bytes 589856 | tf_op jit(solution)/shard_map/ppermute | solution.py:36
  43.8 0.0 collective-permute-done.2
  43.8 1.7 fusion.3
  45.5 0.1 slice.11
  45.6 0.3 copy.11
  45.9 0.2 reshape.31
  46.1 0.0 copy-start.4
  46.2 1.7 multiply_reduce_fusion
  47.9 2.7 %collective-permute-start.5 = (f32[64]{0:T(128)S(1)}, f32[64]{0:T(128)S(1)}, u32[]{:S(2)}, u32[]{:S(2)}) collective-permute-start(f32[64]{0:T(128)S(1)} %get-tuple-element.15), channel_id=1, source_target_pairs={{0,3},{1,0},{2,1},{3,2},{4,7},{5,4},{6,5},{7,6},{8,11},{9,8},{10,9... | collective-permute-start | bytes 776 | tf_op jit(solution)/shard_map/ppermute | solution.py:36
  50.6 0.0 collective-permute-start.4
  50.6 0.7 collective-permute-start.3
  51.3 0.1 collective-permute-done.5
  51.3 3.2 %collective-permute-done.4 = f32[64]{0:T(128)S(1)} collective-permute-done((f32[64]{0:T(128)S(1)}, f32[64]{0:T(128)S(1)}, u32[]{:S(2)}, u32[]{:S(2)}) %collective-permute-start.4) | collective-permute-done | bytes 288 | tf_op jit(solution)/shard_map/ppermute | solution.py:36
  54.5 0.0 collective-permute-done.3
  54.5 0.9 fusion.4
  55.4 0.0 all-gather.3.cloned.1.call-update
  55.4 0.0 all-gather.5.cloned.1.call-start
  55.5 54.6 %all-gather.3.cloned.1.call-done = bf16[1024,2048]{1,0:T(8,128)(2,1)} async-done(((bf16[64,2048]{1,0:T(8,128)(2,1)}), bf16[1024,2048]{1,0:T(8,128)(2,1)}) %all-gather.3.cloned.1.call-update) | async-done | bytes 4194320 | tf_op jit(solution)/shard_map/all_gather | solution.py:172
  110.0 0.0 all-gather.5.cloned.1.call-update
  110.1 0.0 copy-done.4
  110.1 5.0 %sort.17 = (s32[2048]{0:T(1024)}, s32[2048]{0:T(1024)S(1)}) sort(s32[2048]{0:T(1024)S(1)} %copy-done.4, s32[2048]{0:T(1024)S(1)} %iota.12), dimensions={0}, to_apply=%region_1.0 | sort | flops 22528 | bytes 32768 | tf_op jit(solution)/shard_map/jit(argsort)/sort | solution.py:167
  115.1 5.1 %fusion = f32[2048]{0:T(1024)S(1)} fusion(bf16[2048,2048]{1,0:T(8,128)(2,1)} %param.15), kind=kLoop, calls=%fused_computation.3 | loop fusion | flops 12580864 | bytes 8396800 | tf_op jit(solution)/shard_map/reduce_sum | solution.py:144
  120.2 8.7 %psum.7 = f32[2048]{0:T(1024)S(1)} all-reduce(f32[2048]{0:T(1024)S(1)} %fusion), channel_id=1, replica_groups=mesh['chips'=16,'core'=2,'narrow'=4] {'narrow'}, use_global_device_ids=true, to_apply=%region_3.4 | all-reduce | flops 2048 | bytes 16384 | tf_op jit(solution)/shard_map/psum | solution.py:144
  129.0 8.1 %fusion.1.t_ref = bf16[2048,2048]{1,0:T(8,128)(2,1)} fusion(bf16[2048,2048]{1,0:T(8,128)(2,1)} %param.15, f32[2048]{0:T(1024)S(1)} %add_rsqrt_fusion), kind=kLoop, calls=%fused_computation.4 | loop fusion | flops 12582912 | bytes 16785408 | tf_op jit(solution)/shard_map/convert_element_type | solution.py:28
  137.1 0.0 all-gather.5.cloned.1.call-done
  137.1 20.8 %gather_fusion = bf16[2048,2048]{1,0:T(8,128)(2,1)} fusion(bf16[2048,2048]{1,0:T(8,128)(2,1)} %all-gather.5.cloned.1.call-done, s32[2048]{0:T(1024)S(1)} %fusion.12), kind=kCustom, calls=%fused_computation | custom fusion | bytes 16785408 | tf_op jit(solution)/shard_map/gather | solution.py:176
  157.9 0.0 copy-start.1
  157.9 82.6 %shard_map.82 = f32[512,2048]{1,0:T(8,128)} custom-call(bf16[2048,2048]{1,0:T(8,128)(2,1)} %gather_fusion, bf16[2048,2048]{1,0:T(8,128)(2,1)} %fusion.1.t_ref), custom_call_target="tpu_custom_call" | custom-call | flops 17179869184 | bytes 20971520 | tf_op jit(solution)/shard_map/pallas_call | solution.py:105
  240.4 4.7 %copy.20 = f32[512,2048]{1,0:T(8,128)} copy(f32[512,2048]{1,0:T(8,128)} %shard_map.82) | data formatting | bytes 8388608
  245.1 0.0 copy-done.1
  (8 shorter events, 0.1 us)
Async XLA Ops:
  6.5 4.4 %copy-start = (bf16[1024,128]{1,0:T(8,128)(2,1)S(1)}, bf16[1024,128]{1,0:T(8,128)(2,1)}, u32[]{:S(2)}) copy-start(bf16[1024,128]{1,0:T(8,128)(2,1)} %param.11) | copy-start | bytes 786436
  6.5 3.6 %copy-start.3 = (bf16[128,64]{0,1:T(8,128)(2,1)S(1)}, bf16[128,64]{0,1:T(8,128)(2,1)}, u32[]{:S(2)}) copy-start(bf16[128,64]{0,1:T(8,128)(2,1)} %param.12) | copy-start | bytes 49156
  6.5 103.5 %all-gather.3.cloned.1.call-start = ((), (), s32[]{:S(2)}) async-start(), calls=%async_computation | async-start | bytes 4456448 | tf_op jit(solution)/shard_map/all_gather | solution.py:172
  6.5 4.4 %copy-start.2 = (bf16[2048,1024]{1,0:T(8,128)(2,1)S(1)}, bf16[2048,1024]{1,0:T(8,128)(2,1)}, u32[]{:S(2)}) copy-start(bf16[2048,1024]{1,0:T(8,128)(2,1)} %param.8) | copy-start | bytes 12582916
  11.0 8.3 %copy-start.5 = (s32[64]{0:T(128)S(1)}, s32[64]{0:T(128)}, u32[]{:S(2)}) copy-start(s32[64]{0:T(128)} %param.13) | copy-start | bytes 772
  13.6 16.2 %collective-permute-start = (bf16[2048,144]{0,1:T(8,128)(2,1)}, bf16[2048,144]{0,1:T(8,128)(2,1)}, u32[]{:S(2)}, u32[]{:S(2)}) collective-permute-start(bf16[2048,144]{0,1:T(8,128)(2,1)} %get-tuple-element.7), channel_id=1, source_target_pairs={{0,1},{1,2},{2,3},{3,0},{4,5},{5,6},{6,7},{7,4},{8,9},{9,10},{10,1... | collective-permute-start | bytes 1769480 | tf_op jit(solution)/shard_map/ppermute | solution.py:36
  15.6 28.1 %collective-permute-start.1 = (bf16[2048,144]{0,1:T(8,128)(2,1)S(1)}, bf16[2048,144]{0,1:T(8,128)(2,1)}, u32[]{:S(2)}, u32[]{:S(2)}) collective-permute-start(bf16[2048,144]{0,1:T(8,128)(2,1)S(1)} %get-tuple-element.8), channel_id=1, source_target_pairs={{0,2},{1,3},{2,0},{3,1},{4,6},{5,7},{6,4},{7,5},{8,10},{9,11},{10,... | collective-permute-start | bytes 1769480 | tf_op jit(solution)/shard_map/ppermute | solution.py:36
  18.1 25.7 %collective-permute-start.2 = (bf16[2048,144]{0,1:T(8,128)(2,1)S(1)}, bf16[2048,144]{0,1:T(8,128)(2,1)}, u32[]{:S(2)}, u32[]{:S(2)}) collective-permute-start(bf16[2048,144]{0,1:T(8,128)(2,1)S(1)} %get-tuple-element.9), channel_id=1, source_target_pairs={{0,3},{1,0},{2,1},{3,2},{4,7},{5,4},{6,5},{7,6},{8,11},{9,8},{10,9... | collective-permute-start | bytes 1769480 | tf_op jit(solution)/shard_map/ppermute | solution.py:36
  46.1 64.0 %copy-start.4 = (s32[2048]{0:T(1024)S(1)}, s32[2048]{0:T(1024)}, u32[]{:S(2)}) copy-start(s32[2048]{0:T(1024)} %param.14) | copy-start | bytes 24580
  47.9 3.4 %collective-permute-start.5 = (f32[64]{0:T(128)S(1)}, f32[64]{0:T(128)S(1)}, u32[]{:S(2)}, u32[]{:S(2)}) collective-permute-start(f32[64]{0:T(128)S(1)} %get-tuple-element.15), channel_id=1, source_target_pairs={{0,3},{1,0},{2,1},{3,2},{4,7},{5,4},{6,5},{7,6},{8,11},{9,8},{10,9... | collective-permute-start | bytes 776 | tf_op jit(solution)/shard_map/ppermute | solution.py:36
  50.6 3.9 %collective-permute-start.4 = (f32[64]{0:T(128)S(1)}, f32[64]{0:T(128)S(1)}, u32[]{:S(2)}, u32[]{:S(2)}) collective-permute-start(f32[64]{0:T(128)S(1)} %get-tuple-element.15), channel_id=1, source_target_pairs={{0,2},{1,3},{2,0},{3,1},{4,6},{5,7},{6,4},{7,5},{8,10},{9,11},{10,... | collective-permute-start | bytes 776 | tf_op jit(solution)/shard_map/ppermute | solution.py:36
  50.6 3.9 %collective-permute-start.3 = (f32[64]{0:T(128)S(1)}, f32[64]{0:T(128)S(1)}, u32[]{:S(2)}, u32[]{:S(2)}) collective-permute-start(f32[64]{0:T(128)S(1)} %get-tuple-element.15), channel_id=1, source_target_pairs={{0,1},{1,2},{2,3},{3,0},{4,5},{5,6},{6,7},{7,4},{8,9},{9,10},{10,1... | collective-permute-start | bytes 776 | tf_op jit(solution)/shard_map/ppermute | solution.py:36
  55.4 81.6 %all-gather.5.cloned.1.call-start = ((), (), s32[]{:S(2)}) async-start(), calls=%async_computation.1 | async-start | bytes 12582912 | tf_op jit(solution)/shard_map/all_gather | solution.py:173
  157.9 87.3 %copy-start.1 = (bf16[1024,128]{1,0:T(8,128)(2,1)S(1)}, bf16[1024,128]{1,0:T(8,128)(2,1)}, u32[]{:S(2)}) copy-start(bf16[1024,128]{1,0:T(8,128)(2,1)} %param.11) | copy-start | bytes 786436
Sparse Core Ops, SparseCore 0:
  55.5 54.4 all-gather.2
  111.7 22.5 all-gather.4

commit v5 on v3

--- a/solution.py
+++ b/solution.py
@@ -126,6 +126,61 @@
     )(permuted, target_unit)
 
 
+RING = 4
+SLOT = (0, 2, 3, 1)
+
+
+def wide_coords(w):
+    return w // (2 * RING), (w // 2) % RING, w % 2
+
+
+def wide_shift(x, axis_of_core, step):
+    count = 2 * RING * RING
+    perm = []
+    for w in range(count):
+        y, z, c = wide_coords(w)
+        if axis_of_core[c] == "z":
+            z = (z + step) % RING
+        else:
+            y = (y + step) % RING
+        perm.append((w, (y * RING + z) * 2 + c))
+    return lax.ppermute(x, "wide", perm)
+
+
+def ring_gather(block, axis_of_core):
+    half = block.shape[0] // 2
+    from_left = wide_shift(block, axis_of_core, 1)
+    from_right = wide_shift(block, axis_of_core, -1)
+    far = jnp.concatenate(
+        [
+            wide_shift(from_left[:half], axis_of_core, 1),
+            wide_shift(from_right[half:], axis_of_core, -1),
+        ],
+        axis=0,
+    )
+    return jnp.concatenate([block, from_left, from_right, far], axis=0)
+
+
+def wide_gather(unit_rows, row_order):
+    first = ("z", "y")
+    second = ("y", "z")
+    bundle = ring_gather(unit_rows, first)
+    mine = ring_gather(bundle, second)
+    partner = lax.ppermute(mine, "wide", [(w, w ^ 1) for w in range(2 * RING * RING)])
+    gathered = jnp.concatenate([mine, partner], axis=0)
+
+    local = unit_rows.shape[0]
+    y, z, c = wide_coords(lax.axis_index("wide"))
+    slot = jnp.asarray(SLOT, jnp.int32)
+    owner = row_order // local
+    oy, oz, oc = wide_coords(owner)
+    dz, dy = (oz - z) % RING, (oy - y) % RING
+    first_offset = jnp.where(oc == 0, dz, dy)
+    second_offset = jnp.where(oc == 0, dy, dz)
+    block = (oc != c) * (RING * RING) + slot[second_offset] * RING + slot[first_offset]
+    return gathered, block * local + row_order % local
+
+
 def shards(
     layer_input_rows,
     output_gradient_rows,
@@ -167,8 +222,8 @@
     target_unit = normalize_rows(target_wide, target_squares)
     row_order = jnp.argsort(program_output_index)
     root_count = math.sqrt(float(targets.shape[1] * narrow_count))
-    gathered = lax.all_gather(unit_rows, "wide", axis=0, tiled=True)
-    permuted = gathered.at[row_order].get(mode="promise_in_bounds", unique_indices=True)
+    gathered, place = wide_gather(unit_rows, row_order)
+    permuted = gathered.at[place].get(mode="promise_in_bounds", unique_indices=True)
     return ring_scores(permuted, target_unit, narrow_count, root_count)
 
 

time: 231 us -> 238 us (1.030)
  starting transfers between devices: 9 us -> 27.8 us
  local copies, waits for them, and re-layouts: 26.2 us -> 40.3 us
  between operations: 13.6 us -> 0.2 us
  waiting for transfers between devices: 59.3 us -> 46.3 us
  Pallas kernels: 86 us -> 83.1 us
    all_gather x1 -> x0, waiting for transfers between devices: 31.6 us -> none  [shards(): gathered = lax.all_gather(unit_rows, 'wide', axis=0, tiled=True)]
    ppermute x0 -> x9, waiting for transfers between devices: none -> 19.6 us  [the longest x8 19.6 us: wide_shift(): return lax.ppermute(x, 'wide', perm)]
    ppermute x0 -> x9, starting transfers between devices: none -> 18.2 us  [the longest x8 12.6 us: wide_shift(): return lax.ppermute(x, 'wide', perm)]
    unnamed x11 -> x21, local copies, waits for them, and re-layouts: 4.72 us -> 12.9 us
    concatenate x0 -> x2, local copies, waits for them, and re-layouts: none -> 5.85 us  [the longest x1 4.76 us: wide_gather(): gathered = jnp.concatenate([mine, partner], axis=0)]
    pallas_call x1, Pallas kernels: 86 us -> 83.1 us  [ring_scores(): pl.pallas_call(functools.partial(ring_kernel, count, root), out_shape=jax...]
    convert_element_type x2 -> x1, other arithmetic: 8.99 us -> 8.04 us  [normalize_rows(): (features * lax.rsqrt(squares + epsilon)[:, None]).astype(jnp.bfloat16)]
  transfers between devices with their start and end apart: 7 -> 15, of which waited for: 5 -> 8; matrix products, arithmetic and copies ran while one was open for 8% -> 11% of each run, Pallas kernels for 0% -> 0%
where the time goes in v5:
time: 238 us; the launch traced here: 236 us
  Pallas kernels  83.1 us (35%)
  waiting for transfers between devices  46.3 us (19%)
  local copies, waits for them, and re-layouts  40.3 us (17%)
  starting transfers between devices  27.8 us (12%)
  other arithmetic  22 us (9%)
  blocking collectives  8.72 us (4%)
  matrix products  7.61 us (3%)
    pallas_call x1, Pallas kernels, ring_scores(): pl.pallas_call(functools.partial(ring_kernel, count, root), out_shape=jax...  83.1 us
    ppermute x6, waiting for transfers between devices, narrow_sum(): total = total + lax.ppermute(piece, 'narrow', perm).astype(jnp.float32)  26.7 us
    gather x1, local copies, waits for them, and re-layouts, shards(): gathered.at[place].get(mode='promise_in_bounds', unique_indices=True)  20.8 us
    ppermute x8, waiting for transfers between devices, wide_shift(): return lax.ppermute(x, 'wide', perm)  19.6 us
    unnamed x21, local copies, waits for them, and re-layouts  12.9 us
    ppermute x8, starting transfers between devices, wide_shift(): return lax.ppermute(x, 'wide', perm)  12.6 us
    ppermute x6, starting transfers between devices, narrow_sum(): total = total + lax.ppermute(piece, 'narrow', perm).astype(jnp.float32)  9.64 us
    psum x1, blocking collectives, shards(): lax.psum(jnp.sum(target_wide * target_wide, axis=1), 'narrow')  8.72 us
  transfers between devices with their start and end apart: 15, of which 8 were waited for; matrix products, arithmetic and copies ran while one was open for 11% of the time, Pallas kernels for 0%

profile of v5, /device:TPU:1, one launch (start us, length us, event | category | flops | bytes accessed | tf_op | source)
XLA Modules:
  0.0 236.0 jit_solution(6827870712867105532)
XLA Ops:
  0.0 3.6 %fusion.24 = f32[2048,128]{1,0:T(8,128)S(1)} fusion(bf16[2048,1024]{1,0:T(8,128)(2,1)} %param.10, bf16[1024,128]{1,0:T(8,128)(2,1)} %param.11), kind=kOutput, calls=%fused_computation.93 | convolution fusion | flops 536870912 | bytes 5505024 | tf_op jit(solution)/shard_map/dot_general | solution.py:202
  3.7 0.7 fusion.25
  4.4 1.5 fusion.23
  6.0 1.0 pad_maximum_fusion
  7.0 2.1 collective-permute-start
  9.1 2.5 %collective-permute-start.1 = (bf16[2048,144]{0,1:T(8,128)(2,1)S(1)}, bf16[2048,144]{0,1:T(8,128)(2,1)}, u32[]{:S(2)}, u32[]{:S(2)}) collective-permute-start(bf16[2048,144]{0,1:T(8,128)(2,1)S(1)} %get-tuple-element.18), channel_id=1, source_target_pairs={{0,2},{1,3},{2,0},{3,1},{4,6},{5,7},{6,4},{7,5},{8,10},{9,11},{10,... | collective-permute-start | bytes 1769480 | tf_op jit(solution)/shard_map/ppermute | solution.py:36
  11.5 1.1 collective-permute-start.2
  12.8 10.5 %collective-permute-done = bf16[2048,144]{0,1:T(8,128)(2,1)} collective-permute-done((bf16[2048,144]{0,1:T(8,128)(2,1)}, bf16[2048,144]{0,1:T(8,128)(2,1)}, u32[]{:S(2)}, u32[]{:S(2)}) %collective-permute-start) | collective-permute-done | bytes 589856 | tf_op jit(solution)/shard_map/ppermute | solution.py:36
  23.3 13.9 %collective-permute-done.1 = bf16[2048,144]{0,1:T(8,128)(2,1)} collective-permute-done((bf16[2048,144]{0,1:T(8,128)(2,1)S(1)}, bf16[2048,144]{0,1:T(8,128)(2,1)}, u32[]{:S(2)}, u32[]{:S(2)}) %collective-permute-start.1) | collective-permute-done | bytes 589856 | tf_op jit(solution)/shard_map/ppermute | solution.py:36
  37.2 1.7 fusion.3
  39.1 0.3 copy.12
  39.4 0.2 reshape.31
  39.6 1.7 multiply_reduce_fusion
  41.4 0.8 collective-permute-start.3
  42.2 3.0 %collective-permute-start.4 = (f32[64]{0:T(128)S(1)}, f32[64]{0:T(128)S(1)}, u32[]{:S(2)}, u32[]{:S(2)}) collective-permute-start(f32[64]{0:T(128)S(1)} %get-tuple-element.39), channel_id=1, source_target_pairs={{0,2},{1,3},{2,0},{3,1},{4,6},{5,7},{6,4},{7,5},{8,10},{9,11},{10,... | collective-permute-start | bytes 776 | tf_op jit(solution)/shard_map/ppermute | solution.py:36
  45.2 0.1 collective-permute-start.5
  45.4 0.8 collective-permute-done.4
  46.2 1.5 collective-permute-done.5
  47.6 0.9 constant_dynamic-update-slice_fusion.13
  48.5 1.5 collective-permute-start.6
  50.0 1.4 collective-permute-start.7
  51.5 0.7 constant_dynamic-update-slice_fusion.4
  52.2 3.0 %collective-permute-done.6 = bf16[64,2048]{1,0:T(8,128)(2,1)S(1)} collective-permute-done((bf16[64,2048]{1,0:T(8,128)(2,1)S(1)}, bf16[64,2048]{1,0:T(8,128)(2,1)S(1)}, u32[]{:S(2)}, u32[]{:S(2)}) %collective-permute-start.6) | collective-permute-done | bytes 262176 | tf_op jit(solution)/shard_map/ppermute | solution.py:147
  55.2 0.1 collective-permute-start.8
  55.3 2.7 %collective-permute-start.9 = (bf16[32,2048]{1,0:T(8,128)(2,1)S(1)}, bf16[32,2048]{1,0:T(8,128)(2,1)S(1)}, u32[]{:S(2)}, u32[]{:S(2)}) collective-permute-start(bf16[32,2048]{1,0:T(8,128)(2,1)S(1)} %slice.39), channel_id=1, source_target_pairs={{0,24},{4,100},{8,0},{12,108},{16,8},{20,116},{24,16},{28,124},{32... | collective-permute-start | bytes 393224 | tf_op jit(solution)/shard_map/ppermute | solution.py:147
  58.1 0.9 constant_dynamic-update-slice_fusion.12
  58.9 0.9 constant_dynamic-update-slice_fusion.11
  59.8 0.6 collective-permute-done.8
  60.3 0.7 constant_dynamic-update-slice_fusion.10
  61.1 0.7 constant_dynamic-update-slice_fusion.9
  61.8 1.6 collective-permute-start.10
  63.4 2.4 %collective-permute-start.11 = (bf16[256,2048]{1,0:T(8,128)(2,1)S(1)}, bf16[256,2048]{1,0:T(8,128)(2,1)S(1)}, u32[]{:S(2)}, u32[]{:S(2)}) collective-permute-start(bf16[256,2048]{1,0:T(8,128)(2,1)S(1)} %get-tuple-element.33), channel_id=1, source_target_pairs={{0,96},{4,28},{8,104},{12,4},{16,112},{20,12},{24,120},{28,20},{32... | collective-permute-start | bytes 3145736 | tf_op jit(solution)/shard_map/ppermute | solution.py:147
  65.8 12.5 %collective-permute-done.10 = bf16[256,2048]{1,0:T(8,128)(2,1)S(1)} collective-permute-done((bf16[256,2048]{1,0:T(8,128)(2,1)S(1)}, bf16[256,2048]{1,0:T(8,128)(2,1)S(1)}, u32[]{:S(2)}, u32[]{:S(2)}) %collective-permute-start.10) | collective-permute-done | bytes 1048608 | tf_op jit(solution)/shard_map/ppermute | solution.py:147
  78.5 2.7 %collective-permute-start.13 = (bf16[128,2048]{1,0:T(8,128)(2,1)S(1)}, bf16[128,2048]{1,0:T(8,128)(2,1)S(1)}, u32[]{:S(2)}, u32[]{:S(2)}) collective-permute-start(bf16[128,2048]{1,0:T(8,128)(2,1)S(1)} %slice.41), channel_id=1, source_target_pairs={{0,96},{4,28},{8,104},{12,4},{16,112},{20,12},{24,120},{28,20},{32... | collective-permute-start | bytes 1572872 | tf_op jit(solution)/shard_map/ppermute | solution.py:147
  81.2 1.6 constant_dynamic-update-slice_fusion.8
  82.8 1.6 constant_dynamic-update-slice_fusion.7
  84.4 3.6 %collective-permute-done.12 = bf16[128,2048]{1,0:T(8,128)(2,1)S(1)} collective-permute-done((bf16[128,2048]{1,0:T(8,128)(2,1)S(1)}, bf16[128,2048]{1,0:T(8,128)(2,1)S(1)}, u32[]{:S(2)}, u32[]{:S(2)}) %collective-permute-start.12) | collective-permute-done | bytes 524320 | tf_op jit(solution)/shard_map/ppermute | solution.py:147
  88.0 1.1 constant_dynamic-update-slice_fusion.6
  89.1 1.1 constant_dynamic-update-slice_fusion.5
  90.2 5.6 %collective-permute-start.14 = (bf16[1024,2048]{1,0:T(8,128)(2,1)}, bf16[1024,2048]{1,0:T(8,128)(2,1)}, u32[]{:S(2)}, u32[]{:S(2)}) collective-permute-start(bf16[1024,2048]{1,0:T(8,128)(2,1)} %get-tuple-element.13), channel_id=1, source_target_pairs={{0,4},{4,0},{8,12},{12,8},{16,20},{20,16},{24,28},{28,24},{32,36},... | collective-permute-start | bytes 12582920 | tf_op jit(solution)/shard_map/ppermute | solution.py:169
  95.7 5.0 %sort.17 = (s32[2048]{0:T(1024)}, s32[2048]{0:T(1024)S(1)}) sort(s32[2048]{0:T(1024)S(1)} %copy-done.4, s32[2048]{0:T(1024)S(1)} %iota.12), dimensions={0}, to_apply=%region_1.0 | sort | flops 22528 | bytes 32768 | tf_op jit(solution)/shard_map/jit(argsort)/sort | solution.py:223
  100.8 5.1 %fusion = f32[2048]{0:T(1024)S(1)} fusion(bf16[2048,2048]{1,0:T(8,128)(2,1)} %param.16), kind=kLoop, calls=%fused_computation.3 | loop fusion | flops 12580864 | bytes 8396800 | tf_op jit(solution)/shard_map/reduce_sum | solution.py:200
  105.9 8.7 %psum.7 = f32[2048]{0:T(1024)S(1)} all-reduce(f32[2048]{0:T(1024)S(1)} %fusion), channel_id=1, replica_groups=mesh['wide'=32,'narrow'=4] {'narrow'}, use_global_device_ids=true, to_apply=%region_3.4 | all-reduce | flops 2048 | bytes 16384 | tf_op jit(solution)/shard_map/psum | solution.py:200
  114.7 8.0 %fusion.1.t_ref = bf16[2048,2048]{1,0:T(8,128)(2,1)} fusion(bf16[2048,2048]{1,0:T(8,128)(2,1)} %param.16, f32[2048]{0:T(1024)S(1)} %add_rsqrt_fusion), kind=kLoop, calls=%fused_computation.4 | loop fusion | flops 12582912 | bytes 16785408 | tf_op jit(solution)/shard_map/convert_element_type | solution.py:28
  122.7 4.8 %constant_dynamic-update-slice_fusion.14 = bf16[2048,2048]{1,0:T(8,128)(2,1)} fusion(bf16[2048,2048]{1,0:T(8,128)(2,1)} %get-tuple-element.14, bf16[1024,2048]{1,0:T(8,128)(2,1)} %collective-permute-done.14), kind=kLoop, calls=%fused_computation.34 | loop fusion | bytes 8388608 | tf_op jit(solution)/shard_map/concatenate | solution.py:170
  127.5 20.8 %gather_fusion = bf16[2048,2048]{1,0:T(8,128)(2,1)} fusion(bf16[2048,2048]{1,0:T(8,128)(2,1)} %constant_dynamic-update-slice_fusion.14, s32[2048]{0:T(1024)S(1)} %fusion.15), kind=kCustom, calls=%fused_computation | custom fusion | bytes 16785408 | tf_op jit(solution)/shard_map/gather | solution.py:226
  148.3 83.1 %shard_map.91 = f32[512,2048]{1,0:T(8,128)} custom-call(bf16[2048,2048]{1,0:T(8,128)(2,1)} %gather_fusion, bf16[2048,2048]{1,0:T(8,128)(2,1)} %fusion.1.t_ref), custom_call_target="tpu_custom_call" | custom-call | flops 17179869184 | bytes 20971520 | tf_op jit(solution)/shard_map/pallas_call | solution.py:106
  231.3 4.7 %copy.43 = f32[512,2048]{1,0:T(8,128)} copy(f32[512,2048]{1,0:T(8,128)} %shard_map.91) | data formatting | bytes 8388608
  (34 shorter events, 0.5 us)
Async XLA Ops:
  0.0 4.4 %copy-start = (bf16[1024,128]{1,0:T(8,128)(2,1)S(1)}, bf16[1024,128]{1,0:T(8,128)(2,1)}, u32[]{:S(2)}) copy-start(bf16[1024,128]{1,0:T(8,128)(2,1)} %param.12) | copy-start | bytes 786436
  0.0 3.6 %copy-start.3 = (bf16[128,64]{0,1:T(8,128)(2,1)S(1)}, bf16[128,64]{0,1:T(8,128)(2,1)}, u32[]{:S(2)}) copy-start(bf16[128,64]{0,1:T(8,128)(2,1)} %param.13) | copy-start | bytes 49156
  0.0 4.4 %copy-start.2 = (bf16[2048,1024]{1,0:T(8,128)(2,1)S(1)}, bf16[2048,1024]{1,0:T(8,128)(2,1)}, u32[]{:S(2)}) copy-start(bf16[2048,1024]{1,0:T(8,128)(2,1)} %param.9) | copy-start | bytes 12582916
  4.4 8.3 %copy-start.5 = (s32[64]{0:T(128)S(1)}, s32[64]{0:T(128)}, u32[]{:S(2)}) copy-start(s32[64]{0:T(128)} %param.14) | copy-start | bytes 772
  7.0 16.2 %collective-permute-start = (bf16[2048,144]{0,1:T(8,128)(2,1)}, bf16[2048,144]{0,1:T(8,128)(2,1)}, u32[]{:S(2)}, u32[]{:S(2)}) collective-permute-start(bf16[2048,144]{0,1:T(8,128)(2,1)} %get-tuple-element.17), channel_id=1, source_target_pairs={{0,1},{1,2},{2,3},{3,0},{4,5},{5,6},{6,7},{7,4},{8,9},{9,10},{10,1... | collective-permute-start | bytes 1769480 | tf_op jit(solution)/shard_map/ppermute | solution.py:36
  9.1 28.1 %collective-permute-start.1 = (bf16[2048,144]{0,1:T(8,128)(2,1)S(1)}, bf16[2048,144]{0,1:T(8,128)(2,1)}, u32[]{:S(2)}, u32[]{:S(2)}) collective-permute-start(bf16[2048,144]{0,1:T(8,128)(2,1)S(1)} %get-tuple-element.18), channel_id=1, source_target_pairs={{0,2},{1,3},{2,0},{3,1},{4,6},{5,7},{6,4},{7,5},{8,10},{9,11},{10,... | collective-permute-start | bytes 1769480 | tf_op jit(solution)/shard_map/ppermute | solution.py:36
  11.5 25.7 %collective-permute-start.2 = (bf16[2048,144]{0,1:T(8,128)(2,1)S(1)}, bf16[2048,144]{0,1:T(8,128)(2,1)}, u32[]{:S(2)}, u32[]{:S(2)}) collective-permute-start(bf16[2048,144]{0,1:T(8,128)(2,1)S(1)} %get-tuple-element.19), channel_id=1, source_target_pairs={{0,3},{1,0},{2,1},{3,2},{4,7},{5,4},{6,5},{7,6},{8,11},{9,8},{10,9... | collective-permute-start | bytes 1769480 | tf_op jit(solution)/shard_map/ppermute | solution.py:36
  41.4 4.0 %collective-permute-start.3 = (f32[64]{0:T(128)S(1)}, f32[64]{0:T(128)S(1)}, u32[]{:S(2)}, u32[]{:S(2)}) collective-permute-start(f32[64]{0:T(128)S(1)} %get-tuple-element.39), channel_id=1, source_target_pairs={{0,1},{1,2},{2,3},{3,0},{4,5},{5,6},{6,7},{7,4},{8,9},{9,10},{10,1... | collective-permute-start | bytes 776 | tf_op jit(solution)/shard_map/ppermute | solution.py:36
  42.2 4.0 %collective-permute-start.4 = (f32[64]{0:T(128)S(1)}, f32[64]{0:T(128)S(1)}, u32[]{:S(2)}, u32[]{:S(2)}) collective-permute-start(f32[64]{0:T(128)S(1)} %get-tuple-element.39), channel_id=1, source_target_pairs={{0,2},{1,3},{2,0},{3,1},{4,6},{5,7},{6,4},{7,5},{8,10},{9,11},{10,... | collective-permute-start | bytes 776 | tf_op jit(solution)/shard_map/ppermute | solution.py:36
  45.2 2.4 %collective-permute-start.5 = (f32[64]{0:T(128)S(1)}, f32[64]{0:T(128)S(1)}, u32[]{:S(2)}, u32[]{:S(2)}) collective-permute-start(f32[64]{0:T(128)S(1)} %get-tuple-element.39), channel_id=1, source_target_pairs={{0,3},{1,0},{2,1},{3,2},{4,7},{5,4},{6,5},{7,6},{8,11},{9,8},{10,9... | collective-permute-start | bytes 776 | tf_op jit(solution)/shard_map/ppermute | solution.py:36
  48.5 6.7 %collective-permute-start.6 = (bf16[64,2048]{1,0:T(8,128)(2,1)S(1)}, bf16[64,2048]{1,0:T(8,128)(2,1)S(1)}, u32[]{:S(2)}, u32[]{:S(2)}) collective-permute-start(bf16[64,2048]{1,0:T(8,128)(2,1)S(1)} %get-tuple-element.8), channel_id=1, source_target_pairs={{0,8},{4,36},{8,16},{12,44},{16,24},{20,52},{24,0},{28,60},{32,40}... | collective-permute-start | bytes 786440 | tf_op jit(solution)/shard_map/ppermute | solution.py:147
  50.0 5.3 %collective-permute-start.7 = (bf16[64,2048]{1,0:T(8,128)(2,1)S(1)}, bf16[64,2048]{1,0:T(8,128)(2,1)S(1)}, u32[]{:S(2)}, u32[]{:S(2)}) collective-permute-start(bf16[64,2048]{1,0:T(8,128)(2,1)S(1)} %get-tuple-element.8), channel_id=1, source_target_pairs={{0,24},{4,100},{8,0},{12,108},{16,8},{20,116},{24,16},{28,124},{32... | collective-permute-start | bytes 786440 | tf_op jit(solution)/shard_map/ppermute | solution.py:147
  55.2 5.1 %collective-permute-start.8 = (bf16[32,2048]{1,0:T(8,128)(2,1)S(1)}, bf16[32,2048]{1,0:T(8,128)(2,1)S(1)}, u32[]{:S(2)}, u32[]{:S(2)}) collective-permute-start(bf16[32,2048]{1,0:T(8,128)(2,1)S(1)} %slice.38), channel_id=1, source_target_pairs={{0,8},{4,36},{8,16},{12,44},{16,24},{20,52},{24,0},{28,60},{32,40}... | collective-permute-start | bytes 393224 | tf_op jit(solution)/shard_map/ppermute | solution.py:147
  55.3 5.7 %collective-permute-start.9 = (bf16[32,2048]{1,0:T(8,128)(2,1)S(1)}, bf16[32,2048]{1,0:T(8,128)(2,1)S(1)}, u32[]{:S(2)}, u32[]{:S(2)}) collective-permute-start(bf16[32,2048]{1,0:T(8,128)(2,1)S(1)} %slice.39), channel_id=1, source_target_pairs={{0,24},{4,100},{8,0},{12,108},{16,8},{20,116},{24,16},{28,124},{32... | collective-permute-start | bytes 393224 | tf_op jit(solution)/shard_map/ppermute | solution.py:147
  61.8 16.5 %collective-permute-start.10 = (bf16[256,2048]{1,0:T(8,128)(2,1)S(1)}, bf16[256,2048]{1,0:T(8,128)(2,1)S(1)}, u32[]{:S(2)}, u32[]{:S(2)}) collective-permute-start(bf16[256,2048]{1,0:T(8,128)(2,1)S(1)} %get-tuple-element.33), channel_id=1, source_target_pairs={{0,32},{4,12},{8,40},{12,20},{16,48},{20,28},{24,56},{28,4},{32,64... | collective-permute-start | bytes 3145736 | tf_op jit(solution)/shard_map/ppermute | solution.py:147
  63.4 15.0 %collective-permute-start.11 = (bf16[256,2048]{1,0:T(8,128)(2,1)S(1)}, bf16[256,2048]{1,0:T(8,128)(2,1)S(1)}, u32[]{:S(2)}, u32[]{:S(2)}) collective-permute-start(bf16[256,2048]{1,0:T(8,128)(2,1)S(1)} %get-tuple-element.33), channel_id=1, source_target_pairs={{0,96},{4,28},{8,104},{12,4},{16,112},{20,12},{24,120},{28,20},{32... | collective-permute-start | bytes 3145736 | tf_op jit(solution)/shard_map/ppermute | solution.py:147
  78.4 9.6 %collective-permute-start.12 = (bf16[128,2048]{1,0:T(8,128)(2,1)S(1)}, bf16[128,2048]{1,0:T(8,128)(2,1)S(1)}, u32[]{:S(2)}, u32[]{:S(2)}) collective-permute-start(bf16[128,2048]{1,0:T(8,128)(2,1)S(1)} %slice.40), channel_id=1, source_target_pairs={{0,32},{4,12},{8,40},{12,20},{16,48},{20,28},{24,56},{28,4},{32,64... | collective-permute-start | bytes 1572872 | tf_op jit(solution)/shard_map/ppermute | solution.py:147
  78.5 10.6 %collective-permute-start.13 = (bf16[128,2048]{1,0:T(8,128)(2,1)S(1)}, bf16[128,2048]{1,0:T(8,128)(2,1)S(1)}, u32[]{:S(2)}, u32[]{:S(2)}) collective-permute-start(bf16[128,2048]{1,0:T(8,128)(2,1)S(1)} %slice.41), channel_id=1, source_target_pairs={{0,96},{4,28},{8,104},{12,4},{16,112},{20,12},{24,120},{28,20},{32... | collective-permute-start | bytes 1572872 | tf_op jit(solution)/shard_map/ppermute | solution.py:147
  81.2 14.5 %copy-start.4 = (s32[2048]{0:T(1024)S(1)}, s32[2048]{0:T(1024)}, u32[]{:S(2)}) copy-start(s32[2048]{0:T(1024)} %param.15) | copy-start | bytes 24580
  90.2 32.5 %collective-permute-start.14 = (bf16[1024,2048]{1,0:T(8,128)(2,1)}, bf16[1024,2048]{1,0:T(8,128)(2,1)}, u32[]{:S(2)}, u32[]{:S(2)}) collective-permute-start(bf16[1024,2048]{1,0:T(8,128)(2,1)} %get-tuple-element.13), channel_id=1, source_target_pairs={{0,4},{4,0},{8,12},{12,8},{16,20},{20,16},{24,28},{28,24},{32,36},... | collective-permute-start | bytes 12582920 | tf_op jit(solution)/shard_map/ppermute | solution.py:169
  148.3 87.8 %copy-start.1 = (bf16[1024,128]{1,0:T(8,128)(2,1)S(1)}, bf16[1024,128]{1,0:T(8,128)(2,1)}, u32[]{:S(2)}) copy-start(bf16[1024,128]{1,0:T(8,128)(2,1)} %param.12) | copy-start | bytes 786436

commit v6 on v5

--- a/solution.py
+++ b/solution.py
@@ -197,7 +197,16 @@
     length = layer_input_rows.shape[0] // programs
 
     target_wide = targets.astype(jnp.float32)
-    target_squares = lax.psum(jnp.sum(target_wide * target_wide, axis=1), "narrow")
+    target_squares = jnp.sum(target_wide * target_wide, axis=1)
+    target_squares = narrow_sum(
+        target_squares, lambda dest: target_squares, narrow_count, narrow_index, jnp.float32
+    )
+    target_unit = normalize_rows(target_wide, target_squares)
+    row_order = jnp.zeros_like(program_output_index).at[program_output_index].set(
+        jnp.arange(program_output_index.shape[0], dtype=jnp.int32),
+        mode="promise_in_bounds",
+        unique_indices=True,
+    )
 
     reduced_sums = jnp.dot(
         output_gradient_rows, adapter_up_weight, preferred_element_type=jnp.float32
@@ -213,14 +222,15 @@
         return jnp.concatenate([quarter, in_part], axis=1)
 
     summed_parts = narrow_sum(send_for(narrow_index), send_for, narrow_count, narrow_index)
+    summed_parts, target_unit, row_order = lax.optimization_barrier(
+        (summed_parts, target_unit, row_order)
+    )
     quarter = summed_parts[:, :quarter_cols]
     in_all = summed_parts[:, quarter_cols:]
     features = program_features(quarter, in_all, lengths, length)
     squares = jnp.sum(features * features, axis=1)
     squares = narrow_sum(squares, lambda dest: squares, narrow_count, narrow_index, jnp.float32)
     unit_rows = normalize_rows(features, squares)
-    target_unit = normalize_rows(target_wide, target_squares)
-    row_order = jnp.argsort(program_output_index)
     root_count = math.sqrt(float(targets.shape[1] * narrow_count))
     gathered, place = wide_gather(unit_rows, row_order)
     permuted = gathered.at[place].get(mode="promise_in_bounds", unique_indices=True)

time: 238 us -> 230 us (0.966)
  blocking collectives: 8.72 us -> 0 us
  local copies, waits for them, and re-layouts: 40.3 us -> 48.4 us
  waiting for transfers between devices: 46.3 us -> 38.7 us
  other arithmetic: 22 us -> 16.9 us
  starting transfers between devices: 27.8 us -> 31.3 us
    ppermute x6 -> x9, waiting for transfers between devices: 26.7 us -> 12 us  [narrow_sum(): total = total + lax.ppermute(piece, 'narrow', perm).astype(jnp.float32)]
    psum x1 -> x0, blocking collectives: 8.72 us -> none  [shards(): lax.psum(jnp.sum(target_wide * target_wide, axis=1), 'narrow')]
    scatter x0 -> x1, local copies, waits for them, and re-layouts: none -> 8.05 us  [shards(): jnp.zeros_like(program_output_index).at[program_output_index]]
    ppermute x1, waiting for transfers between devices: 0.01 us -> 7.07 us  [wide_gather(): lax.ppermute(mine, 'wide', [(w, w ^ 1) for w in range(2 * RING * RING)])]
    sort x1 -> x0, other arithmetic: 5.04 us -> none  [shards(): row_order = jnp.argsort(program_output_index)]
    ppermute x6 -> x9, starting transfers between devices: 9.64 us -> 13.3 us  [narrow_sum(): total = total + lax.ppermute(piece, 'narrow', perm).astype(jnp.float32)]
    unnamed x21 -> x23, local copies, waits for them, and re-layouts: 12.9 us -> 12.9 us
  transfers between devices with their start and end apart: 15 -> 18, of which waited for: 8 -> 9; matrix products, arithmetic and copies ran while one was open for 11% -> 13% of each run, Pallas kernels for 0% -> 0%
where the time goes in v6:
time: 230 us; the launch traced here: 228 us
  Pallas kernels  85 us (37%)
  local copies, waits for them, and re-layouts  48.4 us (21%)
  waiting for transfers between devices  38.7 us (17%)
  starting transfers between devices  31.3 us (14%)
  other arithmetic  16.9 us (7%)
  matrix products  7.59 us (3%)
    pallas_call x1, Pallas kernels, ring_scores(): pl.pallas_call(functools.partial(ring_kernel, count, root), out_shape=jax...  85 us
    gather x1, local copies, waits for them, and re-layouts, shards(): gathered.at[place].get(mode='promise_in_bounds', unique_indices=True)  20.8 us
    ppermute x8, waiting for transfers between devices, wide_shift(): return lax.ppermute(x, 'wide', perm)  19.6 us
    ppermute x9, starting transfers between devices, narrow_sum(): total = total + lax.ppermute(piece, 'narrow', perm).astype(jnp.float32)  13.3 us
    unnamed x23, local copies, waits for them, and re-layouts  12.9 us
    ppermute x8, starting transfers between devices, wide_shift(): return lax.ppermute(x, 'wide', perm)  12.4 us
    ppermute x9, waiting for transfers between devices, narrow_sum(): total = total + lax.ppermute(piece, 'narrow', perm).astype(jnp.float32)  12 us
    convert_element_type x1, other arithmetic, normalize_rows(): (features * lax.rsqrt(squares + epsilon)[:, None]).astype(jnp.bfloat16)  8.07 us
  transfers between devices with their start and end apart: 18, of which 9 were waited for; matrix products, arithmetic and copies ran while one was open for 13% of the time, Pallas kernels for 0%

profile of v6, /device:TPU:1, one launch (start us, length us, event | category | flops | bytes accessed | tf_op | source)
XLA Modules:
  0.0 228.1 jit_solution(667493126158168000)
XLA Ops:
  0.0 5.1 %fusion = f32[2048]{0:T(1024)S(1)} fusion(bf16[2048,2048]{1,0:T(8,128)(2,1)} %param.16), kind=kLoop, calls=%fused_computation.4 | loop fusion | flops 12580864 | bytes 8396800 | tf_op jit(solution)/shard_map/reduce_sum | solution.py:200
  5.2 2.1 collective-permute-start.3
  7.3 2.5 %collective-permute-start.4 = (f32[2048]{0:T(1024)S(1)}, f32[2048]{0:T(1024)S(1)}, u32[]{:S(2)}, u32[]{:S(2)}) collective-permute-start(f32[2048]{0:T(1024)S(1)} %fusion), channel_id=1, source_target_pairs={{0,2},{1,3},{2,0},{3,1},{4,6},{5,7},{6,4},{7,5},{8,10},{9,11},{10,... | collective-permute-start | bytes 24584 | tf_op jit(solution)/shard_map/ppermute | solution.py:36
  9.7 1.2 collective-permute-start.5
  10.9 3.6 %fusion.26 = f32[2048,128]{1,0:T(8,128)S(1)} fusion(bf16[2048,1024]{1,0:T(8,128)(2,1)} %param.10, bf16[1024,128]{1,0:T(8,128)(2,1)S(1)} %copy-done.3), kind=kOutput, calls=%fused_computation.97 | convolution fusion | flops 536870912 | bytes 5505024 | tf_op jit(solution)/shard_map/dot_general | solution.py:211
  14.5 0.7 fusion.27
  15.3 1.5 fusion.25
  16.8 1.0 pad_maximum_fusion
  17.9 0.3 collective-permute-start
  18.2 0.9 collective-permute-start.1
  19.2 8.0 %scatter_custom_fusion = s32[2048]{0:T(1024)S(1)} fusion(s32[2048]{0:T(1024)S(1)} %compare_select_fusion.3, s32[2048]{0:T(1024)S(1)} %iota.10, s32[]{:T(128)} %constant.126.clone.1), kind=kCustom, calls=%fused_computation.92 | custom fusion | bytes 8196 | tf_op jit(solution)/shard_map/scatter | solution.py:205
  27.3 1.6 collective-permute-start.2
  28.9 8.1 %fusion.1.t_ref = bf16[2048,2048]{1,0:T(8,128)(2,1)} fusion(bf16[2048,2048]{1,0:T(8,128)(2,1)} %param.16, f32[2048]{0:T(1024)S(1)} %add_rsqrt_fusion), kind=kLoop, calls=%fused_computation.5 | loop fusion | flops 12582912 | bytes 16785408 | tf_op jit(solution)/shard_map/convert_element_type | solution.py:28
  37.0 7.2 %collective-permute-done.1 = bf16[2048,144]{0,1:T(8,128)(2,1)} collective-permute-done((bf16[2048,144]{0,1:T(8,128)(2,1)S(1)}, bf16[2048,144]{0,1:T(8,128)(2,1)}, u32[]{:S(2)}, u32[]{:S(2)}) %collective-permute-start.1) | collective-permute-done | bytes 589856 | tf_op jit(solution)/shard_map/ppermute | solution.py:36
  44.2 2.4 %collective-permute-done.2 = bf16[2048,144]{0,1:T(8,128)(2,1)S(1)} collective-permute-done((bf16[2048,144]{0,1:T(8,128)(2,1)S(1)}, bf16[2048,144]{0,1:T(8,128)(2,1)S(1)}, u32[]{:S(2)}, u32[]{:S(2)}) %collective-permute-start.2) | collective-permute-done | bytes 589856 | tf_op jit(solution)/shard_map/ppermute | solution.py:36
  46.5 1.5 fusion.3
  48.2 0.3 copy.12
  48.8 1.7 multiply_reduce_fusion
  50.5 0.5 collective-permute-start.6
  51.0 4.3 %collective-permute-start.7 = (f32[64]{0:T(128)S(1)}, f32[64]{0:T(128)S(1)}, u32[]{:S(2)}, u32[]{:S(2)}) collective-permute-start(f32[64]{0:T(128)S(1)} %get-tuple-element.43), channel_id=1, source_target_pairs={{0,2},{1,3},{2,0},{3,1},{4,6},{5,7},{6,4},{7,5},{8,10},{9,11},{10,... | collective-permute-start | bytes 776 | tf_op jit(solution)/shard_map/ppermute | solution.py:36
  55.3 0.9 collective-permute-done.7
  56.3 1.5 collective-permute-done.8
  57.7 0.9 constant_dynamic-update-slice_fusion.13
  58.6 1.3 collective-permute-start.9
  59.9 1.4 collective-permute-start.10
  61.4 0.7 constant_dynamic-update-slice_fusion.4
  62.1 3.0 %collective-permute-done.9 = bf16[64,2048]{1,0:T(8,128)(2,1)S(1)} collective-permute-done((bf16[64,2048]{1,0:T(8,128)(2,1)S(1)}, bf16[64,2048]{1,0:T(8,128)(2,1)S(1)}, u32[]{:S(2)}, u32[]{:S(2)}) %collective-permute-start.9) | collective-permute-done | bytes 262176 | tf_op jit(solution)/shard_map/ppermute | solution.py:147
  65.2 2.7 %collective-permute-start.12 = (bf16[32,2048]{1,0:T(8,128)(2,1)S(1)}, bf16[32,2048]{1,0:T(8,128)(2,1)S(1)}, u32[]{:S(2)}, u32[]{:S(2)}) collective-permute-start(bf16[32,2048]{1,0:T(8,128)(2,1)S(1)} %slice.37), channel_id=1, source_target_pairs={{0,24},{4,100},{8,0},{12,108},{16,8},{20,116},{24,16},{28,124},{32... | collective-permute-start | bytes 393224 | tf_op jit(solution)/shard_map/ppermute | solution.py:147
  68.0 0.9 constant_dynamic-update-slice_fusion.12
  68.8 0.9 constant_dynamic-update-slice_fusion.11
  69.7 0.5 collective-permute-done.11
  70.2 0.7 constant_dynamic-update-slice_fusion.10
  70.9 0.7 constant_dynamic-update-slice_fusion.9
  71.7 1.6 collective-permute-start.13
  73.3 2.4 %collective-permute-start.14 = (bf16[256,2048]{1,0:T(8,128)(2,1)S(1)}, bf16[256,2048]{1,0:T(8,128)(2,1)S(1)}, u32[]{:S(2)}, u32[]{:S(2)}) collective-permute-start(bf16[256,2048]{1,0:T(8,128)(2,1)S(1)} %get-tuple-element.37), channel_id=1, source_target_pairs={{0,96},{4,28},{8,104},{12,4},{16,112},{20,12},{24,120},{28,20},{32... | collective-permute-start | bytes 3145736 | tf_op jit(solution)/shard_map/ppermute | solution.py:147
  75.7 12.5 %collective-permute-done.13 = bf16[256,2048]{1,0:T(8,128)(2,1)S(1)} collective-permute-done((bf16[256,2048]{1,0:T(8,128)(2,1)S(1)}, bf16[256,2048]{1,0:T(8,128)(2,1)S(1)}, u32[]{:S(2)}, u32[]{:S(2)}) %collective-permute-start.13) | collective-permute-done | bytes 1048608 | tf_op jit(solution)/shard_map/ppermute | solution.py:147
  88.4 2.7 %collective-permute-start.16 = (bf16[128,2048]{1,0:T(8,128)(2,1)S(1)}, bf16[128,2048]{1,0:T(8,128)(2,1)S(1)}, u32[]{:S(2)}, u32[]{:S(2)}) collective-permute-start(bf16[128,2048]{1,0:T(8,128)(2,1)S(1)} %slice.39), channel_id=1, source_target_pairs={{0,96},{4,28},{8,104},{12,4},{16,112},{20,12},{24,120},{28,20},{32... | collective-permute-start | bytes 1572872 | tf_op jit(solution)/shard_map/ppermute | solution.py:147
  91.1 1.6 constant_dynamic-update-slice_fusion.8
  92.7 1.6 constant_dynamic-update-slice_fusion.7
  94.3 3.6 %collective-permute-done.15 = bf16[128,2048]{1,0:T(8,128)(2,1)S(1)} collective-permute-done((bf16[128,2048]{1,0:T(8,128)(2,1)S(1)}, bf16[128,2048]{1,0:T(8,128)(2,1)S(1)}, u32[]{:S(2)}, u32[]{:S(2)}) %collective-permute-start.15) | collective-permute-done | bytes 524320 | tf_op jit(solution)/shard_map/ppermute | solution.py:147
  97.9 1.1 constant_dynamic-update-slice_fusion.6
  99.0 1.1 constant_dynamic-update-slice_fusion.5
  100.1 5.6 %collective-permute-start.17 = (bf16[1024,2048]{1,0:T(8,128)(2,1)}, bf16[1024,2048]{1,0:T(8,128)(2,1)}, u32[]{:S(2)}, u32[]{:S(2)}) collective-permute-start(bf16[1024,2048]{1,0:T(8,128)(2,1)} %get-tuple-element.17), channel_id=1, source_target_pairs={{0,4},{4,0},{8,12},{12,8},{16,20},{20,16},{24,28},{28,24},{32,36},... | collective-permute-start | bytes 12582920 | tf_op jit(solution)/shard_map/ppermute | solution.py:169
  105.7 7.1 %collective-permute-done.17 = bf16[1024,2048]{1,0:T(8,128)(2,1)} collective-permute-done((bf16[1024,2048]{1,0:T(8,128)(2,1)}, bf16[1024,2048]{1,0:T(8,128)(2,1)}, u32[]{:S(2)}, u32[]{:S(2)}) %collective-permute-start.17) | collective-permute-done | bytes 4194336 | tf_op jit(solution)/shard_map/ppermute | solution.py:169
  112.8 4.8 %constant_dynamic-update-slice_fusion.14 = bf16[2048,2048]{1,0:T(8,128)(2,1)} fusion(bf16[2048,2048]{1,0:T(8,128)(2,1)} %get-tuple-element.18, bf16[1024,2048]{1,0:T(8,128)(2,1)} %collective-permute-done.17), kind=kLoop, calls=%fused_computation.35 | loop fusion | bytes 8388608 | tf_op jit(solution)/shard_map/concatenate | solution.py:170
  117.6 20.8 %gather_fusion = bf16[2048,2048]{1,0:T(8,128)(2,1)} fusion(bf16[2048,2048]{1,0:T(8,128)(2,1)} %constant_dynamic-update-slice_fusion.14, s32[2048]{0:T(1024)S(1)} %fusion.15), kind=kCustom, calls=%fused_computation | custom fusion | bytes 16785408 | tf_op jit(solution)/shard_map/gather | solution.py:236
  138.3 85.0 %shard_map.91 = f32[512,2048]{1,0:T(8,128)} custom-call(bf16[2048,2048]{1,0:T(8,128)(2,1)} %gather_fusion, bf16[2048,2048]{1,0:T(8,128)(2,1)} %fusion.1.t_ref), custom_call_target="tpu_custom_call" | custom-call | flops 17179869184 | bytes 20971520 | tf_op jit(solution)/shard_map/pallas_call | solution.py:106
  223.4 4.7 %copy.43 = f32[512,2048]{1,0:T(8,128)} copy(f32[512,2048]{1,0:T(8,128)} %shard_map.91) | data formatting | bytes 8388608
  (42 shorter events, 0.8 us)
Async XLA Ops:
  0.0 15.2 %copy-start = (bf16[1024,128]{1,0:T(8,128)(2,1)S(1)}, bf16[1024,128]{1,0:T(8,128)(2,1)}, u32[]{:S(2)}) copy-start(bf16[1024,128]{1,0:T(8,128)(2,1)} %param.12) | copy-start | bytes 786436
  0.0 10.9 %copy-start.3 = (bf16[1024,128]{1,0:T(8,128)(2,1)S(1)}, bf16[1024,128]{1,0:T(8,128)(2,1)}, u32[]{:S(2)}) copy-start(bf16[1024,128]{1,0:T(8,128)(2,1)} %param.11) | copy-start | bytes 786436
  5.1 9.3 %copy-start.4 = (bf16[128,64]{0,1:T(8,128)(2,1)S(1)}, bf16[128,64]{0,1:T(8,128)(2,1)}, u32[]{:S(2)}) copy-start(bf16[128,64]{0,1:T(8,128)(2,1)} %param.13) | copy-start | bytes 49156
  5.2 22.1 %collective-permute-start.3 = (f32[2048]{0:T(1024)S(1)}, f32[2048]{0:T(1024)S(1)}, u32[]{:S(2)}, u32[]{:S(2)}) collective-permute-start(f32[2048]{0:T(1024)S(1)} %fusion), channel_id=1, source_target_pairs={{0,1},{1,2},{2,3},{3,0},{4,5},{5,6},{6,7},{7,4},{8,9},{9,10},{10,1... | collective-permute-start | bytes 24584 | tf_op jit(solution)/shard_map/ppermute | solution.py:36
  7.3 21.6 %collective-permute-start.4 = (f32[2048]{0:T(1024)S(1)}, f32[2048]{0:T(1024)S(1)}, u32[]{:S(2)}, u32[]{:S(2)}) collective-permute-start(f32[2048]{0:T(1024)S(1)} %fusion), channel_id=1, source_target_pairs={{0,2},{1,3},{2,0},{3,1},{4,6},{5,7},{6,4},{7,5},{8,10},{9,11},{10,... | collective-permute-start | bytes 24584 | tf_op jit(solution)/shard_map/ppermute | solution.py:36
  9.7 19.2 %collective-permute-start.5 = (f32[2048]{0:T(1024)S(1)}, f32[2048]{0:T(1024)S(1)}, u32[]{:S(2)}, u32[]{:S(2)}) collective-permute-start(f32[2048]{0:T(1024)S(1)} %fusion), channel_id=1, source_target_pairs={{0,3},{1,0},{2,1},{3,2},{4,7},{5,4},{6,5},{7,6},{8,11},{9,8},{10,9... | collective-permute-start | bytes 24584 | tf_op jit(solution)/shard_map/ppermute | solution.py:36
  10.9 4.4 %copy-start.2 = (bf16[2048,1024]{1,0:T(8,128)(2,1)S(1)}, bf16[2048,1024]{1,0:T(8,128)(2,1)}, u32[]{:S(2)}) copy-start(bf16[2048,1024]{1,0:T(8,128)(2,1)} %param.9) | copy-start | bytes 12582916
  15.2 3.8 %copy-start.6 = (s32[64]{0:T(128)S(1)}, s32[64]{0:T(128)}, u32[]{:S(2)}) copy-start(s32[64]{0:T(128)} %param.14) | copy-start | bytes 772
  15.3 3.9 %copy-start.5 = (s32[2048]{0:T(1024)S(1)}, s32[2048]{0:T(1024)}, u32[]{:S(2)}) copy-start(s32[2048]{0:T(1024)} %param.15) | copy-start | bytes 24580
  17.9 19.1 %collective-permute-start = (bf16[2048,144]{0,1:T(8,128)(2,1)}, bf16[2048,144]{0,1:T(8,128)(2,1)}, u32[]{:S(2)}, u32[]{:S(2)}) collective-permute-start(bf16[2048,144]{0,1:T(8,128)(2,1)} %get-tuple-element.21), channel_id=1, source_target_pairs={{0,1},{1,2},{2,3},{3,0},{4,5},{5,6},{6,7},{7,4},{8,9},{9,10},{10,1... | collective-permute-start | bytes 1769480 | tf_op jit(solution)/shard_map/ppermute | solution.py:36
  18.2 26.0 %collective-permute-start.1 = (bf16[2048,144]{0,1:T(8,128)(2,1)S(1)}, bf16[2048,144]{0,1:T(8,128)(2,1)}, u32[]{:S(2)}, u32[]{:S(2)}) collective-permute-start(bf16[2048,144]{0,1:T(8,128)(2,1)S(1)} %get-tuple-element.22), channel_id=1, source_target_pairs={{0,2},{1,3},{2,0},{3,1},{4,6},{5,7},{6,4},{7,5},{8,10},{9,11},{10,... | collective-permute-start | bytes 1769480 | tf_op jit(solution)/shard_map/ppermute | solution.py:36
  27.3 19.3 %collective-permute-start.2 = (bf16[2048,144]{0,1:T(8,128)(2,1)S(1)}, bf16[2048,144]{0,1:T(8,128)(2,1)S(1)}, u32[]{:S(2)}, u32[]{:S(2)}) collective-permute-start(bf16[2048,144]{0,1:T(8,128)(2,1)S(1)} %get-tuple-element.23), channel_id=1, source_target_pairs={{0,3},{1,0},{2,1},{3,2},{4,7},{5,4},{6,5},{7,6},{8,11},{9,8},{10,9... | collective-permute-start | bytes 1769480 | tf_op jit(solution)/shard_map/ppermute | solution.py:36
  50.5 4.8 %collective-permute-start.6 = (f32[64]{0:T(128)S(1)}, f32[64]{0:T(128)S(1)}, u32[]{:S(2)}, u32[]{:S(2)}) collective-permute-start(f32[64]{0:T(128)S(1)} %get-tuple-element.43), channel_id=1, source_target_pairs={{0,1},{1,2},{2,3},{3,0},{4,5},{5,6},{6,7},{7,4},{8,9},{9,10},{10,1... | collective-permute-start | bytes 776 | tf_op jit(solution)/shard_map/ppermute | solution.py:36
  51.0 5.3 %collective-permute-start.7 = (f32[64]{0:T(128)S(1)}, f32[64]{0:T(128)S(1)}, u32[]{:S(2)}, u32[]{:S(2)}) collective-permute-start(f32[64]{0:T(128)S(1)} %get-tuple-element.43), channel_id=1, source_target_pairs={{0,2},{1,3},{2,0},{3,1},{4,6},{5,7},{6,4},{7,5},{8,10},{9,11},{10,... | collective-permute-start | bytes 776 | tf_op jit(solution)/shard_map/ppermute | solution.py:36
  55.3 2.4 %collective-permute-start.8 = (f32[64]{0:T(128)S(1)}, f32[64]{0:T(128)S(1)}, u32[]{:S(2)}, u32[]{:S(2)}) collective-permute-start(f32[64]{0:T(128)S(1)} %get-tuple-element.43), channel_id=1, source_target_pairs={{0,3},{1,0},{2,1},{3,2},{4,7},{5,4},{6,5},{7,6},{8,11},{9,8},{10,9... | collective-permute-start | bytes 776 | tf_op jit(solution)/shard_map/ppermute | solution.py:36
  58.6 6.5 %collective-permute-start.9 = (bf16[64,2048]{1,0:T(8,128)(2,1)S(1)}, bf16[64,2048]{1,0:T(8,128)(2,1)S(1)}, u32[]{:S(2)}, u32[]{:S(2)}) collective-permute-start(bf16[64,2048]{1,0:T(8,128)(2,1)S(1)} %get-tuple-element.12), channel_id=1, source_target_pairs={{0,8},{4,36},{8,16},{12,44},{16,24},{20,52},{24,0},{28,60},{32,40}... | collective-permute-start | bytes 786440 | tf_op jit(solution)/shard_map/ppermute | solution.py:147
  59.9 5.3 %collective-permute-start.10 = (bf16[64,2048]{1,0:T(8,128)(2,1)S(1)}, bf16[64,2048]{1,0:T(8,128)(2,1)S(1)}, u32[]{:S(2)}, u32[]{:S(2)}) collective-permute-start(bf16[64,2048]{1,0:T(8,128)(2,1)S(1)} %get-tuple-element.12), channel_id=1, source_target_pairs={{0,24},{4,100},{8,0},{12,108},{16,8},{20,116},{24,16},{28,124},{32... | collective-permute-start | bytes 786440 | tf_op jit(solution)/shard_map/ppermute | solution.py:147
  65.1 5.1 %collective-permute-start.11 = (bf16[32,2048]{1,0:T(8,128)(2,1)S(1)}, bf16[32,2048]{1,0:T(8,128)(2,1)S(1)}, u32[]{:S(2)}, u32[]{:S(2)}) collective-permute-start(bf16[32,2048]{1,0:T(8,128)(2,1)S(1)} %slice.36), channel_id=1, source_target_pairs={{0,8},{4,36},{8,16},{12,44},{16,24},{20,52},{24,0},{28,60},{32,40}... | collective-permute-start | bytes 393224 | tf_op jit(solution)/shard_map/ppermute | solution.py:147
  65.2 5.7 %collective-permute-start.12 = (bf16[32,2048]{1,0:T(8,128)(2,1)S(1)}, bf16[32,2048]{1,0:T(8,128)(2,1)S(1)}, u32[]{:S(2)}, u32[]{:S(2)}) collective-permute-start(bf16[32,2048]{1,0:T(8,128)(2,1)S(1)} %slice.37), channel_id=1, source_target_pairs={{0,24},{4,100},{8,0},{12,108},{16,8},{20,116},{24,16},{28,124},{32... | collective-permute-start | bytes 393224 | tf_op jit(solution)/shard_map/ppermute | solution.py:147
  71.7 16.5 %collective-permute-start.13 = (bf16[256,2048]{1,0:T(8,128)(2,1)S(1)}, bf16[256,2048]{1,0:T(8,128)(2,1)S(1)}, u32[]{:S(2)}, u32[]{:S(2)}) collective-permute-start(bf16[256,2048]{1,0:T(8,128)(2,1)S(1)} %get-tuple-element.37), channel_id=1, source_target_pairs={{0,32},{4,12},{8,40},{12,20},{16,48},{20,28},{24,56},{28,4},{32,64... | collective-permute-start | bytes 3145736 | tf_op jit(solution)/shard_map/ppermute | solution.py:147
  73.3 15.0 %collective-permute-start.14 = (bf16[256,2048]{1,0:T(8,128)(2,1)S(1)}, bf16[256,2048]{1,0:T(8,128)(2,1)S(1)}, u32[]{:S(2)}, u32[]{:S(2)}) collective-permute-start(bf16[256,2048]{1,0:T(8,128)(2,1)S(1)} %get-tuple-element.37), channel_id=1, source_target_pairs={{0,96},{4,28},{8,104},{12,4},{16,112},{20,12},{24,120},{28,20},{32... | collective-permute-start | bytes 3145736 | tf_op jit(solution)/shard_map/ppermute | solution.py:147
  88.3 9.6 %collective-permute-start.15 = (bf16[128,2048]{1,0:T(8,128)(2,1)S(1)}, bf16[128,2048]{1,0:T(8,128)(2,1)S(1)}, u32[]{:S(2)}, u32[]{:S(2)}) collective-permute-start(bf16[128,2048]{1,0:T(8,128)(2,1)S(1)} %slice.38), channel_id=1, source_target_pairs={{0,32},{4,12},{8,40},{12,20},{16,48},{20,28},{24,56},{28,4},{32,64... | collective-permute-start | bytes 1572872 | tf_op jit(solution)/shard_map/ppermute | solution.py:147
  88.4 10.6 %collective-permute-start.16 = (bf16[128,2048]{1,0:T(8,128)(2,1)S(1)}, bf16[128,2048]{1,0:T(8,128)(2,1)S(1)}, u32[]{:S(2)}, u32[]{:S(2)}) collective-permute-start(bf16[128,2048]{1,0:T(8,128)(2,1)S(1)} %slice.39), channel_id=1, source_target_pairs={{0,96},{4,28},{8,104},{12,4},{16,112},{20,12},{24,120},{28,20},{32... | collective-permute-start | bytes 1572872 | tf_op jit(solution)/shard_map/ppermute | solution.py:147
  100.1 12.7 %collective-permute-start.17 = (bf16[1024,2048]{1,0:T(8,128)(2,1)}, bf16[1024,2048]{1,0:T(8,128)(2,1)}, u32[]{:S(2)}, u32[]{:S(2)}) collective-permute-start(bf16[1024,2048]{1,0:T(8,128)(2,1)} %get-tuple-element.17), channel_id=1, source_target_pairs={{0,4},{4,0},{8,12},{12,8},{16,20},{20,16},{24,28},{28,24},{32,36},... | collective-permute-start | bytes 12582920 | tf_op jit(solution)/shard_map/ppermute | solution.py:169
  138.3 89.7 %copy-start.1 = (bf16[1024,128]{1,0:T(8,128)(2,1)S(1)}, bf16[1024,128]{1,0:T(8,128)(2,1)}, u32[]{:S(2)}) copy-start(bf16[1024,128]{1,0:T(8,128)(2,1)} %param.12) | copy-start | bytes 786436

commit v7 on v6

--- a/solution.py
+++ b/solution.py
@@ -37,25 +37,42 @@
     return total
 
 
-def ring_kernel(count, root, u_ref, t_ref, out_ref, send_buf, recv_buf, acc, send_sem, recv_sem):
+def ring_kernel(count, root, place_ref, mine_ref, partner_ref, t_ref, out_ref,
+                ordered, send_buf, recv_buf, acc, send_sem, recv_sem):
     me = lax.axis_index("narrow")
-    wide = lax.axis_index("wide")
     right, left = lax.rem(me + 1, count), lax.rem(me + count - 1, count)
     rows = out_ref.shape[0]
     half = t_ref.shape[0] // 2
+    held = mine_ref.shape[0]
     tiles = rows // TILE
 
     barrier = pltpu.get_barrier_semaphore()
     for neighbour in (left, right):
-        pl.semaphore_signal(barrier, inc=1, device_id=(wide, neighbour), device_id_type=MESH)
+        pl.semaphore_signal(barrier, inc=1, device_id={"narrow": neighbour}, device_id_type=MESH)
     pl.semaphore_wait(barrier, 2)
+
+    def order_block(block):
+        def body(i, carry):
+            start = pl.multiple_of(block * rows + i * TILE, TILE)
+            wanted = place_ref[pl.ds(start, TILE), :]
+            columns = lax.broadcasted_iota(jnp.int32, (TILE, held), 1)
+            pick_mine = (wanted == columns).astype(jnp.bfloat16)
+            pick_partner = (wanted == columns + held).astype(jnp.bfloat16)
+            picked = jnp.dot(pick_mine, mine_ref[...], preferred_element_type=jnp.float32)
+            picked = picked + jnp.dot(
+                pick_partner, partner_ref[...], preferred_element_type=jnp.float32
+            )
+            ordered[pl.ds(start, TILE), :] = picked.astype(jnp.bfloat16)
+            return carry
+
+        lax.fori_loop(0, tiles, body, 0)
 
     def partial_block(block, direction):
         targets = t_ref[direction * half:(direction + 1) * half, :]
 
         def body(i, carry):
             start = pl.multiple_of(block * rows + i * TILE, TILE)
-            lhs = u_ref[pl.ds(start, TILE), :]
+            lhs = ordered[pl.ds(start, TILE), :]
             acc[direction, pl.ds(pl.multiple_of(i * TILE, TILE), TILE), :] = lax.dot_general(
                 lhs, targets, (((1,), (1,)), ((), ())), preferred_element_type=jnp.float32
             )
@@ -69,14 +86,23 @@
             dst_ref=recv_buf.at[direction, step],
             send_sem=send_sem.at[direction, step],
             recv_sem=recv_sem.at[direction, step],
-            device_id=(wide, right if direction == 0 else left),
+            device_id={"narrow": right if direction == 0 else left},
             device_id_type=MESH,
         )
 
+    built = set()
+
+    def need(offset):
+        if offset not in built:
+            built.add(offset)
+            order_block(lax.rem(me + offset, count))
+
     for step in range(count - 1):
-        blocks = (lax.rem(me + 2 * count - 1 - step, count), lax.rem(me + 1 + step, count))
-        for direction in range(2):
-            partial_block(blocks[direction], direction)
+        offsets = ((2 * count - 1 - step) % count, (1 + step) % count)
+        for direction in range(2):
+            need(offsets[direction])
+        for direction in range(2):
+            partial_block(lax.rem(me + offsets[direction], count), direction)
         for direction in range(2):
             if step == 0:
                 send_buf[direction, step] = acc[direction].astype(jnp.bfloat16)
@@ -86,6 +112,7 @@
                     acc[direction] + recv_buf[direction, step - 1].astype(jnp.float32)
                 ).astype(jnp.bfloat16)
             copy_of(direction, step).start()
+    need(0)
     for direction in range(2):
         partial_block(me, direction)
     for direction in range(2):
@@ -98,17 +125,19 @@
             copy_of(direction, step).wait_send()
 
 
-def ring_scores(permuted, target_unit, count, root):
-    programs, depth = permuted.shape
+def ring_scores(place, mine, partner, target_unit, count, root):
+    programs = place.shape[0]
+    depth = mine.shape[1]
     rows = programs // count
     targets = target_unit.shape[0]
     half = targets // 2
     return pl.pallas_call(
         functools.partial(ring_kernel, count, root),
         out_shape=jax.ShapeDtypeStruct((rows, targets), jnp.float32),
-        in_specs=[pl.BlockSpec(memory_space=pltpu.VMEM)] * 2,
+        in_specs=[pl.BlockSpec(memory_space=pltpu.VMEM)] * 4,
         out_specs=pl.BlockSpec(memory_space=pltpu.VMEM),
         scratch_shapes=[
+            pltpu.VMEM((programs, depth), jnp.bfloat16),
             pltpu.VMEM((2, count - 1, rows, half), jnp.bfloat16),
             pltpu.VMEM((2, count - 1, rows, half), jnp.bfloat16),
             pltpu.VMEM((2, rows, half), jnp.float32),
@@ -116,14 +145,14 @@
             pltpu.SemaphoreType.DMA((2, count - 1)),
         ],
         compiler_params=pltpu.CompilerParams(
-            collective_id=0, has_side_effects=True, vmem_limit_bytes=60 * 1024 * 1024
+            collective_id=0, has_side_effects=True, vmem_limit_bytes=62 * 1024 * 1024
         ),
         cost_estimate=pl.CostEstimate(
-            flops=2 * programs * depth * targets,
-            bytes_accessed=2 * (programs + targets) * depth + 4 * rows * targets,
+            flops=4 * programs * depth * targets,
+            bytes_accessed=2 * (2 * programs + targets) * depth + 4 * rows * targets,
             transcendentals=0,
         ),
-    )(permuted, target_unit)
+    )(place.reshape(programs, 1), mine, partner, target_unit)
 
 
 RING = 4
@@ -167,7 +196,6 @@
     bundle = ring_gather(unit_rows, first)
     mine = ring_gather(bundle, second)
     partner = lax.ppermute(mine, "wide", [(w, w ^ 1) for w in range(2 * RING * RING)])
-    gathered = jnp.concatenate([mine, partner], axis=0)
 
     local = unit_rows.shape[0]
     y, z, c = wide_coords(lax.axis_index("wide"))
@@ -178,7 +206,7 @@
     first_offset = jnp.where(oc == 0, dz, dy)
     second_offset = jnp.where(oc == 0, dy, dz)
     block = (oc != c) * (RING * RING) + slot[second_offset] * RING + slot[first_offset]
-    return gathered, block * local + row_order % local
+    return mine, partner, block * local + row_order % local
 
 
 def shards(
@@ -232,9 +260,8 @@
     squares = narrow_sum(squares, lambda dest: squares, narrow_count, narrow_index, jnp.float32)
     unit_rows = normalize_rows(features, squares)
     root_count = math.sqrt(float(targets.shape[1] * narrow_count))
-    gathered, place = wide_gather(unit_rows, row_order)
-    permuted = gathered.at[place].get(mode="promise_in_bounds", unique_indices=True)
-    return ring_scores(permuted, target_unit, narrow_count, root_count)
+    mine, partner, place = wide_gather(unit_rows, row_order)
+    return ring_scores(place, mine, partner, target_unit, narrow_count, root_count)
 
 
 def solution(mesh):

time: 230 us -> 216 us (0.939)
  local copies, waits for them, and re-layouts: 48.4 us -> 22.2 us
  Pallas kernels: 85 us -> 94.5 us
  starting transfers between devices: 31.3 us -> 33.8 us
    gather x1 -> x0, local copies, waits for them, and re-layouts: 20.8 us -> none  [shards(): gathered.at[place].get(mode='promise_in_bounds', unique_indices=True)]
    pallas_call x1, Pallas kernels: 85 us -> 94.5 us  [ring_scores(): pl.pallas_call(functools.partial(ring_kernel, count, root), out_shape=jax...]
    concatenate x1 -> x0, local copies, waits for them, and re-layouts: 4.79 us -> none  [wide_gather(): gathered = jnp.concatenate([mine, partner], axis=0)]
    ppermute x8, waiting for transfers between devices: 19.6 us -> 23 us  [wide_shift(): return lax.ppermute(x, 'wide', perm)]
    unnamed x23 -> x20, local copies, waits for them, and re-layouts: 12.9 us -> 10.5 us
  transfers between devices with their start and end apart: 18 -> 18, of which waited for: 9 -> 9; matrix products, arithmetic and copies ran while one was open for 13% -> 14% of each run, Pallas kernels for 0% -> 0%
where the time goes in v7:
time: 216 us; the launch traced here: 215 us
  Pallas kernels  94.5 us (44%)
  waiting for transfers between devices  40.1 us (19%)
  starting transfers between devices  33.8 us (16%)
  local copies, waits for them, and re-layouts  22.2 us (10%)
  other arithmetic  16.2 us (8%)
  matrix products  7.6 us (4%)
    pallas_call x1, Pallas kernels, ring_scores(): pl.pallas_call(functools.partial(ring_kernel, count, root), out_shape=jax...  94.5 us
    ppermute x8, waiting for transfers between devices, wide_shift(): return lax.ppermute(x, 'wide', perm)  23 us
    ppermute x8, starting transfers between devices, wide_shift(): return lax.ppermute(x, 'wide', perm)  13.2 us
    ppermute x9, starting transfers between devices, narrow_sum(): total = total + lax.ppermute(piece, 'narrow', perm).astype(jnp.float32)  13.2 us
    ppermute x9, waiting for transfers between devices, narrow_sum(): total = total + lax.ppermute(piece, 'narrow', perm).astype(jnp.float32)  11.5 us
    unnamed x20, local copies, waits for them, and re-layouts  10.5 us
    convert_element_type x1, other arithmetic, normalize_rows(): (features * lax.rsqrt(squares + epsilon)[:, None]).astype(jnp.bfloat16)  8.06 us
    scatter x1, local copies, waits for them, and re-layouts, shards(): jnp.zeros_like(program_output_index).at[program_output_index]  8.05 us
  transfers between devices with their start and end apart: 18, of which 9 were waited for; matrix products, arithmetic and copies ran while one was open for 14% of the time, Pallas kernels for 0%

profile of v7, /device:TPU:1, one launch (start us, length us, event | category | flops | bytes accessed | tf_op | source)
XLA Modules:
  0.0 214.6 jit_solution(3585977880419276808)
XLA Ops:
  0.0 5.1 %fusion = f32[2048]{0:T(1024)S(1)} fusion(bf16[2048,2048]{1,0:T(8,128)(2,1)} %param.16), kind=kLoop, calls=%fused_computation.3 | loop fusion | flops 12580864 | bytes 8396800 | tf_op jit(solution)/shard_map/reduce_sum | solution.py:228
  5.2 3.4 %collective-permute-start.5 = (f32[2048]{0:T(1024)S(1)}, f32[2048]{0:T(1024)S(1)}, u32[]{:S(2)}, u32[]{:S(2)}) collective-permute-start(f32[2048]{0:T(1024)S(1)} %fusion), channel_id=1, source_target_pairs={{0,3},{1,0},{2,1},{3,2},{4,7},{5,4},{6,5},{7,6},{8,11},{9,8},{10,9... | collective-permute-start | bytes 24584 | tf_op jit(solution)/shard_map/ppermute | solution.py:36
  8.5 0.5 collective-permute-start.4
  9.1 0.6 collective-permute-start.3
  9.7 3.6 %fusion.25 = f32[2048,128]{1,0:T(8,128)S(1)} fusion(bf16[2048,1024]{1,0:T(8,128)(2,1)} %param.10, bf16[1024,128]{1,0:T(8,128)(2,1)S(1)} %copy-done.2), kind=kOutput, calls=%fused_computation.84 | convolution fusion | flops 536870912 | bytes 5505024 | tf_op jit(solution)/shard_map/dot_general | solution.py:239
  13.3 0.7 fusion.26
  14.1 1.5 fusion.24
  15.6 1.0 pad_maximum_fusion
  16.7 1.5 collective-permute-start
  18.2 1.7 collective-permute-start.1
  20.0 8.0 %scatter_custom_fusion = s32[2048]{0:T(1024)S(1)} fusion(s32[2048]{0:T(1024)S(1)} %compare_select_fusion.2, s32[2048]{0:T(1024)S(1)} %iota.10, s32[]{:T(128)} %constant.126.clone.1), kind=kCustom, calls=%fused_computation.79 | custom fusion | bytes 8196 | tf_op jit(solution)/shard_map/scatter | solution.py:233
  28.1 0.7 collective-permute-start.2
  28.9 8.1 %fusion.1.t_ref = bf16[2048,2048]{1,0:T(8,128)(2,1)} fusion(bf16[2048,2048]{1,0:T(8,128)(2,1)} %param.16, f32[2048]{0:T(1024)S(1)} %add_rsqrt_fusion), kind=kLoop, calls=%fused_computation.4 | loop fusion | flops 12582912 | bytes 16785408 | tf_op jit(solution)/shard_map/convert_element_type | solution.py:28
  36.9 7.8 %collective-permute-done.1 = bf16[2048,144]{0,1:T(8,128)(2,1)} collective-permute-done((bf16[2048,144]{0,1:T(8,128)(2,1)S(1)}, bf16[2048,144]{0,1:T(8,128)(2,1)}, u32[]{:S(2)}, u32[]{:S(2)}) %collective-permute-start.1) | collective-permute-done | bytes 589856 | tf_op jit(solution)/shard_map/ppermute | solution.py:36
  44.7 0.1 collective-permute-done.2
  44.8 1.5 fusion.3
  46.4 0.1 slice.19
  46.5 0.3 copy.12
  46.8 0.2 reshape.35
  47.0 1.7 multiply_reduce_fusion
  48.8 3.6 %collective-permute-start.8 = (f32[64]{0:T(128)S(1)}, f32[64]{0:T(128)S(1)}, u32[]{:S(2)}, u32[]{:S(2)}) collective-permute-start(f32[64]{0:T(128)S(1)} %get-tuple-element.29), channel_id=1, source_target_pairs={{0,3},{1,0},{2,1},{3,2},{4,7},{5,4},{6,5},{7,6},{8,11},{9,8},{10,9... | collective-permute-start | bytes 776 | tf_op jit(solution)/shard_map/ppermute | solution.py:36
  52.4 1.0 collective-permute-start.7
  53.4 2.8 %collective-permute-done.7 = f32[64]{0:T(128)S(1)} collective-permute-done((f32[64]{0:T(128)S(1)}, f32[64]{0:T(128)S(1)}, u32[]{:S(2)}, u32[]{:S(2)}) %collective-permute-start.7) | collective-permute-done | bytes 288 | tf_op jit(solution)/shard_map/ppermute | solution.py:36
  56.3 0.7 collective-permute-done.6
  57.0 0.2 constant_dynamic-update-slice_fusion.4
  57.2 2.8 %collective-permute-start.10 = (bf16[64,2048]{1,0:T(8,128)(2,1)S(1)}, bf16[64,2048]{1,0:T(8,128)(2,1)S(1)}, u32[]{:S(2)}, u32[]{:S(2)}) collective-permute-start(bf16[64,2048]{1,0:T(8,128)(2,1)S(1)} %get-tuple-element.12), channel_id=1, source_target_pairs={{0,24},{4,100},{8,0},{12,108},{16,8},{20,116},{24,16},{28,124},{32... | collective-permute-start | bytes 786440 | tf_op jit(solution)/shard_map/ppermute | solution.py:176
  60.1 0.7 constant_dynamic-update-slice_fusion.13
  60.8 2.6 %collective-permute-done.10 = bf16[64,2048]{1,0:T(8,128)(2,1)S(1)} collective-permute-done((bf16[64,2048]{1,0:T(8,128)(2,1)S(1)}, bf16[64,2048]{1,0:T(8,128)(2,1)S(1)}, u32[]{:S(2)}, u32[]{:S(2)}) %collective-permute-start.10) | collective-permute-done | bytes 262176 | tf_op jit(solution)/shard_map/ppermute | solution.py:176
  63.4 3.2 %collective-permute-start.12 = (bf16[32,2048]{1,0:T(8,128)(2,1)S(1)}, bf16[32,2048]{1,0:T(8,128)(2,1)S(1)}, u32[]{:S(2)}, u32[]{:S(2)}) collective-permute-start(bf16[32,2048]{1,0:T(8,128)(2,1)S(1)} %slice.35), channel_id=1, source_target_pairs={{0,24},{4,100},{8,0},{12,108},{16,8},{20,116},{24,16},{28,124},{32... | collective-permute-start | bytes 393224 | tf_op jit(solution)/shard_map/ppermute | solution.py:176
  66.7 0.7 constant_dynamic-update-slice_fusion.3
  67.4 0.7 constant_dynamic-update-slice_fusion.2
  68.2 3.5 %collective-permute-done.11 = bf16[32,2048]{1,0:T(8,128)(2,1)S(1)} collective-permute-done((bf16[32,2048]{1,0:T(8,128)(2,1)S(1)}, bf16[32,2048]{1,0:T(8,128)(2,1)S(1)}, u32[]{:S(2)}, u32[]{:S(2)}) %collective-permute-start.11) | collective-permute-done | bytes 131104 | tf_op jit(solution)/shard_map/ppermute | solution.py:176
  71.7 0.7 constant_dynamic-update-slice_fusion.1
  72.4 0.7 constant_dynamic-update-slice_fusion
  73.0 1.6 collective-permute-start.13
  74.7 2.7 %collective-permute-start.14 = (bf16[256,2048]{1,0:T(8,128)(2,1)S(1)}, bf16[256,2048]{1,0:T(8,128)(2,1)S(1)}, u32[]{:S(2)}, u32[]{:S(2)}) collective-permute-start(bf16[256,2048]{1,0:T(8,128)(2,1)S(1)} %get-tuple-element.23), channel_id=1, source_target_pairs={{0,96},{4,28},{8,104},{12,4},{16,112},{20,12},{24,120},{28,20},{32... | collective-permute-start | bytes 3145736 | tf_op jit(solution)/shard_map/ppermute | solution.py:176
  77.4 12.5 %collective-permute-done.13 = bf16[256,2048]{1,0:T(8,128)(2,1)S(1)} collective-permute-done((bf16[256,2048]{1,0:T(8,128)(2,1)S(1)}, bf16[256,2048]{1,0:T(8,128)(2,1)S(1)}, u32[]{:S(2)}, u32[]{:S(2)}) %collective-permute-start.13) | collective-permute-done | bytes 1048608 | tf_op jit(solution)/shard_map/ppermute | solution.py:176
  90.0 2.7 %collective-permute-start.16 = (bf16[128,2048]{1,0:T(8,128)(2,1)S(1)}, bf16[128,2048]{1,0:T(8,128)(2,1)S(1)}, u32[]{:S(2)}, u32[]{:S(2)}) collective-permute-start(bf16[128,2048]{1,0:T(8,128)(2,1)S(1)} %slice.37), channel_id=1, source_target_pairs={{0,96},{4,28},{8,104},{12,4},{16,112},{20,12},{24,120},{28,20},{32... | collective-permute-start | bytes 1572872 | tf_op jit(solution)/shard_map/ppermute | solution.py:176
  92.8 1.0 constant_dynamic-update-slice_fusion.8
  93.8 1.0 constant_dynamic-update-slice_fusion.7
  94.8 4.4 %collective-permute-done.15 = bf16[128,2048]{1,0:T(8,128)(2,1)S(1)} collective-permute-done((bf16[128,2048]{1,0:T(8,128)(2,1)S(1)}, bf16[128,2048]{1,0:T(8,128)(2,1)S(1)}, u32[]{:S(2)}, u32[]{:S(2)}) %collective-permute-start.15) | collective-permute-done | bytes 524320 | tf_op jit(solution)/shard_map/ppermute | solution.py:176
  99.2 0.8 constant_dynamic-update-slice_fusion.6
  100.0 0.8 constant_dynamic-update-slice_fusion.5.mine_ref
  100.9 7.4 %collective-permute-start.17 = (bf16[1024,2048]{1,0:T(8,128)(2,1)}, bf16[1024,2048]{1,0:T(8,128)(2,1)}, u32[]{:S(2)}, u32[]{:S(2)}) collective-permute-start(bf16[1024,2048]{1,0:T(8,128)(2,1)} %constant_dynamic-update-slice_fusion.5.mine_ref), channel_id=1, source_target_pairs={{0,4},{4,0},{8,12},{12,8},{16,20},{20,16},{24,28},{28,24},{32,36},... | collective-permute-start | bytes 12582920 | tf_op jit(solution)/shard_map/ppermute | solution.py:198
  108.3 1.4 copy.14.place_ref
  109.7 5.7 %collective-permute-done.17.partner_ref = bf16[1024,2048]{1,0:T(8,128)(2,1)} collective-permute-done((bf16[1024,2048]{1,0:T(8,128)(2,1)}, bf16[1024,2048]{1,0:T(8,128)(2,1)}, u32[]{:S(2)}, u32[]{:S(2)}) %collective-permute-start.17) | collective-permute-done | bytes 4194336 | tf_op jit(solution)/shard_map/ppermute | solution.py:198
  115.4 94.5 %shard_map.91 = f32[512,2048]{1,0:T(8,128)} custom-call(s32[2048,1]{1,0:T(8,128)} %copy.14.place_ref, bf16[1024,2048]{1,0:T(8,128)(2,1)} %constant_dynamic-update-slice_fusion.5.mine_ref, bf16[1024,2048]{1,0:T(8,128)(2,1)} %collective-permute-done.17.partner_ref, bf16[2048,2048]{1,0:T(8,128)(2,1)} %fusion.1.t_ref), custom_call_target="tpu_custom_call" | custom-call | flops 34359738368 | bytes 29360128 | tf_op jit(solution)/shard_map/pallas_call | solution.py:134
  209.9 4.7 %copy.35 = f32[512,2048]{1,0:T(8,128)} copy(f32[512,2048]{1,0:T(8,128)} %shard_map.91) | data formatting | bytes 8388608
  (39 shorter events, 0.5 us)
Async XLA Ops:
  0.0 14.0 %copy-start = (bf16[1024,128]{1,0:T(8,128)(2,1)S(1)}, bf16[1024,128]{1,0:T(8,128)(2,1)}, u32[]{:S(2)}) copy-start(bf16[1024,128]{1,0:T(8,128)(2,1)} %param.12) | copy-start | bytes 786436
  0.0 9.7 %copy-start.2 = (bf16[1024,128]{1,0:T(8,128)(2,1)S(1)}, bf16[1024,128]{1,0:T(8,128)(2,1)}, u32[]{:S(2)}) copy-start(bf16[1024,128]{1,0:T(8,128)(2,1)} %param.11) | copy-start | bytes 786436
  5.1 8.1 %copy-start.3 = (bf16[128,64]{0,1:T(8,128)(2,1)S(1)}, bf16[128,64]{0,1:T(8,128)(2,1)}, u32[]{:S(2)}) copy-start(bf16[128,64]{0,1:T(8,128)(2,1)} %param.13) | copy-start | bytes 49156
  5.2 22.9 %collective-permute-start.5 = (f32[2048]{0:T(1024)S(1)}, f32[2048]{0:T(1024)S(1)}, u32[]{:S(2)}, u32[]{:S(2)}) collective-permute-start(f32[2048]{0:T(1024)S(1)} %fusion), channel_id=1, source_target_pairs={{0,3},{1,0},{2,1},{3,2},{4,7},{5,4},{6,5},{7,6},{8,11},{9,8},{10,9... | collective-permute-start | bytes 24584 | tf_op jit(solution)/shard_map/ppermute | solution.py:36
  8.5 20.3 %collective-permute-start.4 = (f32[2048]{0:T(1024)S(1)}, f32[2048]{0:T(1024)S(1)}, u32[]{:S(2)}, u32[]{:S(2)}) collective-permute-start(f32[2048]{0:T(1024)S(1)} %fusion), channel_id=1, source_target_pairs={{0,2},{1,3},{2,0},{3,1},{4,6},{5,7},{6,4},{7,5},{8,10},{9,11},{10,... | collective-permute-start | bytes 24584 | tf_op jit(solution)/shard_map/ppermute | solution.py:36
  9.1 19.8 %collective-permute-start.3 = (f32[2048]{0:T(1024)S(1)}, f32[2048]{0:T(1024)S(1)}, u32[]{:S(2)}, u32[]{:S(2)}) collective-permute-start(f32[2048]{0:T(1024)S(1)} %fusion), channel_id=1, source_target_pairs={{0,1},{1,2},{2,3},{3,0},{4,5},{5,6},{6,7},{7,4},{8,9},{9,10},{10,1... | collective-permute-start | bytes 24584 | tf_op jit(solution)/shard_map/ppermute | solution.py:36
  9.7 4.4 %copy-start.1 = (bf16[2048,1024]{1,0:T(8,128)(2,1)S(1)}, bf16[2048,1024]{1,0:T(8,128)(2,1)}, u32[]{:S(2)}) copy-start(bf16[2048,1024]{1,0:T(8,128)(2,1)} %param.9) | copy-start | bytes 12582916
  14.0 5.9 %copy-start.5 = (s32[64]{0:T(128)S(1)}, s32[64]{0:T(128)}, u32[]{:S(2)}) copy-start(s32[64]{0:T(128)} %param.14) | copy-start | bytes 772
  14.1 6.0 %copy-start.4 = (s32[2048]{0:T(1024)S(1)}, s32[2048]{0:T(1024)}, u32[]{:S(2)}) copy-start(s32[2048]{0:T(1024)} %param.15) | copy-start | bytes 24580
  16.7 20.3 %collective-permute-start = (bf16[2048,144]{0,1:T(8,128)(2,1)}, bf16[2048,144]{0,1:T(8,128)(2,1)}, u32[]{:S(2)}, u32[]{:S(2)}) collective-permute-start(bf16[2048,144]{0,1:T(8,128)(2,1)} %get-tuple-element.13), channel_id=1, source_target_pairs={{0,1},{1,2},{2,3},{3,0},{4,5},{5,6},{6,7},{7,4},{8,9},{9,10},{10,1... | collective-permute-start | bytes 1769480 | tf_op jit(solution)/shard_map/ppermute | solution.py:36
  18.2 26.5 %collective-permute-start.1 = (bf16[2048,144]{0,1:T(8,128)(2,1)S(1)}, bf16[2048,144]{0,1:T(8,128)(2,1)}, u32[]{:S(2)}, u32[]{:S(2)}) collective-permute-start(bf16[2048,144]{0,1:T(8,128)(2,1)S(1)} %get-tuple-element.14), channel_id=1, source_target_pairs={{0,2},{1,3},{2,0},{3,1},{4,6},{5,7},{6,4},{7,5},{8,10},{9,11},{10,... | collective-permute-start | bytes 1769480 | tf_op jit(solution)/shard_map/ppermute | solution.py:36
  28.1 16.7 %collective-permute-start.2 = (bf16[2048,144]{0,1:T(8,128)(2,1)S(1)}, bf16[2048,144]{0,1:T(8,128)(2,1)S(1)}, u32[]{:S(2)}, u32[]{:S(2)}) collective-permute-start(bf16[2048,144]{0,1:T(8,128)(2,1)S(1)} %get-tuple-element.15), channel_id=1, source_target_pairs={{0,3},{1,0},{2,1},{3,2},{4,7},{5,4},{6,5},{7,6},{8,11},{9,8},{10,9... | collective-permute-start | bytes 1769480 | tf_op jit(solution)/shard_map/ppermute | solution.py:36
  48.8 4.7 %collective-permute-start.8 = (f32[64]{0:T(128)S(1)}, f32[64]{0:T(128)S(1)}, u32[]{:S(2)}, u32[]{:S(2)}) collective-permute-start(f32[64]{0:T(128)S(1)} %get-tuple-element.29), channel_id=1, source_target_pairs={{0,3},{1,0},{2,1},{3,2},{4,7},{5,4},{6,5},{7,6},{8,11},{9,8},{10,9... | collective-permute-start | bytes 776 | tf_op jit(solution)/shard_map/ppermute | solution.py:36
  52.4 3.9 %collective-permute-start.7 = (f32[64]{0:T(128)S(1)}, f32[64]{0:T(128)S(1)}, u32[]{:S(2)}, u32[]{:S(2)}) collective-permute-start(f32[64]{0:T(128)S(1)} %get-tuple-element.29), channel_id=1, source_target_pairs={{0,2},{1,3},{2,0},{3,1},{4,6},{5,7},{6,4},{7,5},{8,10},{9,11},{10,... | collective-permute-start | bytes 776 | tf_op jit(solution)/shard_map/ppermute | solution.py:36
  53.4 3.6 %collective-permute-start.6 = (f32[64]{0:T(128)S(1)}, f32[64]{0:T(128)S(1)}, u32[]{:S(2)}, u32[]{:S(2)}) collective-permute-start(f32[64]{0:T(128)S(1)} %get-tuple-element.29), channel_id=1, source_target_pairs={{0,1},{1,2},{2,3},{3,0},{4,5},{5,6},{6,7},{7,4},{8,9},{9,10},{10,1... | collective-permute-start | bytes 776 | tf_op jit(solution)/shard_map/ppermute | solution.py:36
  57.2 6.1 %collective-permute-start.10 = (bf16[64,2048]{1,0:T(8,128)(2,1)S(1)}, bf16[64,2048]{1,0:T(8,128)(2,1)S(1)}, u32[]{:S(2)}, u32[]{:S(2)}) collective-permute-start(bf16[64,2048]{1,0:T(8,128)(2,1)S(1)} %get-tuple-element.12), channel_id=1, source_target_pairs={{0,24},{4,100},{8,0},{12,108},{16,8},{20,116},{24,16},{28,124},{32... | collective-permute-start | bytes 786440 | tf_op jit(solution)/shard_map/ppermute | solution.py:176
  60.0 6.5 %collective-permute-start.9 = (bf16[64,2048]{1,0:T(8,128)(2,1)S(1)}, bf16[64,2048]{1,0:T(8,128)(2,1)S(1)}, u32[]{:S(2)}, u32[]{:S(2)}) collective-permute-start(bf16[64,2048]{1,0:T(8,128)(2,1)S(1)} %get-tuple-element.12), channel_id=1, source_target_pairs={{0,8},{4,36},{8,16},{12,44},{16,24},{20,52},{24,0},{28,60},{32,40}... | collective-permute-start | bytes 786440 | tf_op jit(solution)/shard_map/ppermute | solution.py:176
  63.4 9.0 %collective-permute-start.12 = (bf16[32,2048]{1,0:T(8,128)(2,1)S(1)}, bf16[32,2048]{1,0:T(8,128)(2,1)S(1)}, u32[]{:S(2)}, u32[]{:S(2)}) collective-permute-start(bf16[32,2048]{1,0:T(8,128)(2,1)S(1)} %slice.35), channel_id=1, source_target_pairs={{0,24},{4,100},{8,0},{12,108},{16,8},{20,116},{24,16},{28,124},{32... | collective-permute-start | bytes 393224 | tf_op jit(solution)/shard_map/ppermute | solution.py:176
  66.6 5.1 %collective-permute-start.11 = (bf16[32,2048]{1,0:T(8,128)(2,1)S(1)}, bf16[32,2048]{1,0:T(8,128)(2,1)S(1)}, u32[]{:S(2)}, u32[]{:S(2)}) collective-permute-start(bf16[32,2048]{1,0:T(8,128)(2,1)S(1)} %slice.34), channel_id=1, source_target_pairs={{0,8},{4,36},{8,16},{12,44},{16,24},{20,52},{24,0},{28,60},{32,40}... | collective-permute-start | bytes 393224 | tf_op jit(solution)/shard_map/ppermute | solution.py:176
  73.0 16.8 %collective-permute-start.13 = (bf16[256,2048]{1,0:T(8,128)(2,1)S(1)}, bf16[256,2048]{1,0:T(8,128)(2,1)S(1)}, u32[]{:S(2)}, u32[]{:S(2)}) collective-permute-start(bf16[256,2048]{1,0:T(8,128)(2,1)S(1)} %get-tuple-element.23), channel_id=1, source_target_pairs={{0,32},{4,12},{8,40},{12,20},{16,48},{20,28},{24,56},{28,4},{32,64... | collective-permute-start | bytes 3145736 | tf_op jit(solution)/shard_map/ppermute | solution.py:176
  74.7 15.3 %collective-permute-start.14 = (bf16[256,2048]{1,0:T(8,128)(2,1)S(1)}, bf16[256,2048]{1,0:T(8,128)(2,1)S(1)}, u32[]{:S(2)}, u32[]{:S(2)}) collective-permute-start(bf16[256,2048]{1,0:T(8,128)(2,1)S(1)} %get-tuple-element.23), channel_id=1, source_target_pairs={{0,96},{4,28},{8,104},{12,4},{16,112},{20,12},{24,120},{28,20},{32... | collective-permute-start | bytes 3145736 | tf_op jit(solution)/shard_map/ppermute | solution.py:176
  89.9 9.3 %collective-permute-start.15 = (bf16[128,2048]{1,0:T(8,128)(2,1)S(1)}, bf16[128,2048]{1,0:T(8,128)(2,1)S(1)}, u32[]{:S(2)}, u32[]{:S(2)}) collective-permute-start(bf16[128,2048]{1,0:T(8,128)(2,1)S(1)} %slice.36), channel_id=1, source_target_pairs={{0,32},{4,12},{8,40},{12,20},{16,48},{20,28},{24,56},{28,4},{32,64... | collective-permute-start | bytes 1572872 | tf_op jit(solution)/shard_map/ppermute | solution.py:176
  90.0 10.0 %collective-permute-start.16 = (bf16[128,2048]{1,0:T(8,128)(2,1)S(1)}, bf16[128,2048]{1,0:T(8,128)(2,1)S(1)}, u32[]{:S(2)}, u32[]{:S(2)}) collective-permute-start(bf16[128,2048]{1,0:T(8,128)(2,1)S(1)} %slice.37), channel_id=1, source_target_pairs={{0,96},{4,28},{8,104},{12,4},{16,112},{20,12},{24,120},{28,20},{32... | collective-permute-start | bytes 1572872 | tf_op jit(solution)/shard_map/ppermute | solution.py:176
  100.9 14.5 %collective-permute-start.17 = (bf16[1024,2048]{1,0:T(8,128)(2,1)}, bf16[1024,2048]{1,0:T(8,128)(2,1)}, u32[]{:S(2)}, u32[]{:S(2)}) collective-permute-start(bf16[1024,2048]{1,0:T(8,128)(2,1)} %constant_dynamic-update-slice_fusion.5.mine_ref), channel_id=1, source_target_pairs={{0,4},{4,0},{8,12},{12,8},{16,20},{20,16},{24,28},{28,24},{32,36},... | collective-permute-start | bytes 12582920 | tf_op jit(solution)/shard_map/ppermute | solution.py:198

commit v8 on v7

--- a/solution.py
+++ b/solution.py
@@ -11,7 +11,7 @@
 MESH = pl.DeviceIdType.MESH
 
 epsilon = 1e-06
-TILE = 256
+TILE = 128
 
 
 def program_features(out_side, in_side, lengths, length):
@@ -51,78 +51,76 @@
         pl.semaphore_signal(barrier, inc=1, device_id={"narrow": neighbour}, device_id_type=MESH)
     pl.semaphore_wait(barrier, 2)
 
-    def order_block(block):
-        def body(i, carry):
-            start = pl.multiple_of(block * rows + i * TILE, TILE)
-            wanted = place_ref[pl.ds(start, TILE), :]
-            columns = lax.broadcasted_iota(jnp.int32, (TILE, held), 1)
-            pick_mine = (wanted == columns).astype(jnp.bfloat16)
-            pick_partner = (wanted == columns + held).astype(jnp.bfloat16)
-            picked = jnp.dot(pick_mine, mine_ref[...], preferred_element_type=jnp.float32)
-            picked = picked + jnp.dot(
-                pick_partner, partner_ref[...], preferred_element_type=jnp.float32
-            )
-            ordered[pl.ds(start, TILE), :] = picked.astype(jnp.bfloat16)
-            return carry
-
-        lax.fori_loop(0, tiles, body, 0)
-
-    def partial_block(block, direction):
+    def order_rows(start):
+        wanted = place_ref[pl.ds(start, TILE), :]
+        columns = lax.broadcasted_iota(jnp.int32, (TILE, held), 1)
+        pick_mine = (wanted == columns).astype(jnp.bfloat16)
+        pick_partner = (wanted == columns + held).astype(jnp.bfloat16)
+        picked = jnp.dot(pick_mine, mine_ref[...], preferred_element_type=jnp.float32)
+        picked = picked + jnp.dot(pick_partner, partner_ref[...], preferred_element_type=jnp.float32)
+        ordered[pl.ds(start, TILE), :] = picked.astype(jnp.bfloat16)
+
+    def partial_rows(start, direction, part):
         targets = t_ref[direction * half:(direction + 1) * half, :]
-
-        def body(i, carry):
-            start = pl.multiple_of(block * rows + i * TILE, TILE)
-            lhs = ordered[pl.ds(start, TILE), :]
-            acc[direction, pl.ds(pl.multiple_of(i * TILE, TILE), TILE), :] = lax.dot_general(
-                lhs, targets, (((1,), (1,)), ((), ())), preferred_element_type=jnp.float32
-            )
-            return carry
-
-        lax.fori_loop(0, tiles, body, 0)
-
-    def copy_of(direction, step):
+        acc[direction, part] = lax.dot_general(
+            ordered[pl.ds(start, TILE), :], targets, (((1,), (1,)), ((), ())),
+            preferred_element_type=jnp.float32,
+        )
+
+    def copy_of(direction, step, part):
         return pltpu.make_async_remote_copy(
-            src_ref=send_buf.at[direction, step],
-            dst_ref=recv_buf.at[direction, step],
-            send_sem=send_sem.at[direction, step],
-            recv_sem=recv_sem.at[direction, step],
+            src_ref=send_buf.at[direction, step, part],
+            dst_ref=recv_buf.at[direction, step, part],
+            send_sem=send_sem.at[direction, step, part],
+            recv_sem=recv_sem.at[direction, step, part],
             device_id={"narrow": right if direction == 0 else left},
             device_id_type=MESH,
         )
 
     built = set()
-
-    def need(offset):
-        if offset not in built:
-            built.add(offset)
-            order_block(lax.rem(me + offset, count))
-
     for step in range(count - 1):
         offsets = ((2 * count - 1 - step) % count, (1 + step) % count)
+        fresh = [offset not in built for offset in offsets]
+        built.update(offsets)
+
+        def body(part, carry, step=step, offsets=offsets, fresh=fresh):
+            for direction in range(2):
+                start = pl.multiple_of(lax.rem(me + offsets[direction], count) * rows + part * TILE, TILE)
+                if fresh[direction] and not (direction == 1 and offsets[1] == offsets[0]):
+                    order_rows(start)
+                partial_rows(start, direction, part)
+                if step == 0:
+                    send_buf[direction, step, part] = acc[direction, part].astype(jnp.bfloat16)
+                else:
+                    copy_of(direction, step - 1, part).wait_recv()
+                    send_buf[direction, step, part] = (
+                        acc[direction, part] + recv_buf[direction, step - 1, part].astype(jnp.float32)
+                    ).astype(jnp.bfloat16)
+                copy_of(direction, step, part).start()
+            return carry
+
+        lax.fori_loop(0, tiles, body, 0)
+
+    def last(part, carry):
+        start = pl.multiple_of(me * rows + part * TILE, TILE)
+        order_rows(start)
         for direction in range(2):
-            need(offsets[direction])
-        for direction in range(2):
-            partial_block(lax.rem(me + offsets[direction], count), direction)
-        for direction in range(2):
-            if step == 0:
-                send_buf[direction, step] = acc[direction].astype(jnp.bfloat16)
-            else:
-                copy_of(direction, step - 1).wait_recv()
-                send_buf[direction, step] = (
-                    acc[direction] + recv_buf[direction, step - 1].astype(jnp.float32)
-                ).astype(jnp.bfloat16)
-            copy_of(direction, step).start()
-    need(0)
-    for direction in range(2):
-        partial_block(me, direction)
-    for direction in range(2):
-        copy_of(direction, count - 2).wait_recv()
-        out_ref[:, direction * half:(direction + 1) * half] = (
-            acc[direction] + recv_buf[direction, count - 2].astype(jnp.float32)
-        ) * root
-    for step in range(count - 1):
-        for direction in range(2):
-            copy_of(direction, step).wait_send()
+            partial_rows(start, direction, part)
+            copy_of(direction, count - 2, part).wait_recv()
+            out_ref[pl.ds(start - me * rows, TILE), direction * half:(direction + 1) * half] = (
+                acc[direction, part] + recv_buf[direction, count - 2, part].astype(jnp.float32)
+            ) * root
+        return carry
+
+    lax.fori_loop(0, tiles, last, 0)
+
+    def drain(part, carry):
+        for step in range(count - 1):
+            for direction in range(2):
+                copy_of(direction, step, part).wait_send()
+        return carry
+
+    lax.fori_loop(0, tiles, drain, 0)
 
 
 def ring_scores(place, mine, partner, target_unit, count, root):
@@ -138,11 +136,11 @@
         out_specs=pl.BlockSpec(memory_space=pltpu.VMEM),
         scratch_shapes=[
             pltpu.VMEM((programs, depth), jnp.bfloat16),
-            pltpu.VMEM((2, count - 1, rows, half), jnp.bfloat16),
-            pltpu.VMEM((2, count - 1, rows, half), jnp.bfloat16),
-            pltpu.VMEM((2, rows, half), jnp.float32),
-            pltpu.SemaphoreType.DMA((2, count - 1)),
-            pltpu.SemaphoreType.DMA((2, count - 1)),
+            pltpu.VMEM((2, count - 1, rows // TILE, TILE, half), jnp.bfloat16),
+            pltpu.VMEM((2, count - 1, rows // TILE, TILE, half), jnp.bfloat16),
+            pltpu.VMEM((2, rows // TILE, TILE, half), jnp.float32),
+            pltpu.SemaphoreType.DMA((2, count - 1, rows // TILE)),
+            pltpu.SemaphoreType.DMA((2, count - 1, rows // TILE)),
         ],
         compiler_params=pltpu.CompilerParams(
             collective_id=0, has_side_effects=True, vmem_limit_bytes=62 * 1024 * 1024

time: 216 us -> 204 us (0.944)
  Pallas kernels: 94.5 us -> 83.7 us
    pallas_call x1, Pallas kernels: 94.5 us -> 83.7 us  [ring_scores(): pl.pallas_call(functools.partial(ring_kernel, count, root), out_shape=jax...]
  transfers between devices with their start and end apart: 18 -> 18, of which waited for: 9 -> 9; matrix products, arithmetic and copies ran while one was open for 14% -> 15% of each run, Pallas kernels for 0% -> 0%
where the time goes in v8:
time: 204 us
  Pallas kernels  83.7 us (41%)
  waiting for transfers between devices  40.1 us (20%)
  starting transfers between devices  33.8 us (17%)
  local copies, waits for them, and re-layouts  22.2 us (11%)
  other arithmetic  16.2 us (8%)
  matrix products  7.6 us (4%)
    pallas_call x1, Pallas kernels, ring_scores(): pl.pallas_call(functools.partial(ring_kernel, count, root), out_shape=jax...  83.7 us
    ppermute x8, waiting for transfers between devices, wide_shift(): return lax.ppermute(x, 'wide', perm)  23 us
    ppermute x8, starting transfers between devices, wide_shift(): return lax.ppermute(x, 'wide', perm)  13.2 us
    ppermute x9, starting transfers between devices, narrow_sum(): total = total + lax.ppermute(piece, 'narrow', perm).astype(jnp.float32)  13.2 us
    ppermute x9, waiting for transfers between devices, narrow_sum(): total = total + lax.ppermute(piece, 'narrow', perm).astype(jnp.float32)  11.5 us
    unnamed x20, local copies, waits for them, and re-layouts  10.5 us
    convert_element_type x1, other arithmetic, normalize_rows(): (features * lax.rsqrt(squares + epsilon)[:, None]).astype(jnp.bfloat16)  8.06 us
    scatter x1, local copies, waits for them, and re-layouts, shards(): jnp.zeros_like(program_output_index).at[program_output_index]  8.05 us
  transfers between devices with their start and end apart: 18, of which 9 were waited for; matrix products, arithmetic and copies ran while one was open for 15% of the time, Pallas kernels for 0%

profile of v8, /device:TPU:1, one launch (start us, length us, event | category | flops | bytes accessed | tf_op | source)
XLA Modules:
  0.0 203.8 jit_solution(5790096574685784564)
XLA Ops:
  0.0 5.1 %fusion = f32[2048]{0:T(1024)S(1)} fusion(bf16[2048,2048]{1,0:T(8,128)(2,1)} %param.16), kind=kLoop, calls=%fused_computation.3 | loop fusion | flops 12580864 | bytes 8396800 | tf_op jit(solution)/shard_map/reduce_sum | solution.py:226
  5.2 3.4 %collective-permute-start.5 = (f32[2048]{0:T(1024)S(1)}, f32[2048]{0:T(1024)S(1)}, u32[]{:S(2)}, u32[]{:S(2)}) collective-permute-start(f32[2048]{0:T(1024)S(1)} %fusion), channel_id=1, source_target_pairs={{0,3},{1,0},{2,1},{3,2},{4,7},{5,4},{6,5},{7,6},{8,11},{9,8},{10,9... | collective-permute-start | bytes 24584 | tf_op jit(solution)/shard_map/ppermute | solution.py:36
  8.5 0.5 collective-permute-start.4
  9.1 0.6 collective-permute-start.3
  9.7 3.6 %fusion.25 = f32[2048,128]{1,0:T(8,128)S(1)} fusion(bf16[2048,1024]{1,0:T(8,128)(2,1)} %param.10, bf16[1024,128]{1,0:T(8,128)(2,1)S(1)} %copy-done.2), kind=kOutput, calls=%fused_computation.84 | convolution fusion | flops 536870912 | bytes 5505024 | tf_op jit(solution)/shard_map/dot_general | solution.py:237
  13.3 0.7 fusion.26
  14.1 1.5 fusion.24
  15.6 1.0 pad_maximum_fusion
  16.7 1.5 collective-permute-start
  18.2 1.7 collective-permute-start.1
  20.0 8.0 %scatter_custom_fusion = s32[2048]{0:T(1024)S(1)} fusion(s32[2048]{0:T(1024)S(1)} %compare_select_fusion.2, s32[2048]{0:T(1024)S(1)} %iota.10, s32[]{:T(128)} %constant.126.clone.1), kind=kCustom, calls=%fused_computation.79 | custom fusion | bytes 8196 | tf_op jit(solution)/shard_map/scatter | solution.py:231
  28.1 0.7 collective-permute-start.2
  28.9 8.1 %fusion.1.t_ref = bf16[2048,2048]{1,0:T(8,128)(2,1)} fusion(bf16[2048,2048]{1,0:T(8,128)(2,1)} %param.16, f32[2048]{0:T(1024)S(1)} %add_rsqrt_fusion), kind=kLoop, calls=%fused_computation.4 | loop fusion | flops 12582912 | bytes 16785408 | tf_op jit(solution)/shard_map/convert_element_type | solution.py:28
  36.9 7.8 %collective-permute-done.1 = bf16[2048,144]{0,1:T(8,128)(2,1)} collective-permute-done((bf16[2048,144]{0,1:T(8,128)(2,1)S(1)}, bf16[2048,144]{0,1:T(8,128)(2,1)}, u32[]{:S(2)}, u32[]{:S(2)}) %collective-permute-start.1) | collective-permute-done | bytes 589856 | tf_op jit(solution)/shard_map/ppermute | solution.py:36
  44.7 0.1 collective-permute-done.2
  44.8 1.5 fusion.3
  46.4 0.1 slice.19
  46.5 0.3 copy.12
  46.8 0.2 reshape.35
  47.0 1.7 multiply_reduce_fusion
  48.8 3.6 %collective-permute-start.8 = (f32[64]{0:T(128)S(1)}, f32[64]{0:T(128)S(1)}, u32[]{:S(2)}, u32[]{:S(2)}) collective-permute-start(f32[64]{0:T(128)S(1)} %get-tuple-element.29), channel_id=1, source_target_pairs={{0,3},{1,0},{2,1},{3,2},{4,7},{5,4},{6,5},{7,6},{8,11},{9,8},{10,9... | collective-permute-start | bytes 776 | tf_op jit(solution)/shard_map/ppermute | solution.py:36
  52.4 1.0 collective-permute-start.7
  53.4 2.8 %collective-permute-done.7 = f32[64]{0:T(128)S(1)} collective-permute-done((f32[64]{0:T(128)S(1)}, f32[64]{0:T(128)S(1)}, u32[]{:S(2)}, u32[]{:S(2)}) %collective-permute-start.7) | collective-permute-done | bytes 288 | tf_op jit(solution)/shard_map/ppermute | solution.py:36
  56.3 0.7 collective-permute-done.6
  57.0 0.2 constant_dynamic-update-slice_fusion.4
  57.2 2.8 %collective-permute-start.10 = (bf16[64,2048]{1,0:T(8,128)(2,1)S(1)}, bf16[64,2048]{1,0:T(8,128)(2,1)S(1)}, u32[]{:S(2)}, u32[]{:S(2)}) collective-permute-start(bf16[64,2048]{1,0:T(8,128)(2,1)S(1)} %get-tuple-element.12), channel_id=1, source_target_pairs={{0,24},{4,100},{8,0},{12,108},{16,8},{20,116},{24,16},{28,124},{32... | collective-permute-start | bytes 786440 | tf_op jit(solution)/shard_map/ppermute | solution.py:174
  60.1 0.7 constant_dynamic-update-slice_fusion.13
  60.8 2.6 %collective-permute-done.10 = bf16[64,2048]{1,0:T(8,128)(2,1)S(1)} collective-permute-done((bf16[64,2048]{1,0:T(8,128)(2,1)S(1)}, bf16[64,2048]{1,0:T(8,128)(2,1)S(1)}, u32[]{:S(2)}, u32[]{:S(2)}) %collective-permute-start.10) | collective-permute-done | bytes 262176 | tf_op jit(solution)/shard_map/ppermute | solution.py:174
  63.4 3.2 %collective-permute-start.12 = (bf16[32,2048]{1,0:T(8,128)(2,1)S(1)}, bf16[32,2048]{1,0:T(8,128)(2,1)S(1)}, u32[]{:S(2)}, u32[]{:S(2)}) collective-permute-start(bf16[32,2048]{1,0:T(8,128)(2,1)S(1)} %slice.35), channel_id=1, source_target_pairs={{0,24},{4,100},{8,0},{12,108},{16,8},{20,116},{24,16},{28,124},{32... | collective-permute-start | bytes 393224 | tf_op jit(solution)/shard_map/ppermute | solution.py:174
  66.7 0.7 constant_dynamic-update-slice_fusion.3
  67.4 0.7 constant_dynamic-update-slice_fusion.2
  68.2 3.5 %collective-permute-done.11 = bf16[32,2048]{1,0:T(8,128)(2,1)S(1)} collective-permute-done((bf16[32,2048]{1,0:T(8,128)(2,1)S(1)}, bf16[32,2048]{1,0:T(8,128)(2,1)S(1)}, u32[]{:S(2)}, u32[]{:S(2)}) %collective-permute-start.11) | collective-permute-done | bytes 131104 | tf_op jit(solution)/shard_map/ppermute | solution.py:174
  71.7 0.7 constant_dynamic-update-slice_fusion.1
  72.4 0.7 constant_dynamic-update-slice_fusion
  73.0 1.6 collective-permute-start.13
  74.7 2.7 %collective-permute-start.14 = (bf16[256,2048]{1,0:T(8,128)(2,1)S(1)}, bf16[256,2048]{1,0:T(8,128)(2,1)S(1)}, u32[]{:S(2)}, u32[]{:S(2)}) collective-permute-start(bf16[256,2048]{1,0:T(8,128)(2,1)S(1)} %get-tuple-element.23), channel_id=1, source_target_pairs={{0,96},{4,28},{8,104},{12,4},{16,112},{20,12},{24,120},{28,20},{32... | collective-permute-start | bytes 3145736 | tf_op jit(solution)/shard_map/ppermute | solution.py:174
  77.4 12.5 %collective-permute-done.13 = bf16[256,2048]{1,0:T(8,128)(2,1)S(1)} collective-permute-done((bf16[256,2048]{1,0:T(8,128)(2,1)S(1)}, bf16[256,2048]{1,0:T(8,128)(2,1)S(1)}, u32[]{:S(2)}, u32[]{:S(2)}) %collective-permute-start.13) | collective-permute-done | bytes 1048608 | tf_op jit(solution)/shard_map/ppermute | solution.py:174
  90.0 2.7 %collective-permute-start.16 = (bf16[128,2048]{1,0:T(8,128)(2,1)S(1)}, bf16[128,2048]{1,0:T(8,128)(2,1)S(1)}, u32[]{:S(2)}, u32[]{:S(2)}) collective-permute-start(bf16[128,2048]{1,0:T(8,128)(2,1)S(1)} %slice.37), channel_id=1, source_target_pairs={{0,96},{4,28},{8,104},{12,4},{16,112},{20,12},{24,120},{28,20},{32... | collective-permute-start | bytes 1572872 | tf_op jit(solution)/shard_map/ppermute | solution.py:174
  92.8 1.0 constant_dynamic-update-slice_fusion.8
  93.8 1.0 constant_dynamic-update-slice_fusion.7
  94.8 4.4 %collective-permute-done.15 = bf16[128,2048]{1,0:T(8,128)(2,1)S(1)} collective-permute-done((bf16[128,2048]{1,0:T(8,128)(2,1)S(1)}, bf16[128,2048]{1,0:T(8,128)(2,1)S(1)}, u32[]{:S(2)}, u32[]{:S(2)}) %collective-permute-start.15) | collective-permute-done | bytes 524320 | tf_op jit(solution)/shard_map/ppermute | solution.py:174
  99.2 0.8 constant_dynamic-update-slice_fusion.6
  100.0 0.8 constant_dynamic-update-slice_fusion.5.mine_ref
  100.9 7.4 %collective-permute-start.17 = (bf16[1024,2048]{1,0:T(8,128)(2,1)}, bf16[1024,2048]{1,0:T(8,128)(2,1)}, u32[]{:S(2)}, u32[]{:S(2)}) collective-permute-start(bf16[1024,2048]{1,0:T(8,128)(2,1)} %constant_dynamic-update-slice_fusion.5.mine_ref), channel_id=1, source_target_pairs={{0,4},{4,0},{8,12},{12,8},{16,20},{20,16},{24,28},{28,24},{32,36},... | collective-permute-start | bytes 12582920 | tf_op jit(solution)/shard_map/ppermute | solution.py:196
  108.3 1.4 copy.14.place_ref
  109.7 5.7 %collective-permute-done.17.partner_ref = bf16[1024,2048]{1,0:T(8,128)(2,1)} collective-permute-done((bf16[1024,2048]{1,0:T(8,128)(2,1)}, bf16[1024,2048]{1,0:T(8,128)(2,1)}, u32[]{:S(2)}, u32[]{:S(2)}) %collective-permute-start.17) | collective-permute-done | bytes 4194336 | tf_op jit(solution)/shard_map/ppermute | solution.py:196
  115.4 83.7 %shard_map.91 = f32[512,2048]{1,0:T(8,128)} custom-call(s32[2048,1]{1,0:T(8,128)} %copy.14.place_ref, bf16[1024,2048]{1,0:T(8,128)(2,1)} %constant_dynamic-update-slice_fusion.5.mine_ref, bf16[1024,2048]{1,0:T(8,128)(2,1)} %collective-permute-done.17.partner_ref, bf16[2048,2048]{1,0:T(8,128)(2,1)} %fusion.1.t_ref), custom_call_target="tpu_custom_call" | custom-call | flops 34359738368 | bytes 29360128 | tf_op jit(solution)/shard_map/pallas_call | solution.py:132
  199.1 4.7 %copy.35 = f32[512,2048]{1,0:T(8,128)} copy(f32[512,2048]{1,0:T(8,128)} %shard_map.91) | data formatting | bytes 8388608
  (39 shorter events, 0.5 us)
Async XLA Ops:
  0.0 14.0 %copy-start = (bf16[1024,128]{1,0:T(8,128)(2,1)S(1)}, bf16[1024,128]{1,0:T(8,128)(2,1)}, u32[]{:S(2)}) copy-start(bf16[1024,128]{1,0:T(8,128)(2,1)} %param.12) | copy-start | bytes 786436
  0.0 9.7 %copy-start.2 = (bf16[1024,128]{1,0:T(8,128)(2,1)S(1)}, bf16[1024,128]{1,0:T(8,128)(2,1)}, u32[]{:S(2)}) copy-start(bf16[1024,128]{1,0:T(8,128)(2,1)} %param.11) | copy-start | bytes 786436
  5.1 8.1 %copy-start.3 = (bf16[128,64]{0,1:T(8,128)(2,1)S(1)}, bf16[128,64]{0,1:T(8,128)(2,1)}, u32[]{:S(2)}) copy-start(bf16[128,64]{0,1:T(8,128)(2,1)} %param.13) | copy-start | bytes 49156
  5.2 22.9 %collective-permute-start.5 = (f32[2048]{0:T(1024)S(1)}, f32[2048]{0:T(1024)S(1)}, u32[]{:S(2)}, u32[]{:S(2)}) collective-permute-start(f32[2048]{0:T(1024)S(1)} %fusion), channel_id=1, source_target_pairs={{0,3},{1,0},{2,1},{3,2},{4,7},{5,4},{6,5},{7,6},{8,11},{9,8},{10,9... | collective-permute-start | bytes 24584 | tf_op jit(solution)/shard_map/ppermute | solution.py:36
  8.5 20.3 %collective-permute-start.4 = (f32[2048]{0:T(1024)S(1)}, f32[2048]{0:T(1024)S(1)}, u32[]{:S(2)}, u32[]{:S(2)}) collective-permute-start(f32[2048]{0:T(1024)S(1)} %fusion), channel_id=1, source_target_pairs={{0,2},{1,3},{2,0},{3,1},{4,6},{5,7},{6,4},{7,5},{8,10},{9,11},{10,... | collective-permute-start | bytes 24584 | tf_op jit(solution)/shard_map/ppermute | solution.py:36
  9.1 19.8 %collective-permute-start.3 = (f32[2048]{0:T(1024)S(1)}, f32[2048]{0:T(1024)S(1)}, u32[]{:S(2)}, u32[]{:S(2)}) collective-permute-start(f32[2048]{0:T(1024)S(1)} %fusion), channel_id=1, source_target_pairs={{0,1},{1,2},{2,3},{3,0},{4,5},{5,6},{6,7},{7,4},{8,9},{9,10},{10,1... | collective-permute-start | bytes 24584 | tf_op jit(solution)/shard_map/ppermute | solution.py:36
  9.7 4.4 %copy-start.1 = (bf16[2048,1024]{1,0:T(8,128)(2,1)S(1)}, bf16[2048,1024]{1,0:T(8,128)(2,1)}, u32[]{:S(2)}) copy-start(bf16[2048,1024]{1,0:T(8,128)(2,1)} %param.9) | copy-start | bytes 12582916
  14.0 5.9 %copy-start.5 = (s32[64]{0:T(128)S(1)}, s32[64]{0:T(128)}, u32[]{:S(2)}) copy-start(s32[64]{0:T(128)} %param.14) | copy-start | bytes 772
  14.1 6.0 %copy-start.4 = (s32[2048]{0:T(1024)S(1)}, s32[2048]{0:T(1024)}, u32[]{:S(2)}) copy-start(s32[2048]{0:T(1024)} %param.15) | copy-start | bytes 24580
  16.7 20.3 %collective-permute-start = (bf16[2048,144]{0,1:T(8,128)(2,1)}, bf16[2048,144]{0,1:T(8,128)(2,1)}, u32[]{:S(2)}, u32[]{:S(2)}) collective-permute-start(bf16[2048,144]{0,1:T(8,128)(2,1)} %get-tuple-element.13), channel_id=1, source_target_pairs={{0,1},{1,2},{2,3},{3,0},{4,5},{5,6},{6,7},{7,4},{8,9},{9,10},{10,1... | collective-permute-start | bytes 1769480 | tf_op jit(solution)/shard_map/ppermute | solution.py:36
  18.2 26.5 %collective-permute-start.1 = (bf16[2048,144]{0,1:T(8,128)(2,1)S(1)}, bf16[2048,144]{0,1:T(8,128)(2,1)}, u32[]{:S(2)}, u32[]{:S(2)}) collective-permute-start(bf16[2048,144]{0,1:T(8,128)(2,1)S(1)} %get-tuple-element.14), channel_id=1, source_target_pairs={{0,2},{1,3},{2,0},{3,1},{4,6},{5,7},{6,4},{7,5},{8,10},{9,11},{10,... | collective-permute-start | bytes 1769480 | tf_op jit(solution)/shard_map/ppermute | solution.py:36
  28.1 16.7 %collective-permute-start.2 = (bf16[2048,144]{0,1:T(8,128)(2,1)S(1)}, bf16[2048,144]{0,1:T(8,128)(2,1)S(1)}, u32[]{:S(2)}, u32[]{:S(2)}) collective-permute-start(bf16[2048,144]{0,1:T(8,128)(2,1)S(1)} %get-tuple-element.15), channel_id=1, source_target_pairs={{0,3},{1,0},{2,1},{3,2},{4,7},{5,4},{6,5},{7,6},{8,11},{9,8},{10,9... | collective-permute-start | bytes 1769480 | tf_op jit(solution)/shard_map/ppermute | solution.py:36
  48.8 4.7 %collective-permute-start.8 = (f32[64]{0:T(128)S(1)}, f32[64]{0:T(128)S(1)}, u32[]{:S(2)}, u32[]{:S(2)}) collective-permute-start(f32[64]{0:T(128)S(1)} %get-tuple-element.29), channel_id=1, source_target_pairs={{0,3},{1,0},{2,1},{3,2},{4,7},{5,4},{6,5},{7,6},{8,11},{9,8},{10,9... | collective-permute-start | bytes 776 | tf_op jit(solution)/shard_map/ppermute | solution.py:36
  52.4 3.9 %collective-permute-start.7 = (f32[64]{0:T(128)S(1)}, f32[64]{0:T(128)S(1)}, u32[]{:S(2)}, u32[]{:S(2)}) collective-permute-start(f32[64]{0:T(128)S(1)} %get-tuple-element.29), channel_id=1, source_target_pairs={{0,2},{1,3},{2,0},{3,1},{4,6},{5,7},{6,4},{7,5},{8,10},{9,11},{10,... | collective-permute-start | bytes 776 | tf_op jit(solution)/shard_map/ppermute | solution.py:36
  53.4 3.6 %collective-permute-start.6 = (f32[64]{0:T(128)S(1)}, f32[64]{0:T(128)S(1)}, u32[]{:S(2)}, u32[]{:S(2)}) collective-permute-start(f32[64]{0:T(128)S(1)} %get-tuple-element.29), channel_id=1, source_target_pairs={{0,1},{1,2},{2,3},{3,0},{4,5},{5,6},{6,7},{7,4},{8,9},{9,10},{10,1... | collective-permute-start | bytes 776 | tf_op jit(solution)/shard_map/ppermute | solution.py:36
  57.2 6.1 %collective-permute-start.10 = (bf16[64,2048]{1,0:T(8,128)(2,1)S(1)}, bf16[64,2048]{1,0:T(8,128)(2,1)S(1)}, u32[]{:S(2)}, u32[]{:S(2)}) collective-permute-start(bf16[64,2048]{1,0:T(8,128)(2,1)S(1)} %get-tuple-element.12), channel_id=1, source_target_pairs={{0,24},{4,100},{8,0},{12,108},{16,8},{20,116},{24,16},{28,124},{32... | collective-permute-start | bytes 786440 | tf_op jit(solution)/shard_map/ppermute | solution.py:174
  60.0 6.5 %collective-permute-start.9 = (bf16[64,2048]{1,0:T(8,128)(2,1)S(1)}, bf16[64,2048]{1,0:T(8,128)(2,1)S(1)}, u32[]{:S(2)}, u32[]{:S(2)}) collective-permute-start(bf16[64,2048]{1,0:T(8,128)(2,1)S(1)} %get-tuple-element.12), channel_id=1, source_target_pairs={{0,8},{4,36},{8,16},{12,44},{16,24},{20,52},{24,0},{28,60},{32,40}... | collective-permute-start | bytes 786440 | tf_op jit(solution)/shard_map/ppermute | solution.py:174
  63.4 9.0 %collective-permute-start.12 = (bf16[32,2048]{1,0:T(8,128)(2,1)S(1)}, bf16[32,2048]{1,0:T(8,128)(2,1)S(1)}, u32[]{:S(2)}, u32[]{:S(2)}) collective-permute-start(bf16[32,2048]{1,0:T(8,128)(2,1)S(1)} %slice.35), channel_id=1, source_target_pairs={{0,24},{4,100},{8,0},{12,108},{16,8},{20,116},{24,16},{28,124},{32... | collective-permute-start | bytes 393224 | tf_op jit(solution)/shard_map/ppermute | solution.py:174
  66.6 5.1 %collective-permute-start.11 = (bf16[32,2048]{1,0:T(8,128)(2,1)S(1)}, bf16[32,2048]{1,0:T(8,128)(2,1)S(1)}, u32[]{:S(2)}, u32[]{:S(2)}) collective-permute-start(bf16[32,2048]{1,0:T(8,128)(2,1)S(1)} %slice.34), channel_id=1, source_target_pairs={{0,8},{4,36},{8,16},{12,44},{16,24},{20,52},{24,0},{28,60},{32,40}... | collective-permute-start | bytes 393224 | tf_op jit(solution)/shard_map/ppermute | solution.py:174
  73.0 16.8 %collective-permute-start.13 = (bf16[256,2048]{1,0:T(8,128)(2,1)S(1)}, bf16[256,2048]{1,0:T(8,128)(2,1)S(1)}, u32[]{:S(2)}, u32[]{:S(2)}) collective-permute-start(bf16[256,2048]{1,0:T(8,128)(2,1)S(1)} %get-tuple-element.23), channel_id=1, source_target_pairs={{0,32},{4,12},{8,40},{12,20},{16,48},{20,28},{24,56},{28,4},{32,64... | collective-permute-start | bytes 3145736 | tf_op jit(solution)/shard_map/ppermute | solution.py:174
  74.7 15.3 %collective-permute-start.14 = (bf16[256,2048]{1,0:T(8,128)(2,1)S(1)}, bf16[256,2048]{1,0:T(8,128)(2,1)S(1)}, u32[]{:S(2)}, u32[]{:S(2)}) collective-permute-start(bf16[256,2048]{1,0:T(8,128)(2,1)S(1)} %get-tuple-element.23), channel_id=1, source_target_pairs={{0,96},{4,28},{8,104},{12,4},{16,112},{20,12},{24,120},{28,20},{32... | collective-permute-start | bytes 3145736 | tf_op jit(solution)/shard_map/ppermute | solution.py:174
  89.9 9.3 %collective-permute-start.15 = (bf16[128,2048]{1,0:T(8,128)(2,1)S(1)}, bf16[128,2048]{1,0:T(8,128)(2,1)S(1)}, u32[]{:S(2)}, u32[]{:S(2)}) collective-permute-start(bf16[128,2048]{1,0:T(8,128)(2,1)S(1)} %slice.36), channel_id=1, source_target_pairs={{0,32},{4,12},{8,40},{12,20},{16,48},{20,28},{24,56},{28,4},{32,64... | collective-permute-start | bytes 1572872 | tf_op jit(solution)/shard_map/ppermute | solution.py:174
  90.0 10.0 %collective-permute-start.16 = (bf16[128,2048]{1,0:T(8,128)(2,1)S(1)}, bf16[128,2048]{1,0:T(8,128)(2,1)S(1)}, u32[]{:S(2)}, u32[]{:S(2)}) collective-permute-start(bf16[128,2048]{1,0:T(8,128)(2,1)S(1)} %slice.37), channel_id=1, source_target_pairs={{0,96},{4,28},{8,104},{12,4},{16,112},{20,12},{24,120},{28,20},{32... | collective-permute-start | bytes 1572872 | tf_op jit(solution)/shard_map/ppermute | solution.py:174
  100.9 14.5 %collective-permute-start.17 = (bf16[1024,2048]{1,0:T(8,128)(2,1)}, bf16[1024,2048]{1,0:T(8,128)(2,1)}, u32[]{:S(2)}, u32[]{:S(2)}) collective-permute-start(bf16[1024,2048]{1,0:T(8,128)(2,1)} %constant_dynamic-update-slice_fusion.5.mine_ref), channel_id=1, source_target_pairs={{0,4},{4,0},{8,12},{12,8},{16,20},{20,16},{24,28},{28,24},{32,36},... | collective-permute-start | bytes 12582920 | tf_op jit(solution)/shard_map/ppermute | solution.py:196

commit v9 on v8

--- a/solution.py
+++ b/solution.py
@@ -37,7 +37,7 @@
     return total
 
 
-def ring_kernel(count, root, place_ref, mine_ref, partner_ref, t_ref, out_ref,
+def ring_kernel(count, root, place_ref, scale_ref, mine_ref, partner_ref, t_ref, out_ref,
                 ordered, send_buf, recv_buf, acc, send_sem, recv_sem):
     me = lax.axis_index("narrow")
     right, left = lax.rem(me + 1, count), lax.rem(me + count - 1, count)
@@ -58,7 +58,9 @@
         pick_partner = (wanted == columns + held).astype(jnp.bfloat16)
         picked = jnp.dot(pick_mine, mine_ref[...], preferred_element_type=jnp.float32)
         picked = picked + jnp.dot(pick_partner, partner_ref[...], preferred_element_type=jnp.float32)
-        ordered[pl.ds(start, TILE), :] = picked.astype(jnp.bfloat16)
+        ordered[pl.ds(start, TILE), :] = (picked * scale_ref[pl.ds(start, TILE), :]).astype(
+            jnp.bfloat16
+        )
 
     def partial_rows(start, direction, part):
         targets = t_ref[direction * half:(direction + 1) * half, :]
@@ -123,7 +125,7 @@
     lax.fori_loop(0, tiles, drain, 0)
 
 
-def ring_scores(place, mine, partner, target_unit, count, root):
+def ring_scores(place, scale, mine, partner, target_unit, count, root):
     programs = place.shape[0]
     depth = mine.shape[1]
     rows = programs // count
@@ -132,7 +134,7 @@
     return pl.pallas_call(
         functools.partial(ring_kernel, count, root),
         out_shape=jax.ShapeDtypeStruct((rows, targets), jnp.float32),
-        in_specs=[pl.BlockSpec(memory_space=pltpu.VMEM)] * 4,
+        in_specs=[pl.BlockSpec(memory_space=pltpu.VMEM)] * 5,
         out_specs=pl.BlockSpec(memory_space=pltpu.VMEM),
         scratch_shapes=[
             pltpu.VMEM((programs, depth), jnp.bfloat16),
@@ -150,7 +152,7 @@
             bytes_accessed=2 * (2 * programs + targets) * depth + 4 * rows * targets,
             transcendentals=0,
         ),
-    )(place.reshape(programs, 1), mine, partner, target_unit)
+    )(place.reshape(programs, 1), scale.reshape(programs, 1), mine, partner, target_unit)
 
 
 RING = 4
@@ -188,14 +190,16 @@
     return jnp.concatenate([block, from_left, from_right, far], axis=0)
 
 
-def wide_gather(unit_rows, row_order):
+def wide_gather(unit_rows):
     first = ("z", "y")
     second = ("y", "z")
     bundle = ring_gather(unit_rows, first)
     mine = ring_gather(bundle, second)
     partner = lax.ppermute(mine, "wide", [(w, w ^ 1) for w in range(2 * RING * RING)])
-
-    local = unit_rows.shape[0]
+    return mine, partner
+
+
+def gathered_place(row_order, local):
     y, z, c = wide_coords(lax.axis_index("wide"))
     slot = jnp.asarray(SLOT, jnp.int32)
     owner = row_order // local
@@ -204,7 +208,7 @@
     first_offset = jnp.where(oc == 0, dz, dy)
     second_offset = jnp.where(oc == 0, dy, dz)
     block = (oc != c) * (RING * RING) + slot[second_offset] * RING + slot[first_offset]
-    return mine, partner, block * local + row_order % local
+    return block * local + row_order % local
 
 
 def shards(
@@ -254,12 +258,15 @@
     quarter = summed_parts[:, :quarter_cols]
     in_all = summed_parts[:, quarter_cols:]
     features = program_features(quarter, in_all, lengths, length)
+    mine, partner = wide_gather(features.astype(jnp.bfloat16))
     squares = jnp.sum(features * features, axis=1)
     squares = narrow_sum(squares, lambda dest: squares, narrow_count, narrow_index, jnp.float32)
-    unit_rows = normalize_rows(features, squares)
+    scale = lax.rsqrt(squares + epsilon)[:, None]
+    scale_mine, scale_partner = wide_gather(scale)
+    place = gathered_place(row_order, features.shape[0])
+    scale = jnp.concatenate([scale_mine, scale_partner], axis=0)[place, 0]
     root_count = math.sqrt(float(targets.shape[1] * narrow_count))
-    mine, partner, place = wide_gather(unit_rows, row_order)
-    return ring_scores(place, mine, partner, target_unit, narrow_count, root_count)
+    return ring_scores(place, scale, mine, partner, target_unit, narrow_count, root_count)
 
 
 def solution(mesh):

time: 204 us -> 234 us (1.15)
  local copies, waits for them, and re-layouts: 22.2 us -> 36.4 us
  starting transfers between devices: 33.8 us -> 46.6 us
    gather x0 -> x1, local copies, waits for them, and re-layouts: none -> 12.4 us  [shards(): scale = jnp.concatenate([scale_mine, scale_partner], axis=0)[place, 0]]
    ppermute x8 -> x16, waiting for transfers between devices: 23 us -> 31.5 us  [wide_shift(): return lax.ppermute(x, 'wide', perm)]
    ppermute x8 -> x16, starting transfers between devices: 13.2 us -> 21.6 us  [wide_shift(): return lax.ppermute(x, 'wide', perm)]
    ppermute x1 -> x2, starting transfers between devices: 7.4 us -> 14.1 us  [wide_gather(): lax.ppermute(mine, 'wide', [(w, w ^ 1) for w in range(2 * RING * RING)])]
    ppermute x1 -> x2, waiting for transfers between devices: 5.7 us -> 0.01 us  [wide_gather(): lax.ppermute(mine, 'wide', [(w, w ^ 1) for w in range(2 * RING * RING)])]
    unnamed x20 -> x21, local copies, waits for them, and re-layouts: 10.5 us -> 10.7 us
  transfers between devices with their start and end apart: 18 -> 27, of which waited for: 9 -> 14; matrix products, arithmetic and copies ran while one was open for 15% -> 19% of each run, Pallas kernels for 0% -> 0%
where the time goes in v9:
time: 234 us; the launch traced here: 233 us
  Pallas kernels  84.2 us (36%)
  starting transfers between devices  46.6 us (20%)
  waiting for transfers between devices  42.3 us (18%)
  local copies, waits for them, and re-layouts  36.4 us (16%)
  other arithmetic  16 us (7%)
  matrix products  7.6 us (3%)
    pallas_call x1, Pallas kernels, ring_scores(): pl.pallas_call(functools.partial(ring_kernel, count, root), out_shape=jax...  84.2 us
    ppermute x16, waiting for transfers between devices, wide_shift(): return lax.ppermute(x, 'wide', perm)  31.5 us
    ppermute x16, starting transfers between devices, wide_shift(): return lax.ppermute(x, 'wide', perm)  21.6 us
    ppermute x2, starting transfers between devices, wide_gather(): lax.ppermute(mine, 'wide', [(w, w ^ 1) for w in range(2 * RING * RING)])  14.1 us
    gather x1, local copies, waits for them, and re-layouts, shards(): scale = jnp.concatenate([scale_mine, scale_partner], axis=0)[place, 0]  12.4 us
    ppermute x9, starting transfers between devices, narrow_sum(): total = total + lax.ppermute(piece, 'narrow', perm).astype(jnp.float32)  10.9 us
    ppermute x9, waiting for transfers between devices, narrow_sum(): total = total + lax.ppermute(piece, 'narrow', perm).astype(jnp.float32)  10.8 us
    unnamed x21, local copies, waits for them, and re-layouts  10.7 us
  transfers between devices with their start and end apart: 27, of which 14 were waited for; matrix products, arithmetic and copies ran while one was open for 19% of the time, Pallas kernels for 0%

profile of v9, /device:TPU:1, one launch (start us, length us, event | category | flops | bytes accessed | tf_op | source)
XLA Modules:
  0.0 233.3 jit_solution(4666292088959049275)
XLA Ops:
  0.0 5.1 %fusion = f32[2048]{0:T(1024)S(1)} fusion(bf16[2048,2048]{1,0:T(8,128)(2,1)} %param.16), kind=kLoop, calls=%fused_computation.4 | loop fusion | flops 12580864 | bytes 8396800 | tf_op jit(solution)/shard_map/reduce_sum | solution.py:230
  5.2 3.4 %collective-permute-start.5 = (f32[2048]{0:T(1024)S(1)}, f32[2048]{0:T(1024)S(1)}, u32[]{:S(2)}, u32[]{:S(2)}) collective-permute-start(f32[2048]{0:T(1024)S(1)} %fusion), channel_id=1, source_target_pairs={{0,3},{1,0},{2,1},{3,2},{4,7},{5,4},{6,5},{7,6},{8,11},{9,8},{10,9... | collective-permute-start | bytes 24584 | tf_op jit(solution)/shard_map/ppermute | solution.py:36
  9.7 3.6 %fusion.27 = f32[2048,128]{1,0:T(8,128)S(1)} fusion(bf16[2048,1024]{1,0:T(8,128)(2,1)} %param.10, bf16[1024,128]{1,0:T(8,128)(2,1)S(1)} %copy-done.2), kind=kOutput, calls=%fused_computation.88 | convolution fusion | flops 536870912 | bytes 5505024 | tf_op jit(solution)/shard_map/dot_general | solution.py:241
  13.3 0.7 fusion.28
  14.1 1.5 fusion.26
  15.6 1.0 pad_maximum_fusion
  16.7 1.5 collective-permute-start
  18.2 1.7 collective-permute-start.1
  20.0 8.0 %scatter_custom_fusion = s32[2048]{0:T(1024)S(1)} fusion(s32[2048]{0:T(1024)S(1)} %compare_select_fusion.3, s32[2048]{0:T(1024)S(1)} %iota.10, s32[]{:T(128)} %constant.127.clone.1), kind=kCustom, calls=%fused_computation.82 | custom fusion | bytes 8196 | tf_op jit(solution)/shard_map/scatter | solution.py:235
  28.1 0.7 collective-permute-start.2
  28.9 8.1 %fusion.1.t_ref = bf16[2048,2048]{1,0:T(8,128)(2,1)} fusion(bf16[2048,2048]{1,0:T(8,128)(2,1)} %param.16, f32[2048]{0:T(1024)S(1)} %add_rsqrt_fusion), kind=kLoop, calls=%fused_computation.5 | loop fusion | flops 12582912 | bytes 16785408 | tf_op jit(solution)/shard_map/convert_element_type | solution.py:28
  36.9 7.8 %collective-permute-done.1 = bf16[2048,144]{0,1:T(8,128)(2,1)} collective-permute-done((bf16[2048,144]{0,1:T(8,128)(2,1)S(1)}, bf16[2048,144]{0,1:T(8,128)(2,1)}, u32[]{:S(2)}, u32[]{:S(2)}) %collective-permute-start.1) | collective-permute-done | bytes 589856 | tf_op jit(solution)/shard_map/ppermute | solution.py:36
  44.8 1.5 fusion.3
  47.0 1.7 fusion.25
  48.8 3.0 %collective-permute-start.19 = (bf16[64,2048]{1,0:T(8,128)(2,1)S(1)}, bf16[64,2048]{1,0:T(8,128)(2,1)S(1)}, u32[]{:S(2)}, u32[]{:S(2)}) collective-permute-start(bf16[64,2048]{1,0:T(8,128)(2,1)S(1)} %bitcast.27), channel_id=1, source_target_pairs={{0,24},{4,100},{8,0},{12,108},{16,8},{20,116},{24,16},{28,124},{32... | collective-permute-start | bytes 786440 | tf_op jit(solution)/shard_map/ppermute | solution.py:176
  51.8 0.8 constant_dynamic-update-slice_fusion.4
  52.6 2.5 %collective-permute-done.19 = bf16[64,2048]{1,0:T(8,128)(2,1)S(1)} collective-permute-done((bf16[64,2048]{1,0:T(8,128)(2,1)S(1)}, bf16[64,2048]{1,0:T(8,128)(2,1)S(1)}, u32[]{:S(2)}, u32[]{:S(2)}) %collective-permute-start.19) | collective-permute-done | bytes 262176 | tf_op jit(solution)/shard_map/ppermute | solution.py:176
  55.1 3.2 %collective-permute-start.21 = (bf16[32,2048]{1,0:T(8,128)(2,1)S(1)}, bf16[32,2048]{1,0:T(8,128)(2,1)S(1)}, u32[]{:S(2)}, u32[]{:S(2)}) collective-permute-start(bf16[32,2048]{1,0:T(8,128)(2,1)S(1)} %slice.55), channel_id=1, source_target_pairs={{0,24},{4,100},{8,0},{12,108},{16,8},{20,116},{24,16},{28,124},{32... | collective-permute-start | bytes 393224 | tf_op jit(solution)/shard_map/ppermute | solution.py:176
  58.4 0.8 constant_dynamic-update-slice_fusion.3
  59.2 0.8 constant_dynamic-update-slice_fusion.2
  59.9 3.5 %collective-permute-done.20 = bf16[32,2048]{1,0:T(8,128)(2,1)S(1)} collective-permute-done((bf16[32,2048]{1,0:T(8,128)(2,1)S(1)}, bf16[32,2048]{1,0:T(8,128)(2,1)S(1)}, u32[]{:S(2)}, u32[]{:S(2)}) %collective-permute-start.20) | collective-permute-done | bytes 131104 | tf_op jit(solution)/shard_map/ppermute | solution.py:176
  64.8 1.6 collective-permute-start.22
  66.4 2.6 %collective-permute-start.23 = (bf16[256,2048]{1,0:T(8,128)(2,1)S(1)}, bf16[256,2048]{1,0:T(8,128)(2,1)S(1)}, u32[]{:S(2)}, u32[]{:S(2)}) collective-permute-start(bf16[256,2048]{1,0:T(8,128)(2,1)S(1)} %get-tuple-element.27), channel_id=1, source_target_pairs={{0,96},{4,28},{8,104},{12,4},{16,112},{20,12},{24,120},{28,20},{32... | collective-permute-start | bytes 3145736 | tf_op jit(solution)/shard_map/ppermute | solution.py:176
  69.1 12.5 %collective-permute-done.22 = bf16[256,2048]{1,0:T(8,128)(2,1)S(1)} collective-permute-done((bf16[256,2048]{1,0:T(8,128)(2,1)S(1)}, bf16[256,2048]{1,0:T(8,128)(2,1)S(1)}, u32[]{:S(2)}, u32[]{:S(2)}) %collective-permute-start.22) | collective-permute-done | bytes 1048608 | tf_op jit(solution)/shard_map/ppermute | solution.py:176
  81.7 2.7 %collective-permute-start.25 = (bf16[128,2048]{1,0:T(8,128)(2,1)S(1)}, bf16[128,2048]{1,0:T(8,128)(2,1)S(1)}, u32[]{:S(2)}, u32[]{:S(2)}) collective-permute-start(bf16[128,2048]{1,0:T(8,128)(2,1)S(1)} %slice.57), channel_id=1, source_target_pairs={{0,96},{4,28},{8,104},{12,4},{16,112},{20,12},{24,120},{28,20},{32... | collective-permute-start | bytes 1572872 | tf_op jit(solution)/shard_map/ppermute | solution.py:176
  84.5 1.0 constant_dynamic-update-slice_fusion.8
  85.5 1.0 constant_dynamic-update-slice_fusion.7
  86.5 4.4 %collective-permute-done.24 = bf16[128,2048]{1,0:T(8,128)(2,1)S(1)} collective-permute-done((bf16[128,2048]{1,0:T(8,128)(2,1)S(1)}, bf16[128,2048]{1,0:T(8,128)(2,1)S(1)}, u32[]{:S(2)}, u32[]{:S(2)}) %collective-permute-start.24) | collective-permute-done | bytes 524320 | tf_op jit(solution)/shard_map/ppermute | solution.py:176
  90.9 0.8 constant_dynamic-update-slice_fusion.6
  91.7 0.8 constant_dynamic-update-slice_fusion.5.mine_ref
  92.6 7.5 %collective-permute-start.26 = (bf16[1024,2048]{1,0:T(8,128)(2,1)}, bf16[1024,2048]{1,0:T(8,128)(2,1)}, u32[]{:S(2)}, u32[]{:S(2)}) collective-permute-start(bf16[1024,2048]{1,0:T(8,128)(2,1)} %constant_dynamic-update-slice_fusion.5.mine_ref), channel_id=1, source_target_pairs={{0,4},{4,0},{8,12},{12,8},{16,20},{20,16},{24,28},{28,24},{32,36},... | collective-permute-start | bytes 12582920 | tf_op jit(solution)/shard_map/ppermute | solution.py:198
  100.1 1.5 collective-permute-start.8
  101.8 0.8 collective-permute-start.6
  102.6 2.9 %collective-permute-done.7 = f32[64]{0:T(128)S(1)} collective-permute-done((f32[64]{0:T(128)S(1)}, f32[64]{0:T(128)S(1)}, u32[]{:S(2)}, u32[]{:S(2)}) %collective-permute-start.7) | collective-permute-done | bytes 288 | tf_op jit(solution)/shard_map/ppermute | solution.py:36
  105.5 2.3 collective-permute-start.10
  108.6 2.9 %collective-permute-start.12 = (f32[32,1]{0,1:T(1,128)S(1)}, f32[32,1]{0,1:T(1,128)S(1)}, u32[]{:S(2)}, u32[]{:S(2)}) collective-permute-start(f32[32,1]{0,1:T(1,128)S(1)} %slice.33), channel_id=1, source_target_pairs={{0,24},{4,100},{8,0},{12,108},{16,8},{20,116},{24,16},{28,124},{32... | collective-permute-start | bytes 392 | tf_op jit(solution)/shard_map/ppermute | solution.py:176
  112.2 2.9 %collective-permute-done.11 = f32[32,1]{0,1:T(1,128)S(1)} collective-permute-done((f32[32,1]{0,1:T(1,128)S(1)}, f32[32,1]{0,1:T(1,128)S(1)}, u32[]{:S(2)}, u32[]{:S(2)}) %collective-permute-start.11) | collective-permute-done | bytes 160 | tf_op jit(solution)/shard_map/ppermute | solution.py:176
  115.2 1.5 collective-permute-start.13
  116.7 1.0 collective-permute-done.14
  117.6 1.2 collective-permute-start.16
  119.3 0.7 collective-permute-done.16
  120.0 2.5 %collective-permute-done.15 = f32[128,1]{0,1:T(1,128)S(1)} collective-permute-done((f32[128,1]{0,1:T(1,128)S(1)}, f32[128,1]{0,1:T(1,128)S(1)}, u32[]{:S(2)}, u32[]{:S(2)}) %collective-permute-start.15) | collective-permute-done | bytes 544 | tf_op jit(solution)/shard_map/ppermute | solution.py:176
  122.6 6.6 %collective-permute-start.17 = (f32[1024,1]{0,1:T(1,128)S(1)}, f32[1024,1]{0,1:T(1,128)S(1)}, u32[]{:S(2)}, u32[]{:S(2)}) collective-permute-start(f32[1024,1]{0,1:T(1,128)S(1)} %concatenate.41), channel_id=1, source_target_pairs={{0,4},{4,0},{8,12},{12,8},{16,20},{20,16},{24,28},{28,24},{32,36},... | collective-permute-start | bytes 12296 | tf_op jit(solution)/shard_map/ppermute | solution.py:198
  129.2 1.4 copy.14.place_ref
  130.7 12.4 %gather_fusion = f32[2048]{0:T(1024)S(1)} fusion(f32[2048,1]{0,1:T(1,128)S(1)} %concatenate.42, s32[2048]{0:T(1024)S(1)} %get-tuple-element.11), kind=kCustom, calls=%fused_computation | custom fusion | bytes 32768 | tf_op jit(solution)/shard_map/gather | solution.py:267
  143.1 1.3 copy.15.scale_ref
  144.4 84.2 %shard_map.91 = f32[512,2048]{1,0:T(8,128)} custom-call(s32[2048,1]{1,0:T(8,128)} %copy.14.place_ref, f32[2048,1]{1,0:T(8,128)} %copy.15.scale_ref, bf16[1024,2048]{1,0:T(8,128)(2,1)} %constant_dynamic-update-slice_fusion.5.mine_ref, bf16[1024,2048]{1,0:T(8,128)(2,1)} %collective-permute-done.26.partner_ref, bf16[2048,2048]{1,0:T(8,128)(2,1)} %fusion.1.t_ref), custom_call_target="tpu_custom_call" | custom-call | flops 34359738368 | bytes 29360128 | tf_op jit(solution)/shard_map/pallas_call | solution.py:134
  228.6 4.7 %copy.40 = f32[512,2048]{1,0:T(8,128)} copy(f32[512,2048]{1,0:T(8,128)} %shard_map.91) | data formatting | bytes 8388608
  (65 shorter events, 6.2 us)
Async XLA Ops:
  0.0 14.0 %copy-start = (bf16[1024,128]{1,0:T(8,128)(2,1)S(1)}, bf16[1024,128]{1,0:T(8,128)(2,1)}, u32[]{:S(2)}) copy-start(bf16[1024,128]{1,0:T(8,128)(2,1)} %param.12) | copy-start | bytes 786436
  0.0 9.7 %copy-start.2 = (bf16[1024,128]{1,0:T(8,128)(2,1)S(1)}, bf16[1024,128]{1,0:T(8,128)(2,1)}, u32[]{:S(2)}) copy-start(bf16[1024,128]{1,0:T(8,128)(2,1)} %param.11) | copy-start | bytes 786436
  5.1 8.1 %copy-start.3 = (bf16[128,64]{0,1:T(8,128)(2,1)S(1)}, bf16[128,64]{0,1:T(8,128)(2,1)}, u32[]{:S(2)}) copy-start(bf16[128,64]{0,1:T(8,128)(2,1)} %param.13) | copy-start | bytes 49156
  5.2 22.9 %collective-permute-start.5 = (f32[2048]{0:T(1024)S(1)}, f32[2048]{0:T(1024)S(1)}, u32[]{:S(2)}, u32[]{:S(2)}) collective-permute-start(f32[2048]{0:T(1024)S(1)} %fusion), channel_id=1, source_target_pairs={{0,3},{1,0},{2,1},{3,2},{4,7},{5,4},{6,5},{7,6},{8,11},{9,8},{10,9... | collective-permute-start | bytes 24584 | tf_op jit(solution)/shard_map/ppermute | solution.py:36
  8.5 20.3 %collective-permute-start.4 = (f32[2048]{0:T(1024)S(1)}, f32[2048]{0:T(1024)S(1)}, u32[]{:S(2)}, u32[]{:S(2)}) collective-permute-start(f32[2048]{0:T(1024)S(1)} %fusion), channel_id=1, source_target_pairs={{0,2},{1,3},{2,0},{3,1},{4,6},{5,7},{6,4},{7,5},{8,10},{9,11},{10,... | collective-permute-start | bytes 24584 | tf_op jit(solution)/shard_map/ppermute | solution.py:36
  9.1 19.8 %collective-permute-start.3 = (f32[2048]{0:T(1024)S(1)}, f32[2048]{0:T(1024)S(1)}, u32[]{:S(2)}, u32[]{:S(2)}) collective-permute-start(f32[2048]{0:T(1024)S(1)} %fusion), channel_id=1, source_target_pairs={{0,1},{1,2},{2,3},{3,0},{4,5},{5,6},{6,7},{7,4},{8,9},{9,10},{10,1... | collective-permute-start | bytes 24584 | tf_op jit(solution)/shard_map/ppermute | solution.py:36
  9.7 4.4 %copy-start.1 = (bf16[2048,1024]{1,0:T(8,128)(2,1)S(1)}, bf16[2048,1024]{1,0:T(8,128)(2,1)}, u32[]{:S(2)}) copy-start(bf16[2048,1024]{1,0:T(8,128)(2,1)} %param.9) | copy-start | bytes 12582916
  14.0 5.9 %copy-start.5 = (s32[64]{0:T(128)S(1)}, s32[64]{0:T(128)}, u32[]{:S(2)}) copy-start(s32[64]{0:T(128)} %param.14) | copy-start | bytes 772
  14.1 6.0 %copy-start.4 = (s32[2048]{0:T(1024)S(1)}, s32[2048]{0:T(1024)}, u32[]{:S(2)}) copy-start(s32[2048]{0:T(1024)} %param.15) | copy-start | bytes 24580
  16.7 20.3 %collective-permute-start = (bf16[2048,144]{0,1:T(8,128)(2,1)}, bf16[2048,144]{0,1:T(8,128)(2,1)}, u32[]{:S(2)}, u32[]{:S(2)}) collective-permute-start(bf16[2048,144]{0,1:T(8,128)(2,1)} %get-tuple-element.15), channel_id=1, source_target_pairs={{0,1},{1,2},{2,3},{3,0},{4,5},{5,6},{6,7},{7,4},{8,9},{9,10},{10,1... | collective-permute-start | bytes 1769480 | tf_op jit(solution)/shard_map/ppermute | solution.py:36
  18.2 26.5 %collective-permute-start.1 = (bf16[2048,144]{0,1:T(8,128)(2,1)S(1)}, bf16[2048,144]{0,1:T(8,128)(2,1)}, u32[]{:S(2)}, u32[]{:S(2)}) collective-permute-start(bf16[2048,144]{0,1:T(8,128)(2,1)S(1)} %get-tuple-element.16), channel_id=1, source_target_pairs={{0,2},{1,3},{2,0},{3,1},{4,6},{5,7},{6,4},{7,5},{8,10},{9,11},{10,... | collective-permute-start | bytes 1769480 | tf_op jit(solution)/shard_map/ppermute | solution.py:36
  28.1 16.7 %collective-permute-start.2 = (bf16[2048,144]{0,1:T(8,128)(2,1)S(1)}, bf16[2048,144]{0,1:T(8,128)(2,1)S(1)}, u32[]{:S(2)}, u32[]{:S(2)}) collective-permute-start(bf16[2048,144]{0,1:T(8,128)(2,1)S(1)} %get-tuple-element.17), channel_id=1, source_target_pairs={{0,3},{1,0},{2,1},{3,2},{4,7},{5,4},{6,5},{7,6},{8,11},{9,8},{10,9... | collective-permute-start | bytes 1769480 | tf_op jit(solution)/shard_map/ppermute | solution.py:36
  48.8 6.3 %collective-permute-start.19 = (bf16[64,2048]{1,0:T(8,128)(2,1)S(1)}, bf16[64,2048]{1,0:T(8,128)(2,1)S(1)}, u32[]{:S(2)}, u32[]{:S(2)}) collective-permute-start(bf16[64,2048]{1,0:T(8,128)(2,1)S(1)} %bitcast.27), channel_id=1, source_target_pairs={{0,24},{4,100},{8,0},{12,108},{16,8},{20,116},{24,16},{28,124},{32... | collective-permute-start | bytes 786440 | tf_op jit(solution)/shard_map/ppermute | solution.py:176
  51.8 6.5 %collective-permute-start.18 = (bf16[64,2048]{1,0:T(8,128)(2,1)S(1)}, bf16[64,2048]{1,0:T(8,128)(2,1)S(1)}, u32[]{:S(2)}, u32[]{:S(2)}) collective-permute-start(bf16[64,2048]{1,0:T(8,128)(2,1)S(1)} %bitcast.28), channel_id=1, source_target_pairs={{0,8},{4,36},{8,16},{12,44},{16,24},{20,52},{24,0},{28,60},{32,40}... | collective-permute-start | bytes 786440 | tf_op jit(solution)/shard_map/ppermute | solution.py:176
  55.1 9.0 %collective-permute-start.21 = (bf16[32,2048]{1,0:T(8,128)(2,1)S(1)}, bf16[32,2048]{1,0:T(8,128)(2,1)S(1)}, u32[]{:S(2)}, u32[]{:S(2)}) collective-permute-start(bf16[32,2048]{1,0:T(8,128)(2,1)S(1)} %slice.55), channel_id=1, source_target_pairs={{0,24},{4,100},{8,0},{12,108},{16,8},{20,116},{24,16},{28,124},{32... | collective-permute-start | bytes 393224 | tf_op jit(solution)/shard_map/ppermute | solution.py:176
  58.3 5.1 %collective-permute-start.20 = (bf16[32,2048]{1,0:T(8,128)(2,1)S(1)}, bf16[32,2048]{1,0:T(8,128)(2,1)S(1)}, u32[]{:S(2)}, u32[]{:S(2)}) collective-permute-start(bf16[32,2048]{1,0:T(8,128)(2,1)S(1)} %slice.54), channel_id=1, source_target_pairs={{0,8},{4,36},{8,16},{12,44},{16,24},{20,52},{24,0},{28,60},{32,40}... | collective-permute-start | bytes 393224 | tf_op jit(solution)/shard_map/ppermute | solution.py:176
  64.8 16.8 %collective-permute-start.22 = (bf16[256,2048]{1,0:T(8,128)(2,1)S(1)}, bf16[256,2048]{1,0:T(8,128)(2,1)S(1)}, u32[]{:S(2)}, u32[]{:S(2)}) collective-permute-start(bf16[256,2048]{1,0:T(8,128)(2,1)S(1)} %get-tuple-element.27), channel_id=1, source_target_pairs={{0,32},{4,12},{8,40},{12,20},{16,48},{20,28},{24,56},{28,4},{32,64... | collective-permute-start | bytes 3145736 | tf_op jit(solution)/shard_map/ppermute | solution.py:176
  66.4 15.3 %collective-permute-start.23 = (bf16[256,2048]{1,0:T(8,128)(2,1)S(1)}, bf16[256,2048]{1,0:T(8,128)(2,1)S(1)}, u32[]{:S(2)}, u32[]{:S(2)}) collective-permute-start(bf16[256,2048]{1,0:T(8,128)(2,1)S(1)} %get-tuple-element.27), channel_id=1, source_target_pairs={{0,96},{4,28},{8,104},{12,4},{16,112},{20,12},{24,120},{28,20},{32... | collective-permute-start | bytes 3145736 | tf_op jit(solution)/shard_map/ppermute | solution.py:176
  81.6 9.3 %collective-permute-start.24 = (bf16[128,2048]{1,0:T(8,128)(2,1)S(1)}, bf16[128,2048]{1,0:T(8,128)(2,1)S(1)}, u32[]{:S(2)}, u32[]{:S(2)}) collective-permute-start(bf16[128,2048]{1,0:T(8,128)(2,1)S(1)} %slice.56), channel_id=1, source_target_pairs={{0,32},{4,12},{8,40},{12,20},{16,48},{20,28},{24,56},{28,4},{32,64... | collective-permute-start | bytes 1572872 | tf_op jit(solution)/shard_map/ppermute | solution.py:176
  81.7 10.0 %collective-permute-start.25 = (bf16[128,2048]{1,0:T(8,128)(2,1)S(1)}, bf16[128,2048]{1,0:T(8,128)(2,1)S(1)}, u32[]{:S(2)}, u32[]{:S(2)}) collective-permute-start(bf16[128,2048]{1,0:T(8,128)(2,1)S(1)} %slice.57), channel_id=1, source_target_pairs={{0,96},{4,28},{8,104},{12,4},{16,112},{20,12},{24,120},{28,20},{32... | collective-permute-start | bytes 1572872 | tf_op jit(solution)/shard_map/ppermute | solution.py:176
  92.6 51.8 %collective-permute-start.26 = (bf16[1024,2048]{1,0:T(8,128)(2,1)}, bf16[1024,2048]{1,0:T(8,128)(2,1)}, u32[]{:S(2)}, u32[]{:S(2)}) collective-permute-start(bf16[1024,2048]{1,0:T(8,128)(2,1)} %constant_dynamic-update-slice_fusion.5.mine_ref), channel_id=1, source_target_pairs={{0,4},{4,0},{8,12},{12,8},{16,20},{20,16},{24,28},{28,24},{32,36},... | collective-permute-start | bytes 12582920 | tf_op jit(solution)/shard_map/ppermute | solution.py:198
  100.1 2.5 %collective-permute-start.8 = (f32[64]{0:T(128)S(1)}, f32[64]{0:T(128)S(1)}, u32[]{:S(2)}, u32[]{:S(2)}) collective-permute-start(f32[64]{0:T(128)S(1)} %get-tuple-element.14), channel_id=1, source_target_pairs={{0,3},{1,0},{2,1},{3,2},{4,7},{5,4},{6,5},{7,6},{8,11},{9,8},{10,9... | collective-permute-start | bytes 776 | tf_op jit(solution)/shard_map/ppermute | solution.py:36
  101.6 3.9 %collective-permute-start.7 = (f32[64]{0:T(128)S(1)}, f32[64]{0:T(128)S(1)}, u32[]{:S(2)}, u32[]{:S(2)}) collective-permute-start(f32[64]{0:T(128)S(1)} %get-tuple-element.14), channel_id=1, source_target_pairs={{0,2},{1,3},{2,0},{3,1},{4,6},{5,7},{6,4},{7,5},{8,10},{9,11},{10,... | collective-permute-start | bytes 776 | tf_op jit(solution)/shard_map/ppermute | solution.py:36
  101.8 3.7 %collective-permute-start.6 = (f32[64]{0:T(128)S(1)}, f32[64]{0:T(128)S(1)}, u32[]{:S(2)}, u32[]{:S(2)}) collective-permute-start(f32[64]{0:T(128)S(1)} %get-tuple-element.14), channel_id=1, source_target_pairs={{0,1},{1,2},{2,3},{3,0},{4,5},{5,6},{6,7},{7,4},{8,9},{9,10},{10,1... | collective-permute-start | bytes 776 | tf_op jit(solution)/shard_map/ppermute | solution.py:36
  105.5 3.0 %collective-permute-start.10 = (f32[64,1]{0,1:T(1,128)S(1)}, f32[64,1]{0,1:T(1,128)S(1)}, u32[]{:S(2)}, u32[]{:S(2)}) collective-permute-start(f32[64,1]{0,1:T(1,128)S(1)} %rsqrt_bitcast_fusion), channel_id=1, source_target_pairs={{0,24},{4,100},{8,0},{12,108},{16,8},{20,116},{24,16},{28,124},{32... | collective-permute-start | bytes 776 | tf_op jit(solution)/shard_map/ppermute | solution.py:176
  107.8 3.7 %collective-permute-start.9 = (f32[64,1]{0,1:T(1,128)S(1)}, f32[64,1]{0,1:T(1,128)S(1)}, u32[]{:S(2)}, u32[]{:S(2)}) collective-permute-start(f32[64,1]{0,1:T(1,128)S(1)} %rsqrt_bitcast_fusion), channel_id=1, source_target_pairs={{0,8},{4,36},{8,16},{12,44},{16,24},{20,52},{24,0},{28,60},{32,40}... | collective-permute-start | bytes 776 | tf_op jit(solution)/shard_map/ppermute | solution.py:176
  108.6 3.6 %collective-permute-start.12 = (f32[32,1]{0,1:T(1,128)S(1)}, f32[32,1]{0,1:T(1,128)S(1)}, u32[]{:S(2)}, u32[]{:S(2)}) collective-permute-start(f32[32,1]{0,1:T(1,128)S(1)} %slice.33), channel_id=1, source_target_pairs={{0,24},{4,100},{8,0},{12,108},{16,8},{20,116},{24,16},{28,124},{32... | collective-permute-start | bytes 392 | tf_op jit(solution)/shard_map/ppermute | solution.py:176
  111.5 3.6 %collective-permute-start.11 = (f32[32,1]{0,1:T(1,128)S(1)}, f32[32,1]{0,1:T(1,128)S(1)}, u32[]{:S(2)}, u32[]{:S(2)}) collective-permute-start(f32[32,1]{0,1:T(1,128)S(1)} %bitcast.31), channel_id=1, source_target_pairs={{0,8},{4,36},{8,16},{12,44},{16,24},{20,52},{24,0},{28,60},{32,40}... | collective-permute-start | bytes 392 | tf_op jit(solution)/shard_map/ppermute | solution.py:176
  115.2 2.4 %collective-permute-start.14 = (f32[256,1]{0,1:T(1,128)S(1)}, f32[256,1]{0,1:T(1,128)S(1)}, u32[]{:S(2)}, u32[]{:S(2)}) collective-permute-start(f32[256,1]{0,1:T(1,128)S(1)} %concatenate.40), channel_id=1, source_target_pairs={{0,96},{4,28},{8,104},{12,4},{16,112},{20,12},{24,120},{28,20},{32... | collective-permute-start | bytes 3080 | tf_op jit(solution)/shard_map/ppermute | solution.py:176
  115.2 3.7 %collective-permute-start.13 = (f32[256,1]{0,1:T(1,128)S(1)}, f32[256,1]{0,1:T(1,128)S(1)}, u32[]{:S(2)}, u32[]{:S(2)}) collective-permute-start(f32[256,1]{0,1:T(1,128)S(1)} %concatenate.40), channel_id=1, source_target_pairs={{0,32},{4,12},{8,40},{12,20},{16,48},{20,28},{24,56},{28,4},{32,64... | collective-permute-start | bytes 3080 | tf_op jit(solution)/shard_map/ppermute | solution.py:176
  117.6 2.4 %collective-permute-start.16 = (f32[128,1]{0,1:T(1,128)S(1)}, f32[128,1]{0,1:T(1,128)S(1)}, u32[]{:S(2)}, u32[]{:S(2)}) collective-permute-start(f32[128,1]{0,1:T(1,128)S(1)} %slice.53), channel_id=1, source_target_pairs={{0,96},{4,28},{8,104},{12,4},{16,112},{20,12},{24,120},{28,20},{32... | collective-permute-start | bytes 1544 | tf_op jit(solution)/shard_map/ppermute | solution.py:176
  118.9 3.6 %collective-permute-start.15 = (f32[128,1]{0,1:T(1,128)S(1)}, f32[128,1]{0,1:T(1,128)S(1)}, u32[]{:S(2)}, u32[]{:S(2)}) collective-permute-start(f32[128,1]{0,1:T(1,128)S(1)} %slice.52), channel_id=1, source_target_pairs={{0,32},{4,12},{8,40},{12,20},{16,48},{20,28},{24,56},{28,4},{32,64... | collective-permute-start | bytes 1544 | tf_op jit(solution)/shard_map/ppermute | solution.py:176
  122.6 8.0 %collective-permute-start.17 = (f32[1024,1]{0,1:T(1,128)S(1)}, f32[1024,1]{0,1:T(1,128)S(1)}, u32[]{:S(2)}, u32[]{:S(2)}) collective-permute-start(f32[1024,1]{0,1:T(1,128)S(1)} %concatenate.41), channel_id=1, source_target_pairs={{0,4},{4,0},{8,12},{12,8},{16,20},{20,16},{24,28},{28,24},{32,36},... | collective-permute-start | bytes 12296 | tf_op jit(solution)/shard_map/ppermute | solution.py:198

commit v10 on v8

--- a/solution.py
+++ b/solution.py
@@ -37,27 +37,96 @@
     return total
 
 
-def ring_kernel(count, root, place_ref, mine_ref, partner_ref, t_ref, out_ref,
-                ordered, send_buf, recv_buf, acc, send_sem, recv_sem):
+def ring_kernel(count, root, place_ref, rows_ref, t_ref, out_ref, gathered,
+                ordered, send_buf, recv_buf, acc, send_sem, recv_sem, wide_send, wide_recv):
     me = lax.axis_index("narrow")
     right, left = lax.rem(me + 1, count), lax.rem(me + count - 1, count)
     rows = out_ref.shape[0]
     half = t_ref.shape[0] // 2
-    held = mine_ref.shape[0]
     tiles = rows // TILE
+    local = rows_ref.shape[0]
+    everyone = gathered.shape[0]
+
+    wide = lax.axis_index("wide")
+    y, z, core = wide // (2 * RING), (wide // 2) % RING, wide % 2
+
+    def wide_peer(first_axis, step):
+        along_z = (1 - core) if first_axis else core
+        along_y = 1 - along_z
+        return {"wide": (lax.rem(y + RING + step * along_y, RING) * RING
+                         + lax.rem(z + RING + step * along_z, RING)) * 2 + core}
+
+    partner = {"wide": wide + 1 - 2 * core}
+    peers = [wide_peer(True, 1), wide_peer(True, -1), wide_peer(False, 1), wide_peer(False, -1), partner]
 
     barrier = pltpu.get_barrier_semaphore()
     for neighbour in (left, right):
         pl.semaphore_signal(barrier, inc=1, device_id={"narrow": neighbour}, device_id_type=MESH)
-    pl.semaphore_wait(barrier, 2)
+    for peer in peers:
+        pl.semaphore_signal(barrier, inc=1, device_id=peer, device_id_type=MESH)
+    pl.semaphore_wait(barrier, 2 + len(peers))
+
+    def wide_copy(index, src, dst_start, size, peer):
+        return pltpu.make_async_remote_copy(
+            src_ref=src,
+            dst_ref=gathered.at[pl.ds(dst_start, size)],
+            send_sem=wide_send.at[index],
+            recv_sem=wide_recv.at[index],
+            device_id=peer,
+            device_id_type=MESH,
+        )
+
+    def at(start, size):
+        return gathered.at[pl.ds(start, size)]
+
+    block, bundle = local, RING * local
+    part_half, bundle_half = local // 2, bundle // 2
+    plan = []
+    plan.append(wide_copy(0, rows_ref, SLOT[RING - 1] * block, block, peers[0]))
+    plan.append(wide_copy(1, rows_ref, SLOT[1] * block, block, peers[1]))
+    gathered[0:block, :] = rows_ref[...]
+    plan[0].start()
+    plan[1].start()
+    plan[0].wait_recv()
+    plan.append(wide_copy(2, at(SLOT[RING - 1] * block, part_half), SLOT[2] * block, part_half, peers[0]))
+    plan[2].start()
+    plan[1].wait_recv()
+    plan.append(wide_copy(3, at(SLOT[1] * block + part_half, part_half),
+                          SLOT[2] * block + part_half, part_half, peers[1]))
+    plan[3].start()
+    plan[2].wait_recv()
+    plan[3].wait_recv()
+    plan.append(wide_copy(4, at(0, bundle), SLOT[RING - 1] * bundle, bundle, peers[2]))
+    plan.append(wide_copy(5, at(0, bundle), SLOT[1] * bundle, bundle, peers[3]))
+    plan.append(wide_copy(6, at(0, bundle), everyone // 2, bundle, partner))
+    for copy in plan[4:7]:
+        copy.start()
+    plan[4].wait_recv()
+    plan.append(wide_copy(7, at(SLOT[RING - 1] * bundle, bundle_half), SLOT[2] * bundle, bundle_half, peers[2]))
+    plan.append(wide_copy(8, at(SLOT[RING - 1] * bundle, bundle), everyone // 2 + SLOT[RING - 1] * bundle,
+                          bundle, partner))
+    plan[7].start()
+    plan[8].start()
+    plan[5].wait_recv()
+    plan.append(wide_copy(9, at(SLOT[1] * bundle + bundle_half, bundle_half),
+                          SLOT[2] * bundle + bundle_half, bundle_half, peers[3]))
+    plan.append(wide_copy(10, at(SLOT[1] * bundle, bundle), everyone // 2 + SLOT[1] * bundle,
+                          bundle, partner))
+    plan[9].start()
+    plan[10].start()
+    plan[7].wait_recv()
+    plan[9].wait_recv()
+    plan.append(wide_copy(11, at(SLOT[2] * bundle, bundle), everyone // 2 + SLOT[2] * bundle,
+                          bundle, partner))
+    plan[11].start()
+    for index in (6, 8, 10, 11):
+        plan[index].wait_recv()
 
     def order_rows(start):
         wanted = place_ref[pl.ds(start, TILE), :]
-        columns = lax.broadcasted_iota(jnp.int32, (TILE, held), 1)
-        pick_mine = (wanted == columns).astype(jnp.bfloat16)
-        pick_partner = (wanted == columns + held).astype(jnp.bfloat16)
-        picked = jnp.dot(pick_mine, mine_ref[...], preferred_element_type=jnp.float32)
-        picked = picked + jnp.dot(pick_partner, partner_ref[...], preferred_element_type=jnp.float32)
+        columns = lax.broadcasted_iota(jnp.int32, (TILE, everyone), 1)
+        pick = (wanted == columns).astype(jnp.bfloat16)
+        picked = jnp.dot(pick, gathered[...], preferred_element_type=jnp.float32)
         ordered[pl.ds(start, TILE), :] = picked.astype(jnp.bfloat16)
 
     def partial_rows(start, direction, part):
@@ -121,26 +190,31 @@
         return carry
 
     lax.fori_loop(0, tiles, drain, 0)
-
-
-def ring_scores(place, mine, partner, target_unit, count, root):
+    for copy in plan:
+        copy.wait_send()
+
+
+def ring_scores(place, unit_rows, target_unit, count, root):
     programs = place.shape[0]
-    depth = mine.shape[1]
+    depth = unit_rows.shape[1]
     rows = programs // count
     targets = target_unit.shape[0]
     half = targets // 2
     return pl.pallas_call(
         functools.partial(ring_kernel, count, root),
         out_shape=jax.ShapeDtypeStruct((rows, targets), jnp.float32),
-        in_specs=[pl.BlockSpec(memory_space=pltpu.VMEM)] * 4,
+        in_specs=[pl.BlockSpec(memory_space=pltpu.VMEM)] * 3,
         out_specs=pl.BlockSpec(memory_space=pltpu.VMEM),
         scratch_shapes=[
+            pltpu.VMEM((programs, depth), jnp.bfloat16),
             pltpu.VMEM((programs, depth), jnp.bfloat16),
             pltpu.VMEM((2, count - 1, rows // TILE, TILE, half), jnp.bfloat16),
             pltpu.VMEM((2, count - 1, rows // TILE, TILE, half), jnp.bfloat16),
             pltpu.VMEM((2, rows // TILE, TILE, half), jnp.float32),
             pltpu.SemaphoreType.DMA((2, count - 1, rows // TILE)),
             pltpu.SemaphoreType.DMA((2, count - 1, rows // TILE)),
+            pltpu.SemaphoreType.DMA((12,)),
+            pltpu.SemaphoreType.DMA((12,)),
         ],
         compiler_params=pltpu.CompilerParams(
             collective_id=0, has_side_effects=True, vmem_limit_bytes=62 * 1024 * 1024
@@ -150,7 +224,7 @@
             bytes_accessed=2 * (2 * programs + targets) * depth + 4 * rows * targets,
             transcendentals=0,
         ),
-    )(place.reshape(programs, 1), mine, partner, target_unit)
+    )(place.reshape(programs, 1), unit_rows, target_unit)
 
 
 RING = 4
@@ -188,14 +262,7 @@
     return jnp.concatenate([block, from_left, from_right, far], axis=0)
 
 
-def wide_gather(unit_rows, row_order):
-    first = ("z", "y")
-    second = ("y", "z")
-    bundle = ring_gather(unit_rows, first)
-    mine = ring_gather(bundle, second)
-    partner = lax.ppermute(mine, "wide", [(w, w ^ 1) for w in range(2 * RING * RING)])
-
-    local = unit_rows.shape[0]
+def gathered_place(row_order, local):
     y, z, c = wide_coords(lax.axis_index("wide"))
     slot = jnp.asarray(SLOT, jnp.int32)
     owner = row_order // local
@@ -204,7 +271,7 @@
     first_offset = jnp.where(oc == 0, dz, dy)
     second_offset = jnp.where(oc == 0, dy, dz)
     block = (oc != c) * (RING * RING) + slot[second_offset] * RING + slot[first_offset]
-    return mine, partner, block * local + row_order % local
+    return block * local + row_order % local
 
 
 def shards(
@@ -258,8 +325,8 @@
     squares = narrow_sum(squares, lambda dest: squares, narrow_count, narrow_index, jnp.float32)
     unit_rows = normalize_rows(features, squares)
     root_count = math.sqrt(float(targets.shape[1] * narrow_count))
-    mine, partner, place = wide_gather(unit_rows, row_order)
-    return ring_scores(place, mine, partner, target_unit, narrow_count, root_count)
+    place = gathered_place(row_order, unit_rows.shape[0])
+    return ring_scores(place, unit_rows, target_unit, narrow_count, root_count)
 
 
 def solution(mesh):

time: 204 us -> 184 us (0.902)
  Pallas kernels: 83.7 us -> 121 us
  waiting for transfers between devices: 40.1 us -> 10 us
  starting transfers between devices: 33.8 us -> 13.2 us
  local copies, waits for them, and re-layouts: 22.2 us -> 14.8 us
    pallas_call x1, Pallas kernels: 83.7 us -> 121 us  [ring_scores(): pl.pallas_call(functools.partial(ring_kernel, count, root), out_shape=jax...]
    ppermute x9 -> x0, waiting for transfers between devices: 28.7 us -> none  [the longest x8 23 us: wide_shift(): return lax.ppermute(x, 'wide', perm)]
    ppermute x9 -> x0, starting transfers between devices: 20.6 us -> none  [the longest x8 13.2 us: wide_shift(): return lax.ppermute(x, 'wide', perm)]
    unnamed x20 -> x13, local copies, waits for them, and re-layouts: 10.5 us -> 4.73 us
    convert_element_type x1 -> x2, other arithmetic: 8.06 us -> 8.91 us  [normalize_rows(): (features * lax.rsqrt(squares + epsilon)[:, None]).astype(jnp.bfloat16)]
  transfers between devices with their start and end apart: 18 -> 9, of which waited for: 9 -> 4; matrix products, arithmetic and copies ran while one was open for 15% -> 13% of each run, Pallas kernels for 0% -> 0%
where the time goes in v10:
time: 184 us
  Pallas kernels  121 us (66%)
  other arithmetic  16.8 us (9%)
  local copies, waits for them, and re-layouts  14.8 us (8%)
  starting transfers between devices  13.2 us (7%)
  waiting for transfers between devices  10 us (5%)
  matrix products  7.6 us (4%)
    pallas_call x1, Pallas kernels, ring_scores(): pl.pallas_call(functools.partial(ring_kernel, count, root), out_shape=jax...  121 us
    ppermute x9, starting transfers between devices, narrow_sum(): total = total + lax.ppermute(piece, 'narrow', perm).astype(jnp.float32)  13.2 us
    ppermute x9, waiting for transfers between devices, narrow_sum(): total = total + lax.ppermute(piece, 'narrow', perm).astype(jnp.float32)  10 us
    convert_element_type x2, other arithmetic, normalize_rows(): (features * lax.rsqrt(squares + epsilon)[:, None]).astype(jnp.bfloat16)  8.91 us
    scatter x1, local copies, waits for them, and re-layouts, shards(): jnp.zeros_like(program_output_index).at[program_output_index]  8.05 us
    reduce_sum x1, other arithmetic, shards(): target_squares = jnp.sum(target_wide * target_wide, axis=1)  5.14 us
    unnamed x13, local copies, waits for them, and re-layouts  4.73 us
  transfers between devices with their start and end apart: 9, of which 4 were waited for; matrix products, arithmetic and copies ran while one was open for 13% of the time, Pallas kernels for 0%

profile of v10, /device:TPU:1, one launch (start us, length us, event | category | flops | bytes accessed | tf_op | source)
XLA Modules:
  0.0 183.7 jit_solution(9131598039033316390)
XLA Ops:
  0.0 0.0 copy-start
  0.0 0.0 copy-start.2
  0.0 5.1 %fusion = f32[2048]{0:T(1024)S(1)} fusion(bf16[2048,2048]{1,0:T(8,128)(2,1)} %param.16), kind=kLoop, calls=%fused_computation.3 | loop fusion | flops 12580864 | bytes 8396800 | tf_op jit(solution)/shard_map/reduce_sum | solution.py:293
  5.1 0.0 copy-start.3
  5.2 3.4 %collective-permute-start.5 = (f32[2048]{0:T(1024)S(1)}, f32[2048]{0:T(1024)S(1)}, u32[]{:S(2)}, u32[]{:S(2)}) collective-permute-start(f32[2048]{0:T(1024)S(1)} %fusion), channel_id=1, source_target_pairs={{0,3},{1,0},{2,1},{3,2},{4,7},{5,4},{6,5},{7,6},{8,11},{9,8},{10,9... | collective-permute-start | bytes 24584 | tf_op jit(solution)/shard_map/ppermute | solution.py:36
  8.5 0.5 collective-permute-start.4
  9.1 0.6 collective-permute-start.3
  9.7 0.0 copy-done.2
  9.7 0.0 copy-start.1
  9.7 3.6 %fusion.24 = f32[2048,128]{1,0:T(8,128)S(1)} fusion(bf16[2048,1024]{1,0:T(8,128)(2,1)} %param.10, bf16[1024,128]{1,0:T(8,128)(2,1)S(1)} %copy-done.2), kind=kOutput, calls=%fused_computation.70 | convolution fusion | flops 536870912 | bytes 5505024 | tf_op jit(solution)/shard_map/dot_general | solution.py:304
  13.3 0.0 copy-done.3
  13.3 0.7 fusion.25
  14.0 0.0 copy-done
  14.0 0.0 copy-done.1
  14.0 0.0 copy-start.5
  14.1 0.0 copy-start.4
  14.1 1.5 fusion.23
  15.6 1.0 pad_maximum_fusion
  16.7 1.5 collective-permute-start
  18.2 1.7 collective-permute-start.1
  19.9 0.0 copy-done.5
  19.9 0.1 fusion.7
  20.0 0.0 copy-done.4
  20.1 8.0 %scatter_custom_fusion = s32[2048]{0:T(1024)S(1)} fusion(s32[2048]{0:T(1024)S(1)} %compare_select_fusion.2, s32[2048]{0:T(1024)S(1)} %iota.10, s32[]{:T(128)} %constant.126.clone.1), kind=kCustom, calls=%fused_computation.65 | custom fusion | bytes 8196 | tf_op jit(solution)/shard_map/scatter | solution.py:298
  28.1 0.0 collective-permute-done.5
  28.2 0.7 collective-permute-start.2
  28.9 0.0 collective-permute-done.4
  28.9 0.0 collective-permute-done.3
  28.9 8.0 %fusion.1.t_ref = bf16[2048,2048]{1,0:T(8,128)(2,1)} fusion(bf16[2048,2048]{1,0:T(8,128)(2,1)} %param.16, f32[2048]{0:T(1024)S(1)} %add_rsqrt_fusion), kind=kLoop, calls=%fused_computation.4 | loop fusion | flops 12582912 | bytes 16785408 | tf_op jit(solution)/shard_map/convert_element_type | solution.py:28
  36.9 0.0 collective-permute-done
  36.9 7.8 %collective-permute-done.1 = bf16[2048,144]{0,1:T(8,128)(2,1)} collective-permute-done((bf16[2048,144]{0,1:T(8,128)(2,1)S(1)}, bf16[2048,144]{0,1:T(8,128)(2,1)}, u32[]{:S(2)}, u32[]{:S(2)}) %collective-permute-start.1) | collective-permute-done | bytes 589856 | tf_op jit(solution)/shard_map/ppermute | solution.py:36
  44.7 0.1 collective-permute-done.2
  44.8 1.5 fusion.3
  46.3 0.1 slice.7
  46.4 0.3 copy.12
  46.8 0.2 reshape.35
  47.0 1.7 multiply_reduce_fusion
  48.7 3.6 %collective-permute-start.8 = (f32[64]{0:T(128)S(1)}, f32[64]{0:T(128)S(1)}, u32[]{:S(2)}, u32[]{:S(2)}) collective-permute-start(f32[64]{0:T(128)S(1)} %get-tuple-element.19), channel_id=1, source_target_pairs={{0,3},{1,0},{2,1},{3,2},{4,7},{5,4},{6,5},{7,6},{8,11},{9,8},{10,9... | collective-permute-start | bytes 776 | tf_op jit(solution)/shard_map/ppermute | solution.py:36
  52.4 1.0 collective-permute-start.7
  53.4 0.0 collective-permute-start.6
  53.5 1.3 copy.14.place_ref
  54.8 0.0 collective-permute-done.8
  54.8 1.4 collective-permute-done.7
  56.3 0.7 collective-permute-done.6
  57.0 0.9 fusion.4.rows_ref
  57.9 121.1 %shard_map.91 = f32[512,2048]{1,0:T(8,128)} custom-call(s32[2048,1]{1,0:T(8,128)} %copy.14.place_ref, bf16[64,2048]{1,0:T(8,128)(2,1)} %fusion.4.rows_ref, bf16[2048,2048]{1,0:T(8,128)(2,1)} %fusion.1.t_ref), custom_call_target="tpu_custom_call" | custom-call | flops 34359738368 | bytes 29360128 | tf_op jit(solution)/shard_map/pallas_call | solution.py:203
  179.0 4.7 %copy.22 = f32[512,2048]{1,0:T(8,128)} copy(f32[512,2048]{1,0:T(8,128)} %shard_map.91) | data formatting | bytes 8388608
  (9 shorter events, 0.2 us)
Async XLA Ops:
  0.0 14.0 %copy-start = (bf16[1024,128]{1,0:T(8,128)(2,1)S(1)}, bf16[1024,128]{1,0:T(8,128)(2,1)}, u32[]{:S(2)}) copy-start(bf16[1024,128]{1,0:T(8,128)(2,1)} %param.12) | copy-start | bytes 786436
  0.0 9.7 %copy-start.2 = (bf16[1024,128]{1,0:T(8,128)(2,1)S(1)}, bf16[1024,128]{1,0:T(8,128)(2,1)}, u32[]{:S(2)}) copy-start(bf16[1024,128]{1,0:T(8,128)(2,1)} %param.11) | copy-start | bytes 786436
  5.1 8.1 %copy-start.3 = (bf16[128,64]{0,1:T(8,128)(2,1)S(1)}, bf16[128,64]{0,1:T(8,128)(2,1)}, u32[]{:S(2)}) copy-start(bf16[128,64]{0,1:T(8,128)(2,1)} %param.13) | copy-start | bytes 49156
  5.2 23.0 %collective-permute-start.5 = (f32[2048]{0:T(1024)S(1)}, f32[2048]{0:T(1024)S(1)}, u32[]{:S(2)}, u32[]{:S(2)}) collective-permute-start(f32[2048]{0:T(1024)S(1)} %fusion), channel_id=1, source_target_pairs={{0,3},{1,0},{2,1},{3,2},{4,7},{5,4},{6,5},{7,6},{8,11},{9,8},{10,9... | collective-permute-start | bytes 24584 | tf_op jit(solution)/shard_map/ppermute | solution.py:36
  8.5 20.4 %collective-permute-start.4 = (f32[2048]{0:T(1024)S(1)}, f32[2048]{0:T(1024)S(1)}, u32[]{:S(2)}, u32[]{:S(2)}) collective-permute-start(f32[2048]{0:T(1024)S(1)} %fusion), channel_id=1, source_target_pairs={{0,2},{1,3},{2,0},{3,1},{4,6},{5,7},{6,4},{7,5},{8,10},{9,11},{10,... | collective-permute-start | bytes 24584 | tf_op jit(solution)/shard_map/ppermute | solution.py:36
  9.1 19.9 %collective-permute-start.3 = (f32[2048]{0:T(1024)S(1)}, f32[2048]{0:T(1024)S(1)}, u32[]{:S(2)}, u32[]{:S(2)}) collective-permute-start(f32[2048]{0:T(1024)S(1)} %fusion), channel_id=1, source_target_pairs={{0,1},{1,2},{2,3},{3,0},{4,5},{5,6},{6,7},{7,4},{8,9},{9,10},{10,1... | collective-permute-start | bytes 24584 | tf_op jit(solution)/shard_map/ppermute | solution.py:36
  9.7 4.4 %copy-start.1 = (bf16[2048,1024]{1,0:T(8,128)(2,1)S(1)}, bf16[2048,1024]{1,0:T(8,128)(2,1)}, u32[]{:S(2)}) copy-start(bf16[2048,1024]{1,0:T(8,128)(2,1)} %param.9) | copy-start | bytes 12582916
  14.0 5.9 %copy-start.5 = (s32[64]{0:T(128)S(1)}, s32[64]{0:T(128)}, u32[]{:S(2)}) copy-start(s32[64]{0:T(128)} %param.14) | copy-start | bytes 772
  14.1 6.0 %copy-start.4 = (s32[2048]{0:T(1024)S(1)}, s32[2048]{0:T(1024)}, u32[]{:S(2)}) copy-start(s32[2048]{0:T(1024)} %param.15) | copy-start | bytes 24580
  16.7 20.3 %collective-permute-start = (bf16[2048,144]{0,1:T(8,128)(2,1)}, bf16[2048,144]{0,1:T(8,128)(2,1)}, u32[]{:S(2)}, u32[]{:S(2)}) collective-permute-start(bf16[2048,144]{0,1:T(8,128)(2,1)} %get-tuple-element.11), channel_id=1, source_target_pairs={{0,1},{1,2},{2,3},{3,0},{4,5},{5,6},{6,7},{7,4},{8,9},{9,10},{10,1... | collective-permute-start | bytes 1769480 | tf_op jit(solution)/shard_map/ppermute | solution.py:36
  18.2 26.5 %collective-permute-start.1 = (bf16[2048,144]{0,1:T(8,128)(2,1)S(1)}, bf16[2048,144]{0,1:T(8,128)(2,1)}, u32[]{:S(2)}, u32[]{:S(2)}) collective-permute-start(bf16[2048,144]{0,1:T(8,128)(2,1)S(1)} %get-tuple-element.12), channel_id=1, source_target_pairs={{0,2},{1,3},{2,0},{3,1},{4,6},{5,7},{6,4},{7,5},{8,10},{9,11},{10,... | collective-permute-start | bytes 1769480 | tf_op jit(solution)/shard_map/ppermute | solution.py:36
  28.2 16.6 %collective-permute-start.2 = (bf16[2048,144]{0,1:T(8,128)(2,1)S(1)}, bf16[2048,144]{0,1:T(8,128)(2,1)S(1)}, u32[]{:S(2)}, u32[]{:S(2)}) collective-permute-start(bf16[2048,144]{0,1:T(8,128)(2,1)S(1)} %get-tuple-element.13), channel_id=1, source_target_pairs={{0,3},{1,0},{2,1},{3,2},{4,7},{5,4},{6,5},{7,6},{8,11},{9,8},{10,9... | collective-permute-start | bytes 1769480 | tf_op jit(solution)/shard_map/ppermute | solution.py:36
  48.7 6.1 %collective-permute-start.8 = (f32[64]{0:T(128)S(1)}, f32[64]{0:T(128)S(1)}, u32[]{:S(2)}, u32[]{:S(2)}) collective-permute-start(f32[64]{0:T(128)S(1)} %get-tuple-element.19), channel_id=1, source_target_pairs={{0,3},{1,0},{2,1},{3,2},{4,7},{5,4},{6,5},{7,6},{8,11},{9,8},{10,9... | collective-permute-start | bytes 776 | tf_op jit(solution)/shard_map/ppermute | solution.py:36
  52.4 3.9 %collective-permute-start.7 = (f32[64]{0:T(128)S(1)}, f32[64]{0:T(128)S(1)}, u32[]{:S(2)}, u32[]{:S(2)}) collective-permute-start(f32[64]{0:T(128)S(1)} %get-tuple-element.19), channel_id=1, source_target_pairs={{0,2},{1,3},{2,0},{3,1},{4,6},{5,7},{6,4},{7,5},{8,10},{9,11},{10,... | collective-permute-start | bytes 776 | tf_op jit(solution)/shard_map/ppermute | solution.py:36
  53.4 3.6 %collective-permute-start.6 = (f32[64]{0:T(128)S(1)}, f32[64]{0:T(128)S(1)}, u32[]{:S(2)}, u32[]{:S(2)}) collective-permute-start(f32[64]{0:T(128)S(1)} %get-tuple-element.19), channel_id=1, source_target_pairs={{0,1},{1,2},{2,3},{3,0},{4,5},{5,6},{6,7},{7,4},{8,9},{9,10},{10,1... | collective-permute-start | bytes 776 | tf_op jit(solution)/shard_map/ppermute | solution.py:36

commit v11 on v10

--- a/solution.py
+++ b/solution.py
@@ -37,7 +37,7 @@
     return total
 
 
-def ring_kernel(count, root, place_ref, rows_ref, t_ref, out_ref, gathered,
+def ring_kernel(count, root, dest_ref, rows_ref, t_ref, out_ref, gathered,
                 ordered, send_buf, recv_buf, acc, send_sem, recv_sem, wide_send, wide_recv):
     me = lax.axis_index("narrow")
     right, left = lax.rem(me + 1, count), lax.rem(me + count - 1, count)
@@ -123,9 +123,8 @@
         plan[index].wait_recv()
 
     def order_rows(start):
-        wanted = place_ref[pl.ds(start, TILE), :]
-        columns = lax.broadcasted_iota(jnp.int32, (TILE, everyone), 1)
-        pick = (wanted == columns).astype(jnp.bfloat16)
+        wanted = start + lax.broadcasted_iota(jnp.int32, (TILE, everyone), 0)
+        pick = (dest_ref[...] == wanted).astype(jnp.bfloat16)
         picked = jnp.dot(pick, gathered[...], preferred_element_type=jnp.float32)
         ordered[pl.ds(start, TILE), :] = picked.astype(jnp.bfloat16)
 
@@ -194,8 +193,8 @@
         copy.wait_send()
 
 
-def ring_scores(place, unit_rows, target_unit, count, root):
-    programs = place.shape[0]
+def ring_scores(dest, unit_rows, target_unit, count, root):
+    programs = dest.shape[0]
     depth = unit_rows.shape[1]
     rows = programs // count
     targets = target_unit.shape[0]
@@ -224,7 +223,7 @@
             bytes_accessed=2 * (2 * programs + targets) * depth + 4 * rows * targets,
             transcendentals=0,
         ),
-    )(place.reshape(programs, 1), unit_rows, target_unit)
+    )(dest.reshape(1, programs), unit_rows, target_unit)
 
 
 RING = 4
@@ -262,16 +261,18 @@
     return jnp.concatenate([block, from_left, from_right, far], axis=0)
 
 
-def gathered_place(row_order, local):
+def gathered_dest(program_output_index, local):
     y, z, c = wide_coords(lax.axis_index("wide"))
-    slot = jnp.asarray(SLOT, jnp.int32)
-    owner = row_order // local
-    oy, oz, oc = wide_coords(owner)
-    dz, dy = (oz - z) % RING, (oy - y) % RING
-    first_offset = jnp.where(oc == 0, dz, dy)
-    second_offset = jnp.where(oc == 0, dy, dz)
-    block = (oc != c) * (RING * RING) + slot[second_offset] * RING + slot[first_offset]
-    return block * local + row_order % local
+    offset_of_slot = jnp.asarray([SLOT.index(k) for k in range(RING)], jnp.int32)
+    position = jnp.arange(program_output_index.shape[0], dtype=jnp.int32)
+    region, block, row = position // (RING * RING * local), (position // local) % (RING * RING), position % local
+    first = offset_of_slot[block % RING]
+    second = offset_of_slot[block // RING]
+    oc = jnp.where(region == 0, c, 1 - c)
+    oz = (z + jnp.where(oc == 0, first, second)) % RING
+    oy = (y + jnp.where(oc == 0, second, first)) % RING
+    program = ((oy * RING + oz) * 2 + oc) * local + row
+    return program_output_index[program]
 
 
 def shards(
@@ -295,11 +296,6 @@
         target_squares, lambda dest: target_squares, narrow_count, narrow_index, jnp.float32
     )
     target_unit = normalize_rows(target_wide, target_squares)
-    row_order = jnp.zeros_like(program_output_index).at[program_output_index].set(
-        jnp.arange(program_output_index.shape[0], dtype=jnp.int32),
-        mode="promise_in_bounds",
-        unique_indices=True,
-    )
 
     reduced_sums = jnp.dot(
         output_gradient_rows, adapter_up_weight, preferred_element_type=jnp.float32
@@ -315,9 +311,7 @@
         return jnp.concatenate([quarter, in_part], axis=1)
 
     summed_parts = narrow_sum(send_for(narrow_index), send_for, narrow_count, narrow_index)
-    summed_parts, target_unit, row_order = lax.optimization_barrier(
-        (summed_parts, target_unit, row_order)
-    )
+    summed_parts, target_unit = lax.optimization_barrier((summed_parts, target_unit))
     quarter = summed_parts[:, :quarter_cols]
     in_all = summed_parts[:, quarter_cols:]
     features = program_features(quarter, in_all, lengths, length)
@@ -325,8 +319,8 @@
     squares = narrow_sum(squares, lambda dest: squares, narrow_count, narrow_index, jnp.float32)
     unit_rows = normalize_rows(features, squares)
     root_count = math.sqrt(float(targets.shape[1] * narrow_count))
-    place = gathered_place(row_order, unit_rows.shape[0])
-    return ring_scores(place, unit_rows, target_unit, narrow_count, root_count)
+    dest = gathered_dest(program_output_index, unit_rows.shape[0])
+    return ring_scores(dest, unit_rows, target_unit, narrow_count, root_count)
 
 
 def solution(mesh):

time: 184 us -> 202 us (1.098)
  local copies, waits for them, and re-layouts: 14.8 us -> 25.8 us
  waiting for transfers between devices: 10 us -> 16.4 us
    gather x0 -> x1, local copies, waits for them, and re-layouts: none -> 20.5 us  [gathered_dest(): return program_output_index[program]]
    scatter x1 -> x0, local copies, waits for them, and re-layouts: 8.05 us -> none  [shards(): jnp.zeros_like(program_output_index).at[program_output_index]]
    ppermute x9, waiting for transfers between devices: 10 us -> 16.4 us  [narrow_sum(): total = total + lax.ppermute(piece, 'narrow', perm).astype(jnp.float32)]
  transfers between devices with their start and end apart: 9 -> 9, of which waited for: 4 -> 3; matrix products, arithmetic and copies ran while one was open for 13% -> 18% of each run, Pallas kernels for 0% -> 0%
where the time goes in v11:
time: 202 us; the launch traced here: 201 us
  Pallas kernels  122 us (60%)
  local copies, waits for them, and re-layouts  25.8 us (13%)
  other arithmetic  16.9 us (8%)
  waiting for transfers between devices  16.4 us (8%)
  starting transfers between devices  12.6 us (6%)
  matrix products  7.66 us (4%)
    pallas_call x1, Pallas kernels, ring_scores(): pl.pallas_call(functools.partial(ring_kernel, count, root), out_shape=jax...  122 us
    gather x1, local copies, waits for them, and re-layouts, gathered_dest(): return program_output_index[program]  20.5 us
    ppermute x9, waiting for transfers between devices, narrow_sum(): total = total + lax.ppermute(piece, 'narrow', perm).astype(jnp.float32)  16.4 us
    ppermute x9, starting transfers between devices, narrow_sum(): total = total + lax.ppermute(piece, 'narrow', perm).astype(jnp.float32)  12.6 us
    convert_element_type x2, other arithmetic, normalize_rows(): (features * lax.rsqrt(squares + epsilon)[:, None]).astype(jnp.bfloat16)  8.91 us
    reduce_sum x1, other arithmetic, shards(): target_squares = jnp.sum(target_wide * target_wide, axis=1)  5.14 us
    unnamed x13, local copies, waits for them, and re-layouts  4.73 us
  transfers between devices with their start and end apart: 9, of which 3 were waited for; matrix products, arithmetic and copies ran while one was open for 18% of the time, Pallas kernels for 0%

profile of v11, /device:TPU:1, one launch (start us, length us, event | category | flops | bytes accessed | tf_op | source)
XLA Modules:
  0.0 201.4 jit_solution(14670341902139191683)
XLA Ops:
  0.0 0.0 copy-start
  0.0 0.0 copy-start.3
  0.0 5.1 %fusion = f32[2048]{0:T(1024)S(1)} fusion(bf16[2048,2048]{1,0:T(8,128)(2,1)} %param.16), kind=kLoop, calls=%fused_computation.3 | loop fusion | flops 12580864 | bytes 8396800 | tf_op jit(solution)/shard_map/reduce_sum | solution.py:294
  5.1 0.0 copy-start.4
  5.2 3.4 %collective-permute-start.5 = (f32[2048]{0:T(1024)S(1)}, f32[2048]{0:T(1024)S(1)}, u32[]{:S(2)}, u32[]{:S(2)}) collective-permute-start(f32[2048]{0:T(1024)S(1)} %fusion), channel_id=1, source_target_pairs={{0,3},{1,0},{2,1},{3,2},{4,7},{5,4},{6,5},{7,6},{8,11},{9,8},{10,9... | collective-permute-start | bytes 24584 | tf_op jit(solution)/shard_map/ppermute | solution.py:36
  8.5 0.5 collective-permute-start.4
  9.1 0.6 collective-permute-start.3
  9.7 0.0 copy-done.3
  9.7 0.0 copy-start.2
  9.7 3.6 %fusion.17 = f32[2048,128]{1,0:T(8,128)S(1)} fusion(bf16[2048,1024]{1,0:T(8,128)(2,1)} %param.10, bf16[1024,128]{1,0:T(8,128)(2,1)S(1)} %copy-done.3), kind=kOutput, calls=%fused_computation.69 | convolution fusion | flops 536870912 | bytes 5505024 | tf_op jit(solution)/shard_map/dot_general | solution.py:300
  13.3 0.0 copy-done.4
  13.3 0.7 fusion.18
  14.0 0.0 copy-done
  14.0 0.0 copy-done.2
  14.0 0.0 copy-start.5
  14.1 1.5 fusion.16
  15.6 1.0 pad_maximum_fusion
  16.7 1.5 collective-permute-start
  18.2 1.7 collective-permute-start.1
  19.9 0.0 copy-done.5
  19.9 0.1 fusion.7
  20.0 0.2 compare_select_fusion
  20.2 0.0 collective-permute-done.5
  20.2 0.7 collective-permute-start.2
  20.9 0.0 collective-permute-done.4
  20.9 0.0 collective-permute-done.3
  21.0 8.0 %fusion.1.t_ref = bf16[2048,2048]{1,0:T(8,128)(2,1)} fusion(bf16[2048,2048]{1,0:T(8,128)(2,1)} %param.16, f32[2048]{0:T(1024)S(1)} %add_rsqrt_fusion), kind=kLoop, calls=%fused_computation.4 | loop fusion | flops 12582912 | bytes 16785408 | tf_op jit(solution)/shard_map/convert_element_type | solution.py:28
  29.0 2.5 %collective-permute-done = bf16[2048,144]{0,1:T(8,128)(2,1)} collective-permute-done((bf16[2048,144]{0,1:T(8,128)(2,1)}, bf16[2048,144]{0,1:T(8,128)(2,1)}, u32[]{:S(2)}, u32[]{:S(2)}) %collective-permute-start) | collective-permute-done | bytes 589856 | tf_op jit(solution)/shard_map/ppermute | solution.py:36
  31.5 13.2 %collective-permute-done.1 = bf16[2048,144]{0,1:T(8,128)(2,1)} collective-permute-done((bf16[2048,144]{0,1:T(8,128)(2,1)S(1)}, bf16[2048,144]{0,1:T(8,128)(2,1)}, u32[]{:S(2)}, u32[]{:S(2)}) %collective-permute-start.1) | collective-permute-done | bytes 589856 | tf_op jit(solution)/shard_map/ppermute | solution.py:36
  44.7 0.6 collective-permute-done.2
  45.3 1.5 fusion.3
  46.9 0.0 copy-start.1
  46.9 0.1 slice.7
  47.0 0.3 copy.12
  47.3 0.2 reshape.347
  47.5 1.8 multiply_reduce_fusion
  49.3 3.5 %collective-permute-start.8 = (f32[64]{0:T(128)S(1)}, f32[64]{0:T(128)S(1)}, u32[]{:S(2)}, u32[]{:S(2)}) collective-permute-start(f32[64]{0:T(128)S(1)} %get-tuple-element.17), channel_id=1, source_target_pairs={{0,3},{1,0},{2,1},{3,2},{4,7},{5,4},{6,5},{7,6},{8,11},{9,8},{10,9... | collective-permute-start | bytes 776 | tf_op jit(solution)/shard_map/ppermute | solution.py:36
  52.8 0.6 collective-permute-start.7
  53.4 0.0 collective-permute-start.6
  53.5 0.0 copy-done.1
  53.5 20.5 %gather_fusion = s32[2048]{0:T(1024)} fusion(s32[2048]{0:T(1024)S(1)} %copy-done.1, s32[2048]{0:T(1024)S(1)} %broadcast_clamp_fusion), kind=kCustom, calls=%fused_computation | custom fusion | bytes 24576 | tf_op jit(solution)/shard_map/gather | solution.py:275
  74.0 0.0 collective-permute-done.8
  74.0 0.0 collective-permute-done.7
  74.0 0.0 collective-permute-done.6
  74.0 0.9 fusion.4.rows_ref
  74.9 121.8 %shard_map.91 = f32[512,2048]{1,0:T(8,128)} custom-call(s32[1,2048]{1,0:T(1,128)} %bitcast.20, bf16[64,2048]{1,0:T(8,128)(2,1)} %fusion.4.rows_ref, bf16[2048,2048]{1,0:T(8,128)(2,1)} %fusion.1.t_ref), custom_call_target="tpu_custom_call" | custom-call | flops 34359738368 | bytes 29360128 | tf_op jit(solution)/shard_map/pallas_call | solution.py:202
  196.7 4.7 %copy.21 = f32[512,2048]{1,0:T(8,128)} copy(f32[512,2048]{1,0:T(8,128)} %shard_map.91) | data formatting | bytes 8388608
  (7 shorter events, 0.1 us)
Async XLA Ops:
  0.0 14.0 %copy-start = (bf16[1024,128]{1,0:T(8,128)(2,1)S(1)}, bf16[1024,128]{1,0:T(8,128)(2,1)}, u32[]{:S(2)}) copy-start(bf16[1024,128]{1,0:T(8,128)(2,1)} %param.12) | copy-start | bytes 786436
  0.0 9.7 %copy-start.3 = (bf16[1024,128]{1,0:T(8,128)(2,1)S(1)}, bf16[1024,128]{1,0:T(8,128)(2,1)}, u32[]{:S(2)}) copy-start(bf16[1024,128]{1,0:T(8,128)(2,1)} %param.11) | copy-start | bytes 786436
  5.1 8.1 %copy-start.4 = (bf16[128,64]{0,1:T(8,128)(2,1)S(1)}, bf16[128,64]{0,1:T(8,128)(2,1)}, u32[]{:S(2)}) copy-start(bf16[128,64]{0,1:T(8,128)(2,1)} %param.13) | copy-start | bytes 49156
  5.2 15.0 %collective-permute-start.5 = (f32[2048]{0:T(1024)S(1)}, f32[2048]{0:T(1024)S(1)}, u32[]{:S(2)}, u32[]{:S(2)}) collective-permute-start(f32[2048]{0:T(1024)S(1)} %fusion), channel_id=1, source_target_pairs={{0,3},{1,0},{2,1},{3,2},{4,7},{5,4},{6,5},{7,6},{8,11},{9,8},{10,9... | collective-permute-start | bytes 24584 | tf_op jit(solution)/shard_map/ppermute | solution.py:36
  8.5 12.4 %collective-permute-start.4 = (f32[2048]{0:T(1024)S(1)}, f32[2048]{0:T(1024)S(1)}, u32[]{:S(2)}, u32[]{:S(2)}) collective-permute-start(f32[2048]{0:T(1024)S(1)} %fusion), channel_id=1, source_target_pairs={{0,2},{1,3},{2,0},{3,1},{4,6},{5,7},{6,4},{7,5},{8,10},{9,11},{10,... | collective-permute-start | bytes 24584 | tf_op jit(solution)/shard_map/ppermute | solution.py:36
  9.1 11.9 %collective-permute-start.3 = (f32[2048]{0:T(1024)S(1)}, f32[2048]{0:T(1024)S(1)}, u32[]{:S(2)}, u32[]{:S(2)}) collective-permute-start(f32[2048]{0:T(1024)S(1)} %fusion), channel_id=1, source_target_pairs={{0,1},{1,2},{2,3},{3,0},{4,5},{5,6},{6,7},{7,4},{8,9},{9,10},{10,1... | collective-permute-start | bytes 24584 | tf_op jit(solution)/shard_map/ppermute | solution.py:36
  9.7 4.4 %copy-start.2 = (bf16[2048,1024]{1,0:T(8,128)(2,1)S(1)}, bf16[2048,1024]{1,0:T(8,128)(2,1)}, u32[]{:S(2)}) copy-start(bf16[2048,1024]{1,0:T(8,128)(2,1)} %param.9) | copy-start | bytes 12582916
  14.0 5.9 %copy-start.5 = (s32[64]{0:T(128)S(1)}, s32[64]{0:T(128)}, u32[]{:S(2)}) copy-start(s32[64]{0:T(128)} %param.14) | copy-start | bytes 772
  16.7 14.8 %collective-permute-start = (bf16[2048,144]{0,1:T(8,128)(2,1)}, bf16[2048,144]{0,1:T(8,128)(2,1)}, u32[]{:S(2)}, u32[]{:S(2)}) collective-permute-start(bf16[2048,144]{0,1:T(8,128)(2,1)} %get-tuple-element.9), channel_id=1, source_target_pairs={{0,1},{1,2},{2,3},{3,0},{4,5},{5,6},{6,7},{7,4},{8,9},{9,10},{10,1... | collective-permute-start | bytes 1769480 | tf_op jit(solution)/shard_map/ppermute | solution.py:36
  18.2 26.5 %collective-permute-start.1 = (bf16[2048,144]{0,1:T(8,128)(2,1)S(1)}, bf16[2048,144]{0,1:T(8,128)(2,1)}, u32[]{:S(2)}, u32[]{:S(2)}) collective-permute-start(bf16[2048,144]{0,1:T(8,128)(2,1)S(1)} %get-tuple-element.10), channel_id=1, source_target_pairs={{0,2},{1,3},{2,0},{3,1},{4,6},{5,7},{6,4},{7,5},{8,10},{9,11},{10,... | collective-permute-start | bytes 1769480 | tf_op jit(solution)/shard_map/ppermute | solution.py:36
  20.2 25.1 %collective-permute-start.2 = (bf16[2048,144]{0,1:T(8,128)(2,1)S(1)}, bf16[2048,144]{0,1:T(8,128)(2,1)S(1)}, u32[]{:S(2)}, u32[]{:S(2)}) collective-permute-start(bf16[2048,144]{0,1:T(8,128)(2,1)S(1)} %get-tuple-element.11), channel_id=1, source_target_pairs={{0,3},{1,0},{2,1},{3,2},{4,7},{5,4},{6,5},{7,6},{8,11},{9,8},{10,9... | collective-permute-start | bytes 1769480 | tf_op jit(solution)/shard_map/ppermute | solution.py:36
  46.9 6.6 %copy-start.1 = (s32[2048]{0:T(1024)S(1)}, s32[2048]{0:T(1024)}, u32[]{:S(2)}) copy-start(s32[2048]{0:T(1024)} %param.15) | copy-start | bytes 24580
  49.3 24.6 %collective-permute-start.8 = (f32[64]{0:T(128)S(1)}, f32[64]{0:T(128)S(1)}, u32[]{:S(2)}, u32[]{:S(2)}) collective-permute-start(f32[64]{0:T(128)S(1)} %get-tuple-element.17), channel_id=1, source_target_pairs={{0,3},{1,0},{2,1},{3,2},{4,7},{5,4},{6,5},{7,6},{8,11},{9,8},{10,9... | collective-permute-start | bytes 776 | tf_op jit(solution)/shard_map/ppermute | solution.py:36
  52.8 21.2 %collective-permute-start.7 = (f32[64]{0:T(128)S(1)}, f32[64]{0:T(128)S(1)}, u32[]{:S(2)}, u32[]{:S(2)}) collective-permute-start(f32[64]{0:T(128)S(1)} %get-tuple-element.17), channel_id=1, source_target_pairs={{0,2},{1,3},{2,0},{3,1},{4,6},{5,7},{6,4},{7,5},{8,10},{9,11},{10,... | collective-permute-start | bytes 776 | tf_op jit(solution)/shard_map/ppermute | solution.py:36
  53.4 20.5 %collective-permute-start.6 = (f32[64]{0:T(128)S(1)}, f32[64]{0:T(128)S(1)}, u32[]{:S(2)}, u32[]{:S(2)}) collective-permute-start(f32[64]{0:T(128)S(1)} %get-tuple-element.17), channel_id=1, source_target_pairs={{0,1},{1,2},{2,3},{3,0},{4,5},{5,6},{6,7},{7,4},{8,9},{9,10},{10,1... | collective-permute-start | bytes 776 | tf_op jit(solution)/shard_map/ppermute | solution.py:36

commit v12 on v11

--- a/solution.py
+++ b/solution.py
@@ -264,15 +264,19 @@
 def gathered_dest(program_output_index, local):
     y, z, c = wide_coords(lax.axis_index("wide"))
     offset_of_slot = jnp.asarray([SLOT.index(k) for k in range(RING)], jnp.int32)
-    position = jnp.arange(program_output_index.shape[0], dtype=jnp.int32)
-    region, block, row = position // (RING * RING * local), (position // local) % (RING * RING), position % local
+    blocks = program_output_index.shape[0] // local
+    position = jnp.arange(blocks, dtype=jnp.int32)
+    region, block = position // (RING * RING), position % (RING * RING)
     first = offset_of_slot[block % RING]
     second = offset_of_slot[block // RING]
     oc = jnp.where(region == 0, c, 1 - c)
     oz = (z + jnp.where(oc == 0, first, second)) % RING
     oy = (y + jnp.where(oc == 0, second, first)) % RING
-    program = ((oy * RING + oz) * 2 + oc) * local + row
-    return program_output_index[program]
+    owner = (oy * RING + oz) * 2 + oc
+    pick = (owner[:, None] == jnp.arange(blocks, dtype=jnp.int32)[None, :]).astype(jnp.float32)
+    by_owner = program_output_index.reshape(blocks, local).astype(jnp.float32)
+    picked = jnp.dot(pick, by_owner, precision=lax.Precision.HIGHEST)
+    return picked.astype(jnp.int32).reshape(-1)
 
 
 def shards(

time: 202 us -> 183 us (0.906)
  local copies, waits for them, and re-layouts: 25.8 us -> 6.12 us
  waiting for transfers between devices: 16.4 us -> 19.1 us
    gather x1 -> x0, local copies, waits for them, and re-layouts: 20.5 us -> none  [gathered_dest(): return program_output_index[program]]
    ppermute x9, waiting for transfers between devices: 16.4 us -> 19.1 us  [narrow_sum(): total = total + lax.ppermute(piece, 'narrow', perm).astype(jnp.float32)]
  transfers between devices with their start and end apart: 9 -> 9, of which waited for: 3 -> 5; matrix products, arithmetic and copies ran while one was open for 18% -> 9% of each run, Pallas kernels for 0% -> 0%
where the time goes in v12:
time: 183 us
  Pallas kernels  121 us (66%)
  waiting for transfers between devices  19.1 us (10%)
  other arithmetic  16.8 us (9%)
  starting transfers between devices  12.6 us (7%)
  matrix products  7.79 us (4%)
  local copies, waits for them, and re-layouts  6.12 us (3%)
    pallas_call x1, Pallas kernels, ring_scores(): pl.pallas_call(functools.partial(ring_kernel, count, root), out_shape=jax...  121 us
    ppermute x9, waiting for transfers between devices, narrow_sum(): total = total + lax.ppermute(piece, 'narrow', perm).astype(jnp.float32)  19.1 us
    ppermute x9, starting transfers between devices, narrow_sum(): total = total + lax.ppermute(piece, 'narrow', perm).astype(jnp.float32)  12.6 us
    convert_element_type x2, other arithmetic, normalize_rows(): (features * lax.rsqrt(squares + epsilon)[:, None]).astype(jnp.bfloat16)  8.91 us
    reduce_sum x1, other arithmetic, shards(): target_squares = jnp.sum(target_wide * target_wide, axis=1)  5.14 us
    unnamed x13, local copies, waits for them, and re-layouts  4.73 us
  transfers between devices with their start and end apart: 9, of which 5 were waited for; matrix products, arithmetic and copies ran while one was open for 9% of the time, Pallas kernels for 0%

profile of v12, /device:TPU:1, one launch (start us, length us, event | category | flops | bytes accessed | tf_op | source)
XLA Modules:
  0.0 183.2 jit_solution(11043200706285851253)
XLA Ops:
  0.0 0.0 copy-start
  0.0 0.0 copy-start.2
  0.0 5.1 %fusion = f32[2048]{0:T(1024)S(1)} fusion(bf16[2048,2048]{1,0:T(8,128)(2,1)} %param.16), kind=kLoop, calls=%fused_computation.2 | loop fusion | flops 12580864 | bytes 8396800 | tf_op jit(solution)/shard_map/reduce_sum | solution.py:298
  5.1 0.0 copy-start.3
  5.2 3.4 %collective-permute-start.5 = (f32[2048]{0:T(1024)S(1)}, f32[2048]{0:T(1024)S(1)}, u32[]{:S(2)}, u32[]{:S(2)}) collective-permute-start(f32[2048]{0:T(1024)S(1)} %fusion), channel_id=1, source_target_pairs={{0,3},{1,0},{2,1},{3,2},{4,7},{5,4},{6,5},{7,6},{8,11},{9,8},{10,9... | collective-permute-start | bytes 24584 | tf_op jit(solution)/shard_map/ppermute | solution.py:36
  8.5 0.5 collective-permute-start.4
  9.1 0.6 collective-permute-start.3
  9.7 0.0 copy-done.2
  9.7 0.0 copy-start.1
  9.7 3.6 %fusion.18 = f32[2048,128]{1,0:T(8,128)S(1)} fusion(bf16[2048,1024]{1,0:T(8,128)(2,1)} %param.10, bf16[1024,128]{1,0:T(8,128)(2,1)S(1)} %copy-done.2), kind=kOutput, calls=%fused_computation.64 | convolution fusion | flops 536870912 | bytes 5505024 | tf_op jit(solution)/shard_map/dot_general | solution.py:304
  13.3 0.0 copy-done.3
  13.3 0.7 fusion.19
  14.0 0.0 copy-done
  14.0 0.0 copy-done.1
  14.0 0.0 copy-start.5
  14.1 0.0 copy-start.4
  14.1 1.5 fusion.17
  15.6 1.0 pad_maximum_fusion
  16.7 1.5 collective-permute-start
  18.2 1.7 collective-permute-start.1
  19.9 0.0 copy-done.5
  19.9 0.1 fusion.7
  20.1 0.0 copy-done.4
  20.1 0.1 convert_element_type.40
  20.1 0.0 collective-permute-done.5
  20.2 0.7 collective-permute-start.2
  20.8 0.0 collective-permute-done.4
  20.9 0.0 collective-permute-done.3
  20.9 8.0 %fusion.1.t_ref = bf16[2048,2048]{1,0:T(8,128)(2,1)} fusion(bf16[2048,2048]{1,0:T(8,128)(2,1)} %param.16, f32[2048]{0:T(1024)S(1)} %add_rsqrt_fusion), kind=kLoop, calls=%fused_computation.3 | loop fusion | flops 12582912 | bytes 16785408 | tf_op jit(solution)/shard_map/convert_element_type | solution.py:28
  28.9 2.6 %collective-permute-done = bf16[2048,144]{0,1:T(8,128)(2,1)} collective-permute-done((bf16[2048,144]{0,1:T(8,128)(2,1)}, bf16[2048,144]{0,1:T(8,128)(2,1)}, u32[]{:S(2)}, u32[]{:S(2)}) %collective-permute-start) | collective-permute-done | bytes 589856 | tf_op jit(solution)/shard_map/ppermute | solution.py:36
  31.5 13.2 %collective-permute-done.1 = bf16[2048,144]{0,1:T(8,128)(2,1)} collective-permute-done((bf16[2048,144]{0,1:T(8,128)(2,1)S(1)}, bf16[2048,144]{0,1:T(8,128)(2,1)}, u32[]{:S(2)}, u32[]{:S(2)}) %collective-permute-start.1) | collective-permute-done | bytes 589856 | tf_op jit(solution)/shard_map/ppermute | solution.py:36
  44.7 0.6 collective-permute-done.2
  45.3 1.5 fusion.3
  46.9 0.1 slice.7
  47.0 0.3 copy.12
  47.3 0.2 reshape.188
  47.6 1.7 multiply_reduce_fusion
  49.3 3.5 %collective-permute-start.8 = (f32[64]{0:T(128)S(1)}, f32[64]{0:T(128)S(1)}, u32[]{:S(2)}, u32[]{:S(2)}) collective-permute-start(f32[64]{0:T(128)S(1)} %get-tuple-element.17), channel_id=1, source_target_pairs={{0,3},{1,0},{2,1},{3,2},{4,7},{5,4},{6,5},{7,6},{8,11},{9,8},{10,9... | collective-permute-start | bytes 776 | tf_op jit(solution)/shard_map/ppermute | solution.py:36
  52.8 0.6 collective-permute-start.7
  53.4 0.0 collective-permute-start.6
  53.4 0.2 convolution_convert_fusion
  53.6 0.7 reshape_reshape.3.dest_ref
  54.3 0.0 collective-permute-done.8
  54.3 2.3 %collective-permute-done.7 = f32[64]{0:T(128)S(1)} collective-permute-done((f32[64]{0:T(128)S(1)}, f32[64]{0:T(128)S(1)}, u32[]{:S(2)}, u32[]{:S(2)}) %collective-permute-start.7) | collective-permute-done | bytes 288 | tf_op jit(solution)/shard_map/ppermute | solution.py:36
  56.7 0.3 collective-permute-done.6
  57.0 0.9 fusion.4.rows_ref
  57.9 120.6 %shard_map.91 = f32[512,2048]{1,0:T(8,128)} custom-call(s32[1,2048]{1,0:T(1,128)} %reshape_reshape.3.dest_ref, bf16[64,2048]{1,0:T(8,128)(2,1)} %fusion.4.rows_ref, bf16[2048,2048]{1,0:T(8,128)(2,1)} %fusion.1.t_ref), custom_call_target="tpu_custom_call" | custom-call | flops 34359738368 | bytes 29360128 | tf_op jit(solution)/shard_map/pallas_call | solution.py:202
  178.5 4.7 %copy.21 = f32[512,2048]{1,0:T(8,128)} copy(f32[512,2048]{1,0:T(8,128)} %shard_map.91) | data formatting | bytes 8388608
  (8 shorter events, 0.1 us)
Async XLA Ops:
  0.0 14.0 %copy-start = (bf16[1024,128]{1,0:T(8,128)(2,1)S(1)}, bf16[1024,128]{1,0:T(8,128)(2,1)}, u32[]{:S(2)}) copy-start(bf16[1024,128]{1,0:T(8,128)(2,1)} %param.12) | copy-start | bytes 786436
  0.0 9.7 %copy-start.2 = (bf16[1024,128]{1,0:T(8,128)(2,1)S(1)}, bf16[1024,128]{1,0:T(8,128)(2,1)}, u32[]{:S(2)}) copy-start(bf16[1024,128]{1,0:T(8,128)(2,1)} %param.11) | copy-start | bytes 786436
  5.1 8.1 %copy-start.3 = (bf16[128,64]{0,1:T(8,128)(2,1)S(1)}, bf16[128,64]{0,1:T(8,128)(2,1)}, u32[]{:S(2)}) copy-start(bf16[128,64]{0,1:T(8,128)(2,1)} %param.13) | copy-start | bytes 49156
  5.2 15.0 %collective-permute-start.5 = (f32[2048]{0:T(1024)S(1)}, f32[2048]{0:T(1024)S(1)}, u32[]{:S(2)}, u32[]{:S(2)}) collective-permute-start(f32[2048]{0:T(1024)S(1)} %fusion), channel_id=1, source_target_pairs={{0,3},{1,0},{2,1},{3,2},{4,7},{5,4},{6,5},{7,6},{8,11},{9,8},{10,9... | collective-permute-start | bytes 24584 | tf_op jit(solution)/shard_map/ppermute | solution.py:36
  8.5 12.3 %collective-permute-start.4 = (f32[2048]{0:T(1024)S(1)}, f32[2048]{0:T(1024)S(1)}, u32[]{:S(2)}, u32[]{:S(2)}) collective-permute-start(f32[2048]{0:T(1024)S(1)} %fusion), channel_id=1, source_target_pairs={{0,2},{1,3},{2,0},{3,1},{4,6},{5,7},{6,4},{7,5},{8,10},{9,11},{10,... | collective-permute-start | bytes 24584 | tf_op jit(solution)/shard_map/ppermute | solution.py:36
  9.1 11.8 %collective-permute-start.3 = (f32[2048]{0:T(1024)S(1)}, f32[2048]{0:T(1024)S(1)}, u32[]{:S(2)}, u32[]{:S(2)}) collective-permute-start(f32[2048]{0:T(1024)S(1)} %fusion), channel_id=1, source_target_pairs={{0,1},{1,2},{2,3},{3,0},{4,5},{5,6},{6,7},{7,4},{8,9},{9,10},{10,1... | collective-permute-start | bytes 24584 | tf_op jit(solution)/shard_map/ppermute | solution.py:36
  9.7 4.4 %copy-start.1 = (bf16[2048,1024]{1,0:T(8,128)(2,1)S(1)}, bf16[2048,1024]{1,0:T(8,128)(2,1)}, u32[]{:S(2)}) copy-start(bf16[2048,1024]{1,0:T(8,128)(2,1)} %param.9) | copy-start | bytes 12582916
  14.0 5.9 %copy-start.5 = (s32[64]{0:T(128)S(1)}, s32[64]{0:T(128)}, u32[]{:S(2)}) copy-start(s32[64]{0:T(128)} %param.14) | copy-start | bytes 772
  14.1 6.0 %copy-start.4 = (s32[2048]{0:T(1024)S(1)}, s32[2048]{0:T(1024)}, u32[]{:S(2)}) copy-start(s32[2048]{0:T(1024)} %param.15) | copy-start | bytes 24580
  16.7 14.8 %collective-permute-start = (bf16[2048,144]{0,1:T(8,128)(2,1)}, bf16[2048,144]{0,1:T(8,128)(2,1)}, u32[]{:S(2)}, u32[]{:S(2)}) collective-permute-start(bf16[2048,144]{0,1:T(8,128)(2,1)} %get-tuple-element.9), channel_id=1, source_target_pairs={{0,1},{1,2},{2,3},{3,0},{4,5},{5,6},{6,7},{7,4},{8,9},{9,10},{10,1... | collective-permute-start | bytes 1769480 | tf_op jit(solution)/shard_map/ppermute | solution.py:36
  18.2 26.5 %collective-permute-start.1 = (bf16[2048,144]{0,1:T(8,128)(2,1)S(1)}, bf16[2048,144]{0,1:T(8,128)(2,1)}, u32[]{:S(2)}, u32[]{:S(2)}) collective-permute-start(bf16[2048,144]{0,1:T(8,128)(2,1)S(1)} %get-tuple-element.10), channel_id=1, source_target_pairs={{0,2},{1,3},{2,0},{3,1},{4,6},{5,7},{6,4},{7,5},{8,10},{9,11},{10,... | collective-permute-start | bytes 1769480 | tf_op jit(solution)/shard_map/ppermute | solution.py:36
  20.2 25.2 %collective-permute-start.2 = (bf16[2048,144]{0,1:T(8,128)(2,1)S(1)}, bf16[2048,144]{0,1:T(8,128)(2,1)S(1)}, u32[]{:S(2)}, u32[]{:S(2)}) collective-permute-start(bf16[2048,144]{0,1:T(8,128)(2,1)S(1)} %get-tuple-element.11), channel_id=1, source_target_pairs={{0,3},{1,0},{2,1},{3,2},{4,7},{5,4},{6,5},{7,6},{8,11},{9,8},{10,9... | collective-permute-start | bytes 1769480 | tf_op jit(solution)/shard_map/ppermute | solution.py:36
  49.3 5.0 %collective-permute-start.8 = (f32[64]{0:T(128)S(1)}, f32[64]{0:T(128)S(1)}, u32[]{:S(2)}, u32[]{:S(2)}) collective-permute-start(f32[64]{0:T(128)S(1)} %get-tuple-element.17), channel_id=1, source_target_pairs={{0,3},{1,0},{2,1},{3,2},{4,7},{5,4},{6,5},{7,6},{8,11},{9,8},{10,9... | collective-permute-start | bytes 776 | tf_op jit(solution)/shard_map/ppermute | solution.py:36
  52.8 3.9 %collective-permute-start.7 = (f32[64]{0:T(128)S(1)}, f32[64]{0:T(128)S(1)}, u32[]{:S(2)}, u32[]{:S(2)}) collective-permute-start(f32[64]{0:T(128)S(1)} %get-tuple-element.17), channel_id=1, source_target_pairs={{0,2},{1,3},{2,0},{3,1},{4,6},{5,7},{6,4},{7,5},{8,10},{9,11},{10,... | collective-permute-start | bytes 776 | tf_op jit(solution)/shard_map/ppermute | solution.py:36
  53.4 3.6 %collective-permute-start.6 = (f32[64]{0:T(128)S(1)}, f32[64]{0:T(128)S(1)}, u32[]{:S(2)}, u32[]{:S(2)}) collective-permute-start(f32[64]{0:T(128)S(1)} %get-tuple-element.17), channel_id=1, source_target_pairs={{0,1},{1,2},{2,3},{3,0},{4,5},{5,6},{6,7},{7,4},{8,9},{9,10},{10,1... | collective-permute-start | bytes 776 | tf_op jit(solution)/shard_map/ppermute | solution.py:36

commit v13 on v12

--- a/solution.py
+++ b/solution.py
@@ -11,7 +11,7 @@
 MESH = pl.DeviceIdType.MESH
 
 epsilon = 1e-06
-TILE = 128
+TILE = 64
 
 
 def program_features(out_side, in_side, lengths, length):

time: 183 us -> 249 us (1.36)
  Pallas kernels: 121 us -> 187 us
    pallas_call x1, Pallas kernels: 121 us -> 187 us  [ring_scores(): pl.pallas_call(functools.partial(ring_kernel, count, root), out_shape=jax...]
  transfers between devices with their start and end apart: 9 -> 9, of which waited for: 5 -> 5; matrix products, arithmetic and copies ran while one was open for 9% -> 6% of each run, Pallas kernels for 0% -> 0%
where the time goes in v13:
time: 249 us
  Pallas kernels  187 us (75%)
  waiting for transfers between devices  19.1 us (8%)
  other arithmetic  16.8 us (7%)
  starting transfers between devices  12.6 us (5%)
  matrix products  7.79 us (3%)
  local copies, waits for them, and re-layouts  6.12 us (2%)
    pallas_call x1, Pallas kernels, ring_scores(): pl.pallas_call(functools.partial(ring_kernel, count, root), out_shape=jax...  187 us
    ppermute x9, waiting for transfers between devices, narrow_sum(): total = total + lax.ppermute(piece, 'narrow', perm).astype(jnp.float32)  19.1 us
    ppermute x9, starting transfers between devices, narrow_sum(): total = total + lax.ppermute(piece, 'narrow', perm).astype(jnp.float32)  12.6 us
    convert_element_type x2, other arithmetic, normalize_rows(): (features * lax.rsqrt(squares + epsilon)[:, None]).astype(jnp.bfloat16)  8.91 us
    reduce_sum x1, other arithmetic, shards(): target_squares = jnp.sum(target_wide * target_wide, axis=1)  5.14 us
  transfers between devices with their start and end apart: 9, of which 5 were waited for; matrix products, arithmetic and copies ran while one was open for 6% of the time, Pallas kernels for 0%

profile of v13, /device:TPU:1, one launch (start us, length us, event | category | flops | bytes accessed | tf_op | source)
XLA Modules:
  0.0 249.1 jit_solution(8002968648227469832)
XLA Ops:
  0.0 0.0 copy-start
  0.0 0.0 copy-start.2
  0.0 5.1 %fusion = f32[2048]{0:T(1024)S(1)} fusion(bf16[2048,2048]{1,0:T(8,128)(2,1)} %param.16), kind=kLoop, calls=%fused_computation.2 | loop fusion | flops 12580864 | bytes 8396800 | tf_op jit(solution)/shard_map/reduce_sum | solution.py:298
  5.1 0.0 copy-start.3
  5.2 3.4 %collective-permute-start.5 = (f32[2048]{0:T(1024)S(1)}, f32[2048]{0:T(1024)S(1)}, u32[]{:S(2)}, u32[]{:S(2)}) collective-permute-start(f32[2048]{0:T(1024)S(1)} %fusion), channel_id=1, source_target_pairs={{0,3},{1,0},{2,1},{3,2},{4,7},{5,4},{6,5},{7,6},{8,11},{9,8},{10,9... | collective-permute-start | bytes 24584 | tf_op jit(solution)/shard_map/ppermute | solution.py:36
  8.5 0.5 collective-permute-start.4
  9.1 0.6 collective-permute-start.3
  9.7 0.0 copy-done.2
  9.7 0.0 copy-start.1
  9.7 3.6 %fusion.18 = f32[2048,128]{1,0:T(8,128)S(1)} fusion(bf16[2048,1024]{1,0:T(8,128)(2,1)} %param.10, bf16[1024,128]{1,0:T(8,128)(2,1)S(1)} %copy-done.2), kind=kOutput, calls=%fused_computation.64 | convolution fusion | flops 536870912 | bytes 5505024 | tf_op jit(solution)/shard_map/dot_general | solution.py:304
  13.3 0.0 copy-done.3
  13.3 0.7 fusion.19
  14.0 0.0 copy-done
  14.0 0.0 copy-done.1
  14.0 0.0 copy-start.5
  14.1 0.0 copy-start.4
  14.1 1.5 fusion.17
  15.6 1.0 pad_maximum_fusion
  16.7 1.5 collective-permute-start
  18.2 1.7 collective-permute-start.1
  19.9 0.0 copy-done.5
  19.9 0.1 fusion.7
  20.1 0.0 copy-done.4
  20.1 0.1 convert_element_type.40
  20.1 0.0 collective-permute-done.5
  20.2 0.7 collective-permute-start.2
  20.8 0.0 collective-permute-done.4
  20.9 0.0 collective-permute-done.3
  20.9 8.0 %fusion.1.t_ref = bf16[2048,2048]{1,0:T(8,128)(2,1)} fusion(bf16[2048,2048]{1,0:T(8,128)(2,1)} %param.16, f32[2048]{0:T(1024)S(1)} %add_rsqrt_fusion), kind=kLoop, calls=%fused_computation.3 | loop fusion | flops 12582912 | bytes 16785408 | tf_op jit(solution)/shard_map/convert_element_type | solution.py:28
  28.9 2.6 %collective-permute-done = bf16[2048,144]{0,1:T(8,128)(2,1)} collective-permute-done((bf16[2048,144]{0,1:T(8,128)(2,1)}, bf16[2048,144]{0,1:T(8,128)(2,1)}, u32[]{:S(2)}, u32[]{:S(2)}) %collective-permute-start) | collective-permute-done | bytes 589856 | tf_op jit(solution)/shard_map/ppermute | solution.py:36
  31.5 13.2 %collective-permute-done.1 = bf16[2048,144]{0,1:T(8,128)(2,1)} collective-permute-done((bf16[2048,144]{0,1:T(8,128)(2,1)S(1)}, bf16[2048,144]{0,1:T(8,128)(2,1)}, u32[]{:S(2)}, u32[]{:S(2)}) %collective-permute-start.1) | collective-permute-done | bytes 589856 | tf_op jit(solution)/shard_map/ppermute | solution.py:36
  44.7 0.6 collective-permute-done.2
  45.3 1.5 fusion.3
  46.9 0.1 slice.7
  47.0 0.3 copy.12
  47.3 0.2 reshape.188
  47.6 1.7 multiply_reduce_fusion
  49.3 3.5 %collective-permute-start.8 = (f32[64]{0:T(128)S(1)}, f32[64]{0:T(128)S(1)}, u32[]{:S(2)}, u32[]{:S(2)}) collective-permute-start(f32[64]{0:T(128)S(1)} %get-tuple-element.17), channel_id=1, source_target_pairs={{0,3},{1,0},{2,1},{3,2},{4,7},{5,4},{6,5},{7,6},{8,11},{9,8},{10,9... | collective-permute-start | bytes 776 | tf_op jit(solution)/shard_map/ppermute | solution.py:36
  52.8 0.6 collective-permute-start.7
  53.4 0.0 collective-permute-start.6
  53.4 0.2 convolution_convert_fusion
  53.6 0.7 reshape_reshape.3.dest_ref
  54.3 0.0 collective-permute-done.8
  54.3 2.3 collective-permute-done.7
  56.7 0.3 collective-permute-done.6
  57.0 0.9 fusion.4.rows_ref
  57.9 186.5 %shard_map.91 = f32[512,2048]{1,0:T(8,128)} custom-call(s32[1,2048]{1,0:T(1,128)} %reshape_reshape.3.dest_ref, bf16[64,2048]{1,0:T(8,128)(2,1)} %fusion.4.rows_ref, bf16[2048,2048]{1,0:T(8,128)(2,1)} %fusion.1.t_ref), custom_call_target="tpu_custom_call" | custom-call | flops 34359738368 | bytes 29360128 | tf_op jit(solution)/shard_map/pallas_call | solution.py:202
  244.4 4.7 %copy.21 = f32[512,2048]{1,0:T(8,128)} copy(f32[512,2048]{1,0:T(8,128)} %shard_map.91) | data formatting | bytes 8388608
  (8 shorter events, 0.1 us)
Async XLA Ops:
  0.0 14.0 %copy-start = (bf16[1024,128]{1,0:T(8,128)(2,1)S(1)}, bf16[1024,128]{1,0:T(8,128)(2,1)}, u32[]{:S(2)}) copy-start(bf16[1024,128]{1,0:T(8,128)(2,1)} %param.12) | copy-start | bytes 786436
  0.0 9.7 %copy-start.2 = (bf16[1024,128]{1,0:T(8,128)(2,1)S(1)}, bf16[1024,128]{1,0:T(8,128)(2,1)}, u32[]{:S(2)}) copy-start(bf16[1024,128]{1,0:T(8,128)(2,1)} %param.11) | copy-start | bytes 786436
  5.1 8.1 %copy-start.3 = (bf16[128,64]{0,1:T(8,128)(2,1)S(1)}, bf16[128,64]{0,1:T(8,128)(2,1)}, u32[]{:S(2)}) copy-start(bf16[128,64]{0,1:T(8,128)(2,1)} %param.13) | copy-start | bytes 49156
  5.2 15.0 %collective-permute-start.5 = (f32[2048]{0:T(1024)S(1)}, f32[2048]{0:T(1024)S(1)}, u32[]{:S(2)}, u32[]{:S(2)}) collective-permute-start(f32[2048]{0:T(1024)S(1)} %fusion), channel_id=1, source_target_pairs={{0,3},{1,0},{2,1},{3,2},{4,7},{5,4},{6,5},{7,6},{8,11},{9,8},{10,9... | collective-permute-start | bytes 24584 | tf_op jit(solution)/shard_map/ppermute | solution.py:36
  8.5 12.3 %collective-permute-start.4 = (f32[2048]{0:T(1024)S(1)}, f32[2048]{0:T(1024)S(1)}, u32[]{:S(2)}, u32[]{:S(2)}) collective-permute-start(f32[2048]{0:T(1024)S(1)} %fusion), channel_id=1, source_target_pairs={{0,2},{1,3},{2,0},{3,1},{4,6},{5,7},{6,4},{7,5},{8,10},{9,11},{10,... | collective-permute-start | bytes 24584 | tf_op jit(solution)/shard_map/ppermute | solution.py:36
  9.1 11.8 %collective-permute-start.3 = (f32[2048]{0:T(1024)S(1)}, f32[2048]{0:T(1024)S(1)}, u32[]{:S(2)}, u32[]{:S(2)}) collective-permute-start(f32[2048]{0:T(1024)S(1)} %fusion), channel_id=1, source_target_pairs={{0,1},{1,2},{2,3},{3,0},{4,5},{5,6},{6,7},{7,4},{8,9},{9,10},{10,1... | collective-permute-start | bytes 24584 | tf_op jit(solution)/shard_map/ppermute | solution.py:36
  9.7 4.4 %copy-start.1 = (bf16[2048,1024]{1,0:T(8,128)(2,1)S(1)}, bf16[2048,1024]{1,0:T(8,128)(2,1)}, u32[]{:S(2)}) copy-start(bf16[2048,1024]{1,0:T(8,128)(2,1)} %param.9) | copy-start | bytes 12582916
  14.0 5.9 %copy-start.5 = (s32[64]{0:T(128)S(1)}, s32[64]{0:T(128)}, u32[]{:S(2)}) copy-start(s32[64]{0:T(128)} %param.14) | copy-start | bytes 772
  14.1 6.0 %copy-start.4 = (s32[2048]{0:T(1024)S(1)}, s32[2048]{0:T(1024)}, u32[]{:S(2)}) copy-start(s32[2048]{0:T(1024)} %param.15) | copy-start | bytes 24580
  16.7 14.8 %collective-permute-start = (bf16[2048,144]{0,1:T(8,128)(2,1)}, bf16[2048,144]{0,1:T(8,128)(2,1)}, u32[]{:S(2)}, u32[]{:S(2)}) collective-permute-start(bf16[2048,144]{0,1:T(8,128)(2,1)} %get-tuple-element.9), channel_id=1, source_target_pairs={{0,1},{1,2},{2,3},{3,0},{4,5},{5,6},{6,7},{7,4},{8,9},{9,10},{10,1... | collective-permute-start | bytes 1769480 | tf_op jit(solution)/shard_map/ppermute | solution.py:36
  18.2 26.5 %collective-permute-start.1 = (bf16[2048,144]{0,1:T(8,128)(2,1)S(1)}, bf16[2048,144]{0,1:T(8,128)(2,1)}, u32[]{:S(2)}, u32[]{:S(2)}) collective-permute-start(bf16[2048,144]{0,1:T(8,128)(2,1)S(1)} %get-tuple-element.10), channel_id=1, source_target_pairs={{0,2},{1,3},{2,0},{3,1},{4,6},{5,7},{6,4},{7,5},{8,10},{9,11},{10,... | collective-permute-start | bytes 1769480 | tf_op jit(solution)/shard_map/ppermute | solution.py:36
  20.2 25.2 %collective-permute-start.2 = (bf16[2048,144]{0,1:T(8,128)(2,1)S(1)}, bf16[2048,144]{0,1:T(8,128)(2,1)S(1)}, u32[]{:S(2)}, u32[]{:S(2)}) collective-permute-start(bf16[2048,144]{0,1:T(8,128)(2,1)S(1)} %get-tuple-element.11), channel_id=1, source_target_pairs={{0,3},{1,0},{2,1},{3,2},{4,7},{5,4},{6,5},{7,6},{8,11},{9,8},{10,9... | collective-permute-start | bytes 1769480 | tf_op jit(solution)/shard_map/ppermute | solution.py:36
  49.3 5.0 %collective-permute-start.8 = (f32[64]{0:T(128)S(1)}, f32[64]{0:T(128)S(1)}, u32[]{:S(2)}, u32[]{:S(2)}) collective-permute-start(f32[64]{0:T(128)S(1)} %get-tuple-element.17), channel_id=1, source_target_pairs={{0,3},{1,0},{2,1},{3,2},{4,7},{5,4},{6,5},{7,6},{8,11},{9,8},{10,9... | collective-permute-start | bytes 776 | tf_op jit(solution)/shard_map/ppermute | solution.py:36
  52.8 3.9 %collective-permute-start.7 = (f32[64]{0:T(128)S(1)}, f32[64]{0:T(128)S(1)}, u32[]{:S(2)}, u32[]{:S(2)}) collective-permute-start(f32[64]{0:T(128)S(1)} %get-tuple-element.17), channel_id=1, source_target_pairs={{0,2},{1,3},{2,0},{3,1},{4,6},{5,7},{6,4},{7,5},{8,10},{9,11},{10,... | collective-permute-start | bytes 776 | tf_op jit(solution)/shard_map/ppermute | solution.py:36
  53.4 3.6 %collective-permute-start.6 = (f32[64]{0:T(128)S(1)}, f32[64]{0:T(128)S(1)}, u32[]{:S(2)}, u32[]{:S(2)}) collective-permute-start(f32[64]{0:T(128)S(1)} %get-tuple-element.17), channel_id=1, source_target_pairs={{0,1},{1,2},{2,3},{3,0},{4,5},{5,6},{6,7},{7,4},{8,9},{9,10},{10,1... | collective-permute-start | bytes 776 | tf_op jit(solution)/shard_map/ppermute | solution.py:36

commit v14 on v10

--- a/solution.py
+++ b/solution.py
@@ -37,14 +37,15 @@
     return total
 
 
-def ring_kernel(count, root, place_ref, rows_ref, t_ref, out_ref, gathered,
-                ordered, send_buf, recv_buf, acc, send_sem, recv_sem, wide_send, wide_recv):
+def ring_kernel(count, root, place_ref, feat_ref, t_ref, out_ref, gathered,
+                ordered, send_buf, recv_buf, acc, send_sem, recv_sem, wide_send, wide_recv,
+                rows_ref, sq_send, sq_recv, sq_send_sem, sq_recv_sem):
     me = lax.axis_index("narrow")
     right, left = lax.rem(me + 1, count), lax.rem(me + count - 1, count)
     rows = out_ref.shape[0]
     half = t_ref.shape[0] // 2
     tiles = rows // TILE
-    local = rows_ref.shape[0]
+    local = feat_ref.shape[0]
     everyone = gathered.shape[0]
 
     wide = lax.axis_index("wide")
@@ -59,12 +60,35 @@
     partner = {"wide": wide + 1 - 2 * core}
     peers = [wide_peer(True, 1), wide_peer(True, -1), wide_peer(False, 1), wide_peer(False, -1), partner]
 
+    narrow_peers = [lax.rem(me + shift, count) for shift in range(1, count)]
     barrier = pltpu.get_barrier_semaphore()
-    for neighbour in (left, right):
+    for neighbour in narrow_peers:
         pl.semaphore_signal(barrier, inc=1, device_id={"narrow": neighbour}, device_id_type=MESH)
     for peer in peers:
         pl.semaphore_signal(barrier, inc=1, device_id=peer, device_id_type=MESH)
-    pl.semaphore_wait(barrier, 2 + len(peers))
+    pl.semaphore_wait(barrier, len(narrow_peers) + len(peers))
+
+    features = feat_ref[...]
+    sq_send[...] = jnp.broadcast_to(jnp.sum(features * features, axis=1, keepdims=True), sq_send.shape)
+    squares_in = []
+    for shift in range(1, count):
+        squares_in.append(pltpu.make_async_remote_copy(
+            src_ref=sq_send,
+            dst_ref=sq_recv.at[shift - 1],
+            send_sem=sq_send_sem.at[shift - 1],
+            recv_sem=sq_recv_sem.at[shift - 1],
+            device_id={"narrow": narrow_peers[shift - 1]},
+            device_id_type=MESH,
+        ))
+        squares_in[-1].start()
+    for copy in squares_in:
+        copy.wait_recv()
+    squares = sq_send[:, 0:1]
+    for shift in range(1, count):
+        squares = squares + sq_recv[shift - 1, :, 0:1]
+    rows_ref[...] = (features * lax.rsqrt(squares + epsilon)).astype(jnp.bfloat16)
+    for copy in squares_in:
+        copy.wait_send()
 
     def wide_copy(index, src, dst_start, size, peer):
         return pltpu.make_async_remote_copy(
@@ -194,9 +218,9 @@
         copy.wait_send()
 
 
-def ring_scores(place, unit_rows, target_unit, count, root):
+def ring_scores(place, features, target_unit, count, root):
     programs = place.shape[0]
-    depth = unit_rows.shape[1]
+    local, depth = features.shape
     rows = programs // count
     targets = target_unit.shape[0]
     half = targets // 2
@@ -215,6 +239,11 @@
             pltpu.SemaphoreType.DMA((2, count - 1, rows // TILE)),
             pltpu.SemaphoreType.DMA((12,)),
             pltpu.SemaphoreType.DMA((12,)),
+            pltpu.VMEM((local, depth), jnp.bfloat16),
+            pltpu.VMEM((local, 128), jnp.float32),
+            pltpu.VMEM((count - 1, local, 128), jnp.float32),
+            pltpu.SemaphoreType.DMA((count - 1,)),
+            pltpu.SemaphoreType.DMA((count - 1,)),
         ],
         compiler_params=pltpu.CompilerParams(
             collective_id=0, has_side_effects=True, vmem_limit_bytes=62 * 1024 * 1024
@@ -224,7 +253,7 @@
             bytes_accessed=2 * (2 * programs + targets) * depth + 4 * rows * targets,
             transcendentals=0,
         ),
-    )(place.reshape(programs, 1), unit_rows, target_unit)
+    )(place.reshape(programs, 1), features, target_unit)
 
 
 RING = 4
@@ -321,12 +350,9 @@
     quarter = summed_parts[:, :quarter_cols]
     in_all = summed_parts[:, quarter_cols:]
     features = program_features(quarter, in_all, lengths, length)
-    squares = jnp.sum(features * features, axis=1)
-    squares = narrow_sum(squares, lambda dest: squares, narrow_count, narrow_index, jnp.float32)
-    unit_rows = normalize_rows(features, squares)
     root_count = math.sqrt(float(targets.shape[1] * narrow_count))
-    place = gathered_place(row_order, unit_rows.shape[0])
-    return ring_scores(place, unit_rows, target_unit, narrow_count, root_count)
+    place = gathered_place(row_order, features.shape[0])
+    return ring_scores(place, features, target_unit, narrow_count, root_count)
 
 
 def solution(mesh):

time: 184 us -> 182 us (0.989)
  Pallas kernels: 121 us -> 127 us
  starting transfers between devices: 13.2 us -> 8.67 us
  waiting for transfers between devices: 10 us -> 7.59 us
    pallas_call x1, Pallas kernels: 121 us -> 127 us  [ring_scores(): pl.pallas_call(functools.partial(ring_kernel, count, root), out_shape=jax...]
    ppermute x9 -> x6, starting transfers between devices: 13.2 us -> 8.67 us  [narrow_sum(): total = total + lax.ppermute(piece, 'narrow', perm).astype(jnp.float32)]
    ppermute x9 -> x6, waiting for transfers between devices: 10 us -> 7.59 us  [narrow_sum(): total = total + lax.ppermute(piece, 'narrow', perm).astype(jnp.float32)]
    unnamed x13 -> x14, local copies, waits for them, and re-layouts: 4.73 us -> 5.7 us
    convert_element_type x2 -> x1, other arithmetic: 8.91 us -> 8.02 us  [normalize_rows(): (features * lax.rsqrt(squares + epsilon)[:, None]).astype(jnp.bfloat16)]
  transfers between devices with their start and end apart: 9 -> 6, of which waited for: 4 -> 1; matrix products, arithmetic and copies ran while one was open for 13% -> 13% of each run, Pallas kernels for 0% -> 0%
where the time goes in v14:
time: 182 us
  Pallas kernels  127 us (70%)
  other arithmetic  15.9 us (9%)
  local copies, waits for them, and re-layouts  15.7 us (9%)
  starting transfers between devices  8.67 us (5%)
  waiting for transfers between devices  7.59 us (4%)
  matrix products  7.18 us (4%)
    pallas_call x1, Pallas kernels, ring_scores(): pl.pallas_call(functools.partial(ring_kernel, count, root), out_shape=jax...  127 us
    ppermute x6, starting transfers between devices, narrow_sum(): total = total + lax.ppermute(piece, 'narrow', perm).astype(jnp.float32)  8.67 us
    scatter x1, local copies, waits for them, and re-layouts, shards(): jnp.zeros_like(program_output_index).at[program_output_index]  8.05 us
    convert_element_type x1, other arithmetic, normalize_rows(): (features * lax.rsqrt(squares + epsilon)[:, None]).astype(jnp.bfloat16)  8.02 us
    ppermute x6, waiting for transfers between devices, narrow_sum(): total = total + lax.ppermute(piece, 'narrow', perm).astype(jnp.float32)  7.59 us
    unnamed x14, local copies, waits for them, and re-layouts  5.7 us
    reduce_sum x1, other arithmetic, shards(): target_squares = jnp.sum(target_wide * target_wide, axis=1)  5.14 us
  transfers between devices with their start and end apart: 6, of which 1 were waited for; matrix products, arithmetic and copies ran while one was open for 13% of the time, Pallas kernels for 0%

profile of v14, /device:TPU:1, one launch (start us, length us, event | category | flops | bytes accessed | tf_op | source)
XLA Modules:
  0.0 181.9 jit_solution(16450086492758510286)
XLA Ops:
  0.0 0.0 copy-start
  0.0 0.0 copy-start.2
  0.0 5.1 %fusion = f32[2048]{0:T(1024)S(1)} fusion(bf16[2048,2048]{1,0:T(8,128)(2,1)} %param.16), kind=kLoop, calls=%fused_computation.3 | loop fusion | flops 12580864 | bytes 8396800 | tf_op jit(solution)/shard_map/reduce_sum | solution.py:322
  5.1 0.0 copy-start.3
  5.2 3.4 %collective-permute-start.5 = (f32[2048]{0:T(1024)S(1)}, f32[2048]{0:T(1024)S(1)}, u32[]{:S(2)}, u32[]{:S(2)}) collective-permute-start(f32[2048]{0:T(1024)S(1)} %fusion), channel_id=1, source_target_pairs={{0,3},{1,0},{2,1},{3,2},{4,7},{5,4},{6,5},{7,6},{8,11},{9,8},{10,9... | collective-permute-start | bytes 24584 | tf_op jit(solution)/shard_map/ppermute | solution.py:36
  8.5 0.5 collective-permute-start.4
  9.1 0.6 collective-permute-start.3
  9.7 0.0 copy-done.2
  9.7 0.0 copy-start.1
  9.7 3.6 %fusion.23 = f32[2048,128]{1,0:T(8,128)S(1)} fusion(bf16[2048,1024]{1,0:T(8,128)(2,1)} %param.10, bf16[1024,128]{1,0:T(8,128)(2,1)S(1)} %copy-done.2), kind=kOutput, calls=%fused_computation.67 | convolution fusion | flops 536870912 | bytes 5505024 | tf_op jit(solution)/shard_map/dot_general | solution.py:333
  13.3 0.0 copy-done.3
  13.3 0.7 fusion.24
  14.0 0.0 copy-done
  14.0 0.0 copy-done.1
  14.0 0.0 copy-start.5
  14.1 0.0 copy-start.4
  14.1 1.5 fusion.22
  15.6 1.0 pad_maximum_fusion
  16.7 1.5 collective-permute-start
  18.2 1.7 collective-permute-start.1
  19.9 0.0 copy-done.5
  19.9 0.1 fusion.6
  20.0 0.0 copy-done.4
  20.1 8.0 %scatter_custom_fusion = s32[2048]{0:T(1024)S(1)} fusion(s32[2048]{0:T(1024)S(1)} %compare_select_fusion.2, s32[2048]{0:T(1024)S(1)} %iota.10, s32[]{:T(128)} %constant.125.clone.1), kind=kCustom, calls=%fused_computation.63 | custom fusion | bytes 8196 | tf_op jit(solution)/shard_map/scatter | solution.py:327
  28.1 0.0 collective-permute-done.5
  28.2 0.9 collective-permute-start.2
  29.1 0.0 collective-permute-done.4
  29.1 0.0 collective-permute-done.3
  29.1 8.0 %fusion.1.t_ref = bf16[2048,2048]{1,0:T(8,128)(2,1)} fusion(bf16[2048,2048]{1,0:T(8,128)(2,1)} %param.16, f32[2048]{0:T(1024)S(1)} %add_rsqrt_fusion), kind=kLoop, calls=%fused_computation.4 | loop fusion | flops 12582912 | bytes 16785408 | tf_op jit(solution)/shard_map/convert_element_type | solution.py:28
  37.1 0.0 collective-permute-done
  37.1 7.6 %collective-permute-done.1 = bf16[2048,144]{0,1:T(8,128)(2,1)} collective-permute-done((bf16[2048,144]{0,1:T(8,128)(2,1)S(1)}, bf16[2048,144]{0,1:T(8,128)(2,1)}, u32[]{:S(2)}, u32[]{:S(2)}) %collective-permute-start.1) | collective-permute-done | bytes 589856 | tf_op jit(solution)/shard_map/ppermute | solution.py:36
  44.7 0.0 collective-permute-done.2
  44.7 1.6 fusion.3
  46.3 0.1 slice.7
  46.4 0.3 copy.12
  46.7 0.2 reshape.34
  46.9 1.3 fusion.4
  48.3 1.0 copy.19
  49.3 1.3 copy.14.place_ref
  50.6 126.5 %shard_map.91 = f32[512,2048]{1,0:T(8,128)} custom-call(s32[2048,1]{1,0:T(8,128)} %copy.14.place_ref, f32[64,2048]{1,0:T(8,128)} %bitcast.18, bf16[2048,2048]{1,0:T(8,128)(2,1)} %fusion.1.t_ref), custom_call_target="tpu_custom_call" | custom-call | flops 34359738368 | bytes 29360128 | tf_op jit(solution)/shard_map/pallas_call | solution.py:227
  177.2 4.7 %copy.21 = f32[512,2048]{1,0:T(8,128)} copy(f32[512,2048]{1,0:T(8,128)} %shard_map.91) | data formatting | bytes 8388608
  (8 shorter events, 0.2 us)
Async XLA Ops:
  0.0 14.0 %copy-start = (bf16[1024,128]{1,0:T(8,128)(2,1)S(1)}, bf16[1024,128]{1,0:T(8,128)(2,1)}, u32[]{:S(2)}) copy-start(bf16[1024,128]{1,0:T(8,128)(2,1)} %param.12) | copy-start | bytes 786436
  0.0 9.7 %copy-start.2 = (bf16[1024,128]{1,0:T(8,128)(2,1)S(1)}, bf16[1024,128]{1,0:T(8,128)(2,1)}, u32[]{:S(2)}) copy-start(bf16[1024,128]{1,0:T(8,128)(2,1)} %param.11) | copy-start | bytes 786436
  5.1 8.1 %copy-start.3 = (bf16[128,64]{0,1:T(8,128)(2,1)S(1)}, bf16[128,64]{0,1:T(8,128)(2,1)}, u32[]{:S(2)}) copy-start(bf16[128,64]{0,1:T(8,128)(2,1)} %param.13) | copy-start | bytes 49156
  5.2 23.0 %collective-permute-start.5 = (f32[2048]{0:T(1024)S(1)}, f32[2048]{0:T(1024)S(1)}, u32[]{:S(2)}, u32[]{:S(2)}) collective-permute-start(f32[2048]{0:T(1024)S(1)} %fusion), channel_id=1, source_target_pairs={{0,3},{1,0},{2,1},{3,2},{4,7},{5,4},{6,5},{7,6},{8,11},{9,8},{10,9... | collective-permute-start | bytes 24584 | tf_op jit(solution)/shard_map/ppermute | solution.py:36
  8.5 20.6 %collective-permute-start.4 = (f32[2048]{0:T(1024)S(1)}, f32[2048]{0:T(1024)S(1)}, u32[]{:S(2)}, u32[]{:S(2)}) collective-permute-start(f32[2048]{0:T(1024)S(1)} %fusion), channel_id=1, source_target_pairs={{0,2},{1,3},{2,0},{3,1},{4,6},{5,7},{6,4},{7,5},{8,10},{9,11},{10,... | collective-permute-start | bytes 24584 | tf_op jit(solution)/shard_map/ppermute | solution.py:36
  9.1 20.0 %collective-permute-start.3 = (f32[2048]{0:T(1024)S(1)}, f32[2048]{0:T(1024)S(1)}, u32[]{:S(2)}, u32[]{:S(2)}) collective-permute-start(f32[2048]{0:T(1024)S(1)} %fusion), channel_id=1, source_target_pairs={{0,1},{1,2},{2,3},{3,0},{4,5},{5,6},{6,7},{7,4},{8,9},{9,10},{10,1... | collective-permute-start | bytes 24584 | tf_op jit(solution)/shard_map/ppermute | solution.py:36
  9.7 4.4 %copy-start.1 = (bf16[2048,1024]{1,0:T(8,128)(2,1)S(1)}, bf16[2048,1024]{1,0:T(8,128)(2,1)}, u32[]{:S(2)}) copy-start(bf16[2048,1024]{1,0:T(8,128)(2,1)} %param.9) | copy-start | bytes 12582916
  14.0 5.9 %copy-start.5 = (s32[64]{0:T(128)S(1)}, s32[64]{0:T(128)}, u32[]{:S(2)}) copy-start(s32[64]{0:T(128)} %param.14) | copy-start | bytes 772
  14.1 6.0 %copy-start.4 = (s32[2048]{0:T(1024)S(1)}, s32[2048]{0:T(1024)}, u32[]{:S(2)}) copy-start(s32[2048]{0:T(1024)} %param.15) | copy-start | bytes 24580
  16.7 20.4 %collective-permute-start = (bf16[2048,144]{0,1:T(8,128)(2,1)}, bf16[2048,144]{0,1:T(8,128)(2,1)}, u32[]{:S(2)}, u32[]{:S(2)}) collective-permute-start(bf16[2048,144]{0,1:T(8,128)(2,1)} %get-tuple-element.11), channel_id=1, source_target_pairs={{0,1},{1,2},{2,3},{3,0},{4,5},{5,6},{6,7},{7,4},{8,9},{9,10},{10,1... | collective-permute-start | bytes 1769480 | tf_op jit(solution)/shard_map/ppermute | solution.py:36
  18.2 26.5 %collective-permute-start.1 = (bf16[2048,144]{0,1:T(8,128)(2,1)S(1)}, bf16[2048,144]{0,1:T(8,128)(2,1)}, u32[]{:S(2)}, u32[]{:S(2)}) collective-permute-start(bf16[2048,144]{0,1:T(8,128)(2,1)S(1)} %get-tuple-element.12), channel_id=1, source_target_pairs={{0,2},{1,3},{2,0},{3,1},{4,6},{5,7},{6,4},{7,5},{8,10},{9,11},{10,... | collective-permute-start | bytes 1769480 | tf_op jit(solution)/shard_map/ppermute | solution.py:36
  28.2 16.6 %collective-permute-start.2 = (bf16[2048,144]{0,1:T(8,128)(2,1)S(1)}, bf16[2048,144]{0,1:T(8,128)(2,1)S(1)}, u32[]{:S(2)}, u32[]{:S(2)}) collective-permute-start(bf16[2048,144]{0,1:T(8,128)(2,1)S(1)} %get-tuple-element.13), channel_id=1, source_target_pairs={{0,3},{1,0},{2,1},{3,2},{4,7},{5,4},{6,5},{7,6},{8,11},{9,8},{10,9... | collective-permute-start | bytes 1769480 | tf_op jit(solution)/shard_map/ppermute | solution.py:36

commit v15 on v12

--- a/solution.py
+++ b/solution.py
@@ -37,14 +37,15 @@
     return total
 
 
-def ring_kernel(count, root, dest_ref, rows_ref, t_ref, out_ref, gathered,
-                ordered, send_buf, recv_buf, acc, send_sem, recv_sem, wide_send, wide_recv):
+def ring_kernel(count, root, dest_ref, feat_ref, t_ref, out_ref, gathered,
+                ordered, send_buf, recv_buf, acc, send_sem, recv_sem, wide_send, wide_recv,
+                rows_ref, sq_send, sq_recv, sq_send_sem, sq_recv_sem):
     me = lax.axis_index("narrow")
     right, left = lax.rem(me + 1, count), lax.rem(me + count - 1, count)
     rows = out_ref.shape[0]
     half = t_ref.shape[0] // 2
     tiles = rows // TILE
-    local = rows_ref.shape[0]
+    local = feat_ref.shape[0]
     everyone = gathered.shape[0]
 
     wide = lax.axis_index("wide")
@@ -59,12 +60,34 @@
     partner = {"wide": wide + 1 - 2 * core}
     peers = [wide_peer(True, 1), wide_peer(True, -1), wide_peer(False, 1), wide_peer(False, -1), partner]
 
+    narrow_peers = [lax.rem(me + shift, count) for shift in range(1, count)]
     barrier = pltpu.get_barrier_semaphore()
-    for neighbour in (left, right):
+    for neighbour in narrow_peers:
         pl.semaphore_signal(barrier, inc=1, device_id={"narrow": neighbour}, device_id_type=MESH)
     for peer in peers:
         pl.semaphore_signal(barrier, inc=1, device_id=peer, device_id_type=MESH)
-    pl.semaphore_wait(barrier, 2 + len(peers))
+    features = feat_ref[...]
+    sq_send[...] = jnp.broadcast_to(jnp.sum(features * features, axis=1, keepdims=True), sq_send.shape)
+    pl.semaphore_wait(barrier, len(narrow_peers) + len(peers))
+    squares_in = []
+    for shift in range(1, count):
+        squares_in.append(pltpu.make_async_remote_copy(
+            src_ref=sq_send,
+            dst_ref=sq_recv.at[shift - 1],
+            send_sem=sq_send_sem.at[shift - 1],
+            recv_sem=sq_recv_sem.at[shift - 1],
+            device_id={"narrow": narrow_peers[shift - 1]},
+            device_id_type=MESH,
+        ))
+        squares_in[-1].start()
+    for copy in squares_in:
+        copy.wait_recv()
+    squares = sq_send[:, 0:1]
+    for shift in range(1, count):
+        squares = squares + sq_recv[shift - 1, :, 0:1]
+    rows_ref[...] = (features * lax.rsqrt(squares + epsilon)).astype(jnp.bfloat16)
+    for copy in squares_in:
+        copy.wait_send()
 
     def wide_copy(index, src, dst_start, size, peer):
         return pltpu.make_async_remote_copy(
@@ -193,9 +216,9 @@
         copy.wait_send()
 
 
-def ring_scores(dest, unit_rows, target_unit, count, root):
+def ring_scores(dest, features, target_unit, count, root):
     programs = dest.shape[0]
-    depth = unit_rows.shape[1]
+    local, depth = features.shape
     rows = programs // count
     targets = target_unit.shape[0]
     half = targets // 2
@@ -214,6 +237,11 @@
             pltpu.SemaphoreType.DMA((2, count - 1, rows // TILE)),
             pltpu.SemaphoreType.DMA((12,)),
             pltpu.SemaphoreType.DMA((12,)),
+            pltpu.VMEM((local, depth), jnp.bfloat16),
+            pltpu.VMEM((local, 128), jnp.float32),
+            pltpu.VMEM((count - 1, local, 128), jnp.float32),
+            pltpu.SemaphoreType.DMA((count - 1,)),
+            pltpu.SemaphoreType.DMA((count - 1,)),
         ],
         compiler_params=pltpu.CompilerParams(
             collective_id=0, has_side_effects=True, vmem_limit_bytes=62 * 1024 * 1024
@@ -223,7 +251,7 @@
             bytes_accessed=2 * (2 * programs + targets) * depth + 4 * rows * targets,
             transcendentals=0,
         ),
-    )(dest.reshape(1, programs), unit_rows, target_unit)
+    )(dest.reshape(1, programs), features, target_unit)
 
 
 RING = 4
@@ -319,12 +347,9 @@
     quarter = summed_parts[:, :quarter_cols]
     in_all = summed_parts[:, quarter_cols:]
     features = program_features(quarter, in_all, lengths, length)
-    squares = jnp.sum(features * features, axis=1)
-    squares = narrow_sum(squares, lambda dest: squares, narrow_count, narrow_index, jnp.float32)
-    unit_rows = normalize_rows(features, squares)
     root_count = math.sqrt(float(targets.shape[1] * narrow_count))
-    dest = gathered_dest(program_output_index, unit_rows.shape[0])
-    return ring_scores(dest, unit_rows, target_unit, narrow_count, root_count)
+    dest = gathered_dest(program_output_index, features.shape[0])
+    return ring_scores(dest, features, target_unit, narrow_count, root_count)
 
 
 def solution(mesh):

time: 183 us -> 180 us (0.984)
  starting transfers between devices: 12.6 us -> 8.42 us
  Pallas kernels: 121 us -> 125 us
  waiting for transfers between devices: 19.1 us -> 15.6 us
    pallas_call x1, Pallas kernels: 121 us -> 125 us  [ring_scores(): pl.pallas_call(functools.partial(ring_kernel, count, root), out_shape=jax...]
    ppermute x9 -> x6, starting transfers between devices: 12.6 us -> 8.42 us  [narrow_sum(): total = total + lax.ppermute(piece, 'narrow', perm).astype(jnp.float32)]
    ppermute x9 -> x6, waiting for transfers between devices: 19.1 us -> 15.6 us  [narrow_sum(): total = total + lax.ppermute(piece, 'narrow', perm).astype(jnp.float32)]
    unnamed x13 -> x14, local copies, waits for them, and re-layouts: 4.73 us -> 5.68 us
    convert_element_type x2 -> x1, other arithmetic: 8.91 us -> 8.01 us  [normalize_rows(): (features * lax.rsqrt(squares + epsilon)[:, None]).astype(jnp.bfloat16)]
  transfers between devices with their start and end apart: 9 -> 6, of which waited for: 5 -> 3; matrix products, arithmetic and copies ran while one was open for 9% -> 9% of each run, Pallas kernels for 0% -> 0%
where the time goes in v15:
time: 180 us
  Pallas kernels  125 us (69%)
  other arithmetic  15.9 us (9%)
  waiting for transfers between devices  15.6 us (9%)
  starting transfers between devices  8.42 us (5%)
  matrix products  7.37 us (4%)
  local copies, waits for them, and re-layouts  7.07 us (4%)
    pallas_call x1, Pallas kernels, ring_scores(): pl.pallas_call(functools.partial(ring_kernel, count, root), out_shape=jax...  125 us
    ppermute x6, waiting for transfers between devices, narrow_sum(): total = total + lax.ppermute(piece, 'narrow', perm).astype(jnp.float32)  15.6 us
    ppermute x6, starting transfers between devices, narrow_sum(): total = total + lax.ppermute(piece, 'narrow', perm).astype(jnp.float32)  8.42 us
    convert_element_type x1, other arithmetic, normalize_rows(): (features * lax.rsqrt(squares + epsilon)[:, None]).astype(jnp.bfloat16)  8.01 us
    unnamed x14, local copies, waits for them, and re-layouts  5.68 us
    reduce_sum x1, other arithmetic, shards(): target_squares = jnp.sum(target_wide * target_wide, axis=1)  5.14 us
    dot_general x1, matrix products, shards(): jnp.dot(output_gradient_rows, adapter_up_weight, preferred_element_type=j...  3.61 us
  transfers between devices with their start and end apart: 6, of which 3 were waited for; matrix products, arithmetic and copies ran while one was open for 9% of the time, Pallas kernels for 0%

profile of v15, /device:TPU:1, one launch (start us, length us, event | category | flops | bytes accessed | tf_op | source)
XLA Modules:
  0.0 179.9 jit_solution(3894137662260107981)
XLA Ops:
  0.0 0.0 copy-start
  0.0 0.0 copy-start.2
  0.0 5.1 %fusion = f32[2048]{0:T(1024)S(1)} fusion(bf16[2048,2048]{1,0:T(8,128)(2,1)} %param.16), kind=kLoop, calls=%fused_computation.2 | loop fusion | flops 12580864 | bytes 8396800 | tf_op jit(solution)/shard_map/reduce_sum | solution.py:326
  5.1 0.0 copy-start.3
  5.2 3.4 %collective-permute-start.5 = (f32[2048]{0:T(1024)S(1)}, f32[2048]{0:T(1024)S(1)}, u32[]{:S(2)}, u32[]{:S(2)}) collective-permute-start(f32[2048]{0:T(1024)S(1)} %fusion), channel_id=1, source_target_pairs={{0,3},{1,0},{2,1},{3,2},{4,7},{5,4},{6,5},{7,6},{8,11},{9,8},{10,9... | collective-permute-start | bytes 24584 | tf_op jit(solution)/shard_map/ppermute | solution.py:36
  8.5 0.5 collective-permute-start.4
  9.1 0.6 collective-permute-start.3
  9.7 0.0 copy-done.2
  9.7 0.0 copy-start.1
  9.7 3.6 %fusion.17 = f32[2048,128]{1,0:T(8,128)S(1)} fusion(bf16[2048,1024]{1,0:T(8,128)(2,1)} %param.10, bf16[1024,128]{1,0:T(8,128)(2,1)S(1)} %copy-done.2), kind=kOutput, calls=%fused_computation.61 | convolution fusion | flops 536870912 | bytes 5505024 | tf_op jit(solution)/shard_map/dot_general | solution.py:332
  13.3 0.0 copy-done.3
  13.3 0.7 fusion.18
  14.0 0.0 copy-done
  14.0 0.0 copy-done.1
  14.0 0.0 copy-start.4
  14.1 0.0 copy-start.5
  14.1 1.5 fusion.16
  15.6 1.0 pad_maximum_fusion
  16.7 1.5 collective-permute-start
  18.2 1.7 collective-permute-start.1
  19.9 0.0 copy-done.4
  19.9 0.1 convert_element_type.37
  20.0 0.0 copy-done.5
  20.0 0.1 fusion.6
  20.1 0.2 convolution_convert_fusion
  20.3 0.7 reshape_reshape.3.dest_ref
  21.0 0.0 collective-permute-done.5
  21.0 0.7 collective-permute-start.2
  21.7 0.0 collective-permute-done.4
  21.7 0.0 collective-permute-done.3
  21.7 8.0 %fusion.1.t_ref = bf16[2048,2048]{1,0:T(8,128)(2,1)} fusion(bf16[2048,2048]{1,0:T(8,128)(2,1)} %param.16, f32[2048]{0:T(1024)S(1)} %add_rsqrt_fusion), kind=kLoop, calls=%fused_computation.3 | loop fusion | flops 12582912 | bytes 16785408 | tf_op jit(solution)/shard_map/convert_element_type | solution.py:28
  29.7 1.8 collective-permute-done
  31.5 13.2 %collective-permute-done.1 = bf16[2048,144]{0,1:T(8,128)(2,1)} collective-permute-done((bf16[2048,144]{0,1:T(8,128)(2,1)S(1)}, bf16[2048,144]{0,1:T(8,128)(2,1)}, u32[]{:S(2)}, u32[]{:S(2)}) %collective-permute-start.1) | collective-permute-done | bytes 589856 | tf_op jit(solution)/shard_map/ppermute | solution.py:36
  44.7 0.6 collective-permute-done.2
  45.3 1.5 fusion.3
  46.9 0.1 slice.7
  47.0 0.3 copy.12
  47.3 0.2 reshape.187
  47.6 1.3 fusion.4
  48.9 1.0 copy.18
  49.8 125.4 %shard_map.91 = f32[512,2048]{1,0:T(8,128)} custom-call(s32[1,2048]{1,0:T(1,128)} %reshape_reshape.3.dest_ref, f32[64,2048]{1,0:T(8,128)} %bitcast.25, bf16[2048,2048]{1,0:T(8,128)(2,1)} %fusion.1.t_ref), custom_call_target="tpu_custom_call" | custom-call | flops 34359738368 | bytes 29360128 | tf_op jit(solution)/shard_map/pallas_call | solution.py:225
  175.2 4.7 %copy.20 = f32[512,2048]{1,0:T(8,128)} copy(f32[512,2048]{1,0:T(8,128)} %shard_map.91) | data formatting | bytes 8388608
  (7 shorter events, 0.1 us)
Async XLA Ops:
  0.0 14.0 %copy-start = (bf16[1024,128]{1,0:T(8,128)(2,1)S(1)}, bf16[1024,128]{1,0:T(8,128)(2,1)}, u32[]{:S(2)}) copy-start(bf16[1024,128]{1,0:T(8,128)(2,1)} %param.12) | copy-start | bytes 786436
  0.0 9.7 %copy-start.2 = (bf16[1024,128]{1,0:T(8,128)(2,1)S(1)}, bf16[1024,128]{1,0:T(8,128)(2,1)}, u32[]{:S(2)}) copy-start(bf16[1024,128]{1,0:T(8,128)(2,1)} %param.11) | copy-start | bytes 786436
  5.1 8.1 %copy-start.3 = (bf16[128,64]{0,1:T(8,128)(2,1)S(1)}, bf16[128,64]{0,1:T(8,128)(2,1)}, u32[]{:S(2)}) copy-start(bf16[128,64]{0,1:T(8,128)(2,1)} %param.13) | copy-start | bytes 49156
  5.2 15.9 %collective-permute-start.5 = (f32[2048]{0:T(1024)S(1)}, f32[2048]{0:T(1024)S(1)}, u32[]{:S(2)}, u32[]{:S(2)}) collective-permute-start(f32[2048]{0:T(1024)S(1)} %fusion), channel_id=1, source_target_pairs={{0,3},{1,0},{2,1},{3,2},{4,7},{5,4},{6,5},{7,6},{8,11},{9,8},{10,9... | collective-permute-start | bytes 24584 | tf_op jit(solution)/shard_map/ppermute | solution.py:36
  8.5 13.2 %collective-permute-start.4 = (f32[2048]{0:T(1024)S(1)}, f32[2048]{0:T(1024)S(1)}, u32[]{:S(2)}, u32[]{:S(2)}) collective-permute-start(f32[2048]{0:T(1024)S(1)} %fusion), channel_id=1, source_target_pairs={{0,2},{1,3},{2,0},{3,1},{4,6},{5,7},{6,4},{7,5},{8,10},{9,11},{10,... | collective-permute-start | bytes 24584 | tf_op jit(solution)/shard_map/ppermute | solution.py:36
  9.1 12.7 %collective-permute-start.3 = (f32[2048]{0:T(1024)S(1)}, f32[2048]{0:T(1024)S(1)}, u32[]{:S(2)}, u32[]{:S(2)}) collective-permute-start(f32[2048]{0:T(1024)S(1)} %fusion), channel_id=1, source_target_pairs={{0,1},{1,2},{2,3},{3,0},{4,5},{5,6},{6,7},{7,4},{8,9},{9,10},{10,1... | collective-permute-start | bytes 24584 | tf_op jit(solution)/shard_map/ppermute | solution.py:36
  9.7 4.4 %copy-start.1 = (bf16[2048,1024]{1,0:T(8,128)(2,1)S(1)}, bf16[2048,1024]{1,0:T(8,128)(2,1)}, u32[]{:S(2)}) copy-start(bf16[2048,1024]{1,0:T(8,128)(2,1)} %param.9) | copy-start | bytes 12582916
  14.0 5.9 %copy-start.4 = (s32[2048]{0:T(1024)S(1)}, s32[2048]{0:T(1024)}, u32[]{:S(2)}) copy-start(s32[2048]{0:T(1024)} %param.15) | copy-start | bytes 24580
  14.1 5.9 %copy-start.5 = (s32[64]{0:T(128)S(1)}, s32[64]{0:T(128)}, u32[]{:S(2)}) copy-start(s32[64]{0:T(128)} %param.14) | copy-start | bytes 772
  16.7 14.8 %collective-permute-start = (bf16[2048,144]{0,1:T(8,128)(2,1)}, bf16[2048,144]{0,1:T(8,128)(2,1)}, u32[]{:S(2)}, u32[]{:S(2)}) collective-permute-start(bf16[2048,144]{0,1:T(8,128)(2,1)} %get-tuple-element.9), channel_id=1, source_target_pairs={{0,1},{1,2},{2,3},{3,0},{4,5},{5,6},{6,7},{7,4},{8,9},{9,10},{10,1... | collective-permute-start | bytes 1769480 | tf_op jit(solution)/shard_map/ppermute | solution.py:36
  18.2 26.5 %collective-permute-start.1 = (bf16[2048,144]{0,1:T(8,128)(2,1)S(1)}, bf16[2048,144]{0,1:T(8,128)(2,1)}, u32[]{:S(2)}, u32[]{:S(2)}) collective-permute-start(bf16[2048,144]{0,1:T(8,128)(2,1)S(1)} %get-tuple-element.10), channel_id=1, source_target_pairs={{0,2},{1,3},{2,0},{3,1},{4,6},{5,7},{6,4},{7,5},{8,10},{9,11},{10,... | collective-permute-start | bytes 1769480 | tf_op jit(solution)/shard_map/ppermute | solution.py:36
  21.0 24.3 %collective-permute-start.2 = (bf16[2048,144]{0,1:T(8,128)(2,1)S(1)}, bf16[2048,144]{0,1:T(8,128)(2,1)S(1)}, u32[]{:S(2)}, u32[]{:S(2)}) collective-permute-start(bf16[2048,144]{0,1:T(8,128)(2,1)S(1)} %get-tuple-element.11), channel_id=1, source_target_pairs={{0,3},{1,0},{2,1},{3,2},{4,7},{5,4},{6,5},{7,6},{8,11},{9,8},{10,9... | collective-permute-start | bytes 1769480 | tf_op jit(solution)/shard_map/ppermute | solution.py:36
